TPU v7x, 256 devices: a whole 4x4x8 slice. The times are simulated.
256 devices in a mesh: seq: 32 (over x, z), ch: 8 (over y, core).
Axes of the slice: x: 4, y: 4, z: 8, core: 2. Of those that a mesh axis runs over, the one named last changes fastest.
Arguments:
- out_gate: bfloat16 [12288, 4096], P('seq', 'ch'), may hold values from -6 to 6
- in_gate: bfloat16 [12288, 4096], P('seq', 'ch'), may hold values from -6 to 6
- values: bfloat16 [12288, 4096], P('seq', 'ch'), may hold values from -6 to 6
- short_filter: float32 [3, 3, 4096], P(None, None, 'ch'), may hold values from -3 to 3
- long_filter: float32 [12288, 4096], P('seq', 'ch'), may hold values from -1.5 to 1.5
- skip_gain: float32 [4096], P('ch'), may hold values from -4 to 4
- out_weight: bfloat16 [4096, 4096], P(None, 'ch'), may hold values from -0.09375 to 0.09375
Outputs:
- projected: bfloat16 [12288, 4096], P('seq', 'ch')
All inputs are finite; a program needn't handle non-finite values.
Results may differ from a plain program's by a relative error of at most 0.0049.
Values may be sent and summed in bfloat16 or wider, within the bound.
A program may use at most 128 MiB of HBM per device.

v0:
```python
import math

import jax
import jax.numpy as jnp
from jax import lax
from jax.sharding import PartitionSpec as P

highest = lax.Precision.HIGHEST


def shifted(block, axis, distance):
    devices = range(lax.axis_size(axis))
    route = [(i - distance, i) for i in devices if i - distance in devices]
    return lax.ppermute(block, axis, route)


def phase_table(row_ids, col_ids, modulus, direction):
    product = row_ids[:, None] * col_ids[None, :] % modulus
    angles = product.astype(jnp.float32) * (direction * 2.0 * math.pi / modulus)
    return (jnp.cos(angles), jnp.sin(angles))


def contract(pattern, first_op, second_op):
    return jnp.einsum(pattern, first_op, second_op, precision=highest)


def complex_apply(pattern, phases, operand):
    cosine, sine_part = phases
    real_part, imaginary = operand
    return (
        contract(pattern, cosine, real_part) - contract(pattern, sine_part, imaginary),
        contract(pattern, cosine, imaginary) + contract(pattern, sine_part, real_part),
    )


def complex_times(first_op, second_op):
    return (
        first_op[0] * second_op[0] - first_op[1] * second_op[1],
        first_op[0] * second_op[1] + first_op[1] * second_op[0],
    )


def sequence_conv(mixed_in, long_filter):
    seq_count = lax.axis_size("seq")
    seq_index = lax.axis_index("seq")
    row_count = mixed_in.shape[0]
    total_len = row_count * seq_count
    piece_rows = row_count // seq_count
    rows_b = jnp.arange(row_count, dtype=jnp.int32)
    device_ids = jnp.arange(seq_count, dtype=jnp.int32)
    positions = seq_index * row_count + rows_b
    angles = positions.astype(jnp.float32) * (math.pi / total_len)
    cosines = jnp.cos(angles)[:, None]
    sines = jnp.sin(angles)[:, None]
    planes = jnp.stack([mixed_in, long_filter])[:, None]
    spread = lax.all_to_all(planes, "seq", split_axis=2, concat_axis=1, tiled=True)
    local_b = seq_index * piece_rows + jnp.arange(piece_rows, dtype=jnp.int32)
    arrived_pos = device_ids[:, None] * row_count + local_b[None, :]
    arrived_angles = arrived_pos.astype(jnp.float32) * (math.pi / total_len)
    arrived_cos = jnp.cos(arrived_angles)[:, :, None]
    arrived_sin = jnp.sin(arrived_angles)[:, :, None]
    zeros_plane = jnp.zeros_like(spread[0])
    real_part = jnp.stack([spread[0], spread[0] * arrived_cos, spread[1], spread[1] * arrived_cos])
    imaginary = jnp.stack(
        [zeros_plane, -spread[0] * arrived_sin, zeros_plane, -spread[1] * arrived_sin]
    )
    sectioned = complex_apply(
        "kp,xpbc->xkbc",
        phase_table(device_ids, device_ids, seq_count, -1.0),
        (real_part, imaginary),
    )
    twist_table = phase_table(device_ids, local_b, total_len, -1.0)
    sectioned = complex_times(sectioned, (twist_table[0][:, :, None], twist_table[1][:, :, None]))
    arrived = (
        lax.all_to_all(sectioned[0], "seq", split_axis=1, concat_axis=2, tiled=True),
        lax.all_to_all(sectioned[1], "seq", split_axis=1, concat_axis=2, tiled=True),
    )
    spectra = complex_apply("mb,xkbc->xkmc", phase_table(rows_b, rows_b, row_count, -1.0), arrived)
    product = complex_times((spectra[0][:2], spectra[1][:2]), (spectra[0][2:], spectra[1][2:]))
    sectioned = complex_apply("mb,xkmc->xkbc", phase_table(rows_b, rows_b, row_count, 1.0), product)
    twist_table = phase_table(seq_index.reshape(1), rows_b, total_len, 1.0)
    sectioned = complex_times(sectioned, (twist_table[0][:, :, None], twist_table[1][:, :, None]))
    returned = (
        lax.all_to_all(sectioned[0], "seq", split_axis=2, concat_axis=1, tiled=True),
        lax.all_to_all(sectioned[1], "seq", split_axis=2, concat_axis=1, tiled=True),
    )
    sectioned = complex_apply(
        "kp,xkbc->xpbc", phase_table(device_ids, device_ids, seq_count, 1.0), returned
    )
    restored = (
        lax.all_to_all(sectioned[0], "seq", split_axis=1, concat_axis=2, tiled=True),
        lax.all_to_all(sectioned[1], "seq", split_axis=1, concat_axis=2, tiled=True),
    )
    real_out = restored[0][:, 0] / total_len
    imag_out = restored[1][:, 0] / total_len
    return 0.5 * (real_out[0] + cosines * real_out[1] - sines * imag_out[1])


def on_device(out_gate, in_gate, values, short_filter, long_filter, skip_gain, out_weight):
    tap_count = short_filter.shape[1]
    row_count = out_gate.shape[0]
    stacked = jnp.stack([out_gate, in_gate, values])
    rim_rows = shifted(stacked[:, row_count - (tap_count - 1) :], "seq", 1)
    widened = jnp.concatenate([rim_rows, stacked], axis=1).astype(jnp.float32)
    shorted = short_filter[:, 0, None, :] * widened[:, tap_count - 1 :]
    for offset in range(1, tap_count):
        start_row = tap_count - 1 - offset
        shorted = (
            shorted
            + short_filter[:, offset, None, :] * widened[:, start_row : start_row + row_count]
        )
    gate_late = shorted[0]
    mixed_in = shorted[1] * shorted[2]
    long_out = sequence_conv(mixed_in, long_filter)
    filtered = long_out + skip_gain * mixed_in
    mixed = (gate_late * filtered).astype(jnp.bfloat16)
    summed = jnp.dot(
        lax.all_gather(mixed, "ch", axis=1, tiled=True),
        out_weight,
        preferred_element_type=jnp.float32,
    )
    return summed.astype(jnp.bfloat16)


def solution(mesh):
    return jax.shard_map(
        on_device,
        mesh=mesh,
        in_specs=(
            P("seq", "ch"),
            P("seq", "ch"),
            P("seq", "ch"),
            P(None, None, "ch"),
            P("seq", "ch"),
            P("ch"),
            P(None, "ch"),
        ),
        out_specs=P("seq", "ch"),
        check_vma=False,
    )
```

profile of v0, /device:TPU:1, one launch (start us, length us, event | category | flops | bytes accessed | tf_op | source)
XLA Modules:
  0.0 544.4 jit_solution(16303291833496536461)
XLA Ops:
  19.1 12.4 %all-to-all-start = ((f32[2,1,384,512]{3,0,1,2:T(2,128)}), f32[2,1,384,512]{3,0,1,2:T(2,128)S(1)}, u32[]{:S(2)}, u32[]{:S(2)}) async-start(f32[2,1,384,512]{3,0,1,2:T(2,128)} %copy.68), calls=%async_computation | async-start | bytes 3145728 | tf_op jit(solution)/shard_map/all_to_all | solution.py:56
  31.7 36.7 %all-to-all-done = f32[2,1,384,512]{3,0,1,2:T(2,128)S(1)} async-done(((f32[2,1,384,512]{3,0,1,2:T(2,128)}), f32[2,1,384,512]{3,0,1,2:T(2,128)S(1)}, u32[]{:S(2)}, u32[]{:S(2)}) %all-to-all-start) | async-done | bytes 1572896 | tf_op jit(solution)/shard_map/all_to_all | solution.py:56
  80.6 6.0 %fusion = (f32[4,32,12,512]{3,1,2,0:T(8,128)S(1)}, f32[4,32,12,512]{3,1,2,0:T(8,128)}) fusion(f32[4,12,512,32]{2,3,1,0:T(8,128)S(1)} %convolution_subtract_fusion, f32[32,12]{0,1:T(8,128)S(1)} %get-tuple-element.27, f32[32,12]{0,1:T(8,128)S(1)} %get-tuple-element.26, f32[4,12,512,32]{2,3,1,0:T(8,128)S(1)} %fusion.2, ...), kind=kOutput, calls=%fused_computation.4 | convolution fusion | flops 309868544 | bytes 15731712 | tf_op jit(solution)/shard_map/kp,xpbc->xkbc/dot_general | solution.py:24
  90.3 7.3 %all-to-all-start.1 = ((f32[4,32,12,512]{3,0,2,1:T(4,128)}), f32[4,32,12,512]{3,0,2,1:T(4,128)S(1)}, u32[]{:S(2)}, u32[]{:S(2)}) async-start(f32[4,32,12,512]{3,0,2,1:T(4,128)} %copy.79), calls=%async_computation.1 | async-start | bytes 6291456 | tf_op jit(solution)/shard_map/all_to_all | solution.py:75
  97.6 5.5 %copy.81 = f32[4,32,12,512]{3,0,2,1:T(4,128)} copy(f32[4,32,12,512]{3,1,2,0:T(8,128)} %get-tuple-element.8) | data formatting | bytes 6291456 | tf_op jit(solution)/shard_map/add | solution.py:39
  103.1 65.8 %all-to-all-done.1 = f32[4,32,12,512]{3,0,2,1:T(4,128)S(1)} async-done(((f32[4,32,12,512]{3,0,2,1:T(4,128)}), f32[4,32,12,512]{3,0,2,1:T(4,128)S(1)}, u32[]{:S(2)}, u32[]{:S(2)}) %all-to-all-start.1) | async-done | bytes 3145760 | tf_op jit(solution)/shard_map/all_to_all | solution.py:75
  170.6 7.8 %all-to-all-start.2 = ((f32[4,32,12,512]{3,0,2,1:T(4,128)}), f32[4,32,12,512]{3,0,2,1:T(4,128)}, u32[]{:S(2)}, u32[]{:S(2)}) async-start(f32[4,32,12,512]{3,0,2,1:T(4,128)} %copy.81), calls=%async_computation.2 | async-start | bytes 6291456 | tf_op jit(solution)/shard_map/all_to_all | solution.py:76
  181.7 9.8 %fusion.43 = f32[4,512,384]{2,1,0:T(8,128)} fusion(f32[4,384,512]{1,2,0:T(8,128)S(1)} %copy.80), kind=kOutput, calls=%fused_computation.73 | convolution fusion | flops 3625205760 | bytes 6291456 | tf_op jit(solution)/shard_map/mb,xkbc->xkmc/dot_general | solution.py:24
  191.5 60.2 %all-to-all-done.2 = f32[4,32,12,512]{3,0,2,1:T(4,128)} async-done(((f32[4,32,12,512]{3,0,2,1:T(4,128)}), f32[4,32,12,512]{3,0,2,1:T(4,128)}, u32[]{:S(2)}, u32[]{:S(2)}) %all-to-all-start.2) | async-done | bytes 3145760 | tf_op jit(solution)/shard_map/all_to_all | solution.py:76
  256.8 10.7 %fusion.41 = f32[4,512,384]{2,1,0:T(8,128)S(1)} fusion(f32[4,384,512]{1,2,0:T(8,128)} %copy.82), kind=kOutput, calls=%fused_computation.71 | convolution fusion | flops 3625205760 | bytes 6291456 | tf_op jit(solution)/shard_map/mb,xkbc->xkmc/dot_general | solution.py:24
  267.6 9.2 %subtract_bitcast_fusion = f32[4,1,384,512]{2,3,0,1:T(8,128)S(1)} fusion(f32[4,512,384]{2,1,0:T(8,128)S(1)} %copy-done.4, f32[4,384,512]{1,2,0:T(8,128)S(1)} %copy-done), kind=kOutput, calls=%fused_computation.9 | convolution fusion | flops 3625992192 | bytes 9437184 | tf_op jit(solution)/shard_map/mb,xkbc->xkmc/dot_general | solution.py:24
  276.8 9.0 %add_bitcast_fusion = f32[4,1,384,512]{2,3,0,1:T(8,128)S(1)} fusion(f32[4,512,384]{2,1,0:T(8,128)S(1)} %fusion.41, f32[4,384,512]{1,2,0:T(8,128)S(1)} %copy.80), kind=kOutput, calls=%fused_computation.8 | convolution fusion | flops 3625992192 | bytes 9437184 | tf_op jit(solution)/shard_map/mb,xkbc->xkmc/dot_general | solution.py:24
  291.5 5.8 %fusion.10 = f32[2,512,384]{2,1,0:T(8,128)S(1)} fusion(f32[2,1,384,512]{2,3,0,1:T(8,128)S(1)} %get-tuple-element.10), kind=kOutput, calls=%fused_computation.28 | convolution fusion | flops 1813266432 | bytes 3145728 | tf_op jit(solution)/shard_map/mb,xkmc->xkbc/dot_general | solution.py:24
  302.8 5.5 %fusion.7 = (f32[2,1,384,512]{2,3,0,1:T(8,128)S(1)}, f32[2,1,384,512]{2,3,0,1:T(8,128)S(1)}) fusion(f32[2,512,384]{2,1,0:T(8,128)S(1)} %fusion.18, f32[384]{0:T(512)S(1)} %get-tuple-element.32, f32[384]{0:T(512)S(1)} %get-tuple-element.33, f32[2,512,384]{2,1,0:T(8,128)S(1)} %fusion.10, f32[2,1,384,512]{2,3,0,1:T(8,128)S(1)} %get-tuple-element.9), kind=kOutput, calls=%fused_computation.23 | convolution fusion | flops 1816018944 | bytes 7867392 | tf_op jit(solution)/shard_map/mb,xkmc->xkbc/dot_general | solution.py:24
  310.4 5.9 %all-to-all-start.3 = ((f32[2,1,384,512]{3,0,1,2:T(2,128)}), f32[2,1,384,512]{3,0,1,2:T(2,128)S(1)}, u32[]{:S(2)}, u32[]{:S(2)}) async-start(f32[2,1,384,512]{3,0,1,2:T(2,128)} %copy.85), calls=%async_computation.3 | async-start | bytes 3145728 | tf_op jit(solution)/shard_map/all_to_all | solution.py:84
  318.3 34.6 %all-to-all-done.3 = f32[2,1,384,512]{3,0,1,2:T(2,128)S(1)} async-done(((f32[2,1,384,512]{3,0,1,2:T(2,128)}), f32[2,1,384,512]{3,0,1,2:T(2,128)S(1)}, u32[]{:S(2)}, u32[]{:S(2)}) %all-to-all-start.3) | async-done | bytes 1572896 | tf_op jit(solution)/shard_map/all_to_all | solution.py:84
  352.9 7.7 %all-to-all-start.4 = ((f32[2,1,384,512]{3,0,1,2:T(2,128)}), f32[2,1,384,512]{3,0,1,2:T(2,128)S(1)}, u32[]{:S(2)}, u32[]{:S(2)}) async-start(f32[2,1,384,512]{3,0,1,2:T(2,128)} %copy.87), calls=%async_computation.4 | async-start | bytes 3145728 | tf_op jit(solution)/shard_map/all_to_all | solution.py:85
  364.3 33.1 %all-to-all-done.4 = f32[2,1,384,512]{3,0,1,2:T(2,128)S(1)} async-done(((f32[2,1,384,512]{3,0,1,2:T(2,128)}), f32[2,1,384,512]{3,0,1,2:T(2,128)S(1)}, u32[]{:S(2)}, u32[]{:S(2)}) %all-to-all-start.4) | async-done | bytes 1572896 | tf_op jit(solution)/shard_map/all_to_all | solution.py:85
  403.9 7.8 %all-to-all-start.5 = ((f32[2,32,12,512]{3,0,2,1:T(2,128)}), f32[2,32,12,512]{3,0,2,1:T(2,128)}, u32[]{:S(2)}, u32[]{:S(2)}) async-start(f32[2,32,12,512]{3,0,2,1:T(2,128)} %copy.89), calls=%async_computation.5 | async-start | bytes 3145728 | tf_op jit(solution)/shard_map/all_to_all | solution.py:91
  419.2 29.2 %all-to-all-done.5 = f32[2,32,12,512]{3,0,2,1:T(2,128)} async-done(((f32[2,32,12,512]{3,0,2,1:T(2,128)}), f32[2,32,12,512]{3,0,2,1:T(2,128)}, u32[]{:S(2)}, u32[]{:S(2)}) %all-to-all-start.5) | async-done | bytes 1572896 | tf_op jit(solution)/shard_map/all_to_all | solution.py:91
  448.4 7.8 %all-to-all-start.6 = ((f32[2,32,12,512]{3,0,2,1:T(2,128)}), f32[2,32,12,512]{3,0,2,1:T(2,128)}, u32[]{:S(2)}, u32[]{:S(2)}) async-start(f32[2,32,12,512]{3,0,2,1:T(2,128)} %copy.92), calls=%async_computation.6 | async-start | bytes 3145728 | tf_op jit(solution)/shard_map/all_to_all | solution.py:92
  464.9 28.1 %all-to-all-done.6 = f32[2,32,12,512]{3,0,2,1:T(2,128)} async-done(((f32[2,32,12,512]{3,0,2,1:T(2,128)}), f32[2,32,12,512]{3,0,2,1:T(2,128)}, u32[]{:S(2)}, u32[]{:S(2)}) %all-to-all-start.6) | async-done | bytes 1572896 | tf_op jit(solution)/shard_map/all_to_all | solution.py:92
  500.7 31.0 %all-gather.2.cloned.1.call-done = bf16[384,4096]{1,0:T(8,128)(2,1)} async-done(((bf16[384,512]{1,0:T(8,128)(2,1)}), bf16[384,4096]{1,0:T(8,128)(2,1)}) %all-gather.2.cloned.1.call-update) | async-done | bytes 3145744 | tf_op jit(solution)/shard_map/all_gather | solution.py:118
  531.6 5.7 %convolution_convert_fusion = bf16[384,512]{1,0:T(8,128)(2,1)} fusion(bf16[384,4096]{1,0:T(8,128)(2,1)} %all-gather.2.cloned.1.call-done, bf16[4096,512]{1,0:T(8,128)(2,1)} %param.13), kind=kOutput, calls=%fused_computation.48 | convolution fusion | flops 1610809344 | bytes 7733248 | tf_op jit(solution)/shard_map/dot_general | solution.py:117
  (60 shorter events, 87.9 us)
Async XLA Ops:
  7.3 5.3 collective-permute-start
  14.9 1.8 copy-start.1
  14.9 1.7 copy-start.5
  19.1 49.3 %all-to-all-start = ((f32[2,1,384,512]{3,0,1,2:T(2,128)}), f32[2,1,384,512]{3,0,1,2:T(2,128)S(1)}, u32[]{:S(2)}, u32[]{:S(2)}) async-start(f32[2,1,384,512]{3,0,1,2:T(2,128)} %copy.68), calls=%async_computation | async-start | bytes 3145728 | tf_op jit(solution)/shard_map/all_to_all | solution.py:56
  90.3 78.6 %all-to-all-start.1 = ((f32[4,32,12,512]{3,0,2,1:T(4,128)}), f32[4,32,12,512]{3,0,2,1:T(4,128)S(1)}, u32[]{:S(2)}, u32[]{:S(2)}) async-start(f32[4,32,12,512]{3,0,2,1:T(4,128)} %copy.79), calls=%async_computation.1 | async-start | bytes 6291456 | tf_op jit(solution)/shard_map/all_to_all | solution.py:75
  168.9 1.7 copy-start.3
  170.6 81.0 %all-to-all-start.2 = ((f32[4,32,12,512]{3,0,2,1:T(4,128)}), f32[4,32,12,512]{3,0,2,1:T(4,128)}, u32[]{:S(2)}, u32[]{:S(2)}) async-start(f32[4,32,12,512]{3,0,2,1:T(4,128)} %copy.81), calls=%async_computation.2 | async-start | bytes 6291456 | tf_op jit(solution)/shard_map/all_to_all | solution.py:76
  256.8 10.7 %copy-start = (f32[4,384,512]{1,2,0:T(8,128)S(1)}, f32[4,384,512]{1,2,0:T(8,128)}, u32[]{:S(2)}) copy-start(f32[4,384,512]{1,2,0:T(8,128)} %copy.82) | copy-start | bytes 9437188
  256.8 10.7 %copy-start.4 = (f32[4,512,384]{2,1,0:T(8,128)S(1)}, f32[4,512,384]{2,1,0:T(8,128)}, u32[]{:S(2)}) copy-start(f32[4,512,384]{2,1,0:T(8,128)} %fusion.43) | copy-start | bytes 9437188
  310.4 42.6 %all-to-all-start.3 = ((f32[2,1,384,512]{3,0,1,2:T(2,128)}), f32[2,1,384,512]{3,0,1,2:T(2,128)S(1)}, u32[]{:S(2)}, u32[]{:S(2)}) async-start(f32[2,1,384,512]{3,0,1,2:T(2,128)} %copy.85), calls=%async_computation.3 | async-start | bytes 3145728 | tf_op jit(solution)/shard_map/all_to_all | solution.py:84
  352.9 44.5 %all-to-all-start.4 = ((f32[2,1,384,512]{3,0,1,2:T(2,128)}), f32[2,1,384,512]{3,0,1,2:T(2,128)S(1)}, u32[]{:S(2)}, u32[]{:S(2)}) async-start(f32[2,1,384,512]{3,0,1,2:T(2,128)} %copy.87), calls=%async_computation.4 | async-start | bytes 3145728 | tf_op jit(solution)/shard_map/all_to_all | solution.py:85
  403.9 44.6 %all-to-all-start.5 = ((f32[2,32,12,512]{3,0,2,1:T(2,128)}), f32[2,32,12,512]{3,0,2,1:T(2,128)}, u32[]{:S(2)}, u32[]{:S(2)}) async-start(f32[2,32,12,512]{3,0,2,1:T(2,128)} %copy.89), calls=%async_computation.5 | async-start | bytes 3145728 | tf_op jit(solution)/shard_map/all_to_all | solution.py:91
  448.4 44.6 %all-to-all-start.6 = ((f32[2,32,12,512]{3,0,2,1:T(2,128)}), f32[2,32,12,512]{3,0,2,1:T(2,128)}, u32[]{:S(2)}, u32[]{:S(2)}) async-start(f32[2,32,12,512]{3,0,2,1:T(2,128)} %copy.92), calls=%async_computation.6 | async-start | bytes 3145728 | tf_op jit(solution)/shard_map/all_to_all | solution.py:92
  456.2 75.4 %all-gather.2.cloned.1.call-start = ((), (), s32[]{:S(2)}) async-start(), calls=%async_computation.7 | async-start | bytes 3538944 | tf_op jit(solution)/shard_map/all_gather | solution.py:118
  464.0 34.0 %copy-start.2 = (f32[3,384,512]{2,1,0:T(8,128)S(1)}, f32[3,384,512]{2,1,0:T(8,128)}, u32[]{:S(2)}) copy-start(f32[3,384,512]{2,1,0:T(8,128)} %copy-done.1) | copy-start | bytes 7077892
  464.0 34.0 %copy-start.6 = (f32[512]{0:T(512)S(1)}, f32[512]{0:T(512)}, u32[]{:S(2)}) copy-start(f32[512]{0:T(512)} %param.12) | copy-start | bytes 6148
Sparse Core Ops, SparseCore 0:
  500.8 30.8 all-gather.1
where the time goes:
time: 548 us; the launch traced here: 544 us
  waiting for transfers between devices  319 us (58%)
  matrix products  95.5 us (17%)
  starting transfers between devices  61.3 us (11%)
  local copies, waits for them, and re-layouts  41.5 us (8%)
  between operations  14 us (3%)
  other arithmetic  13.5 us (2%)
    all_to_all x2, waiting for transfers between devices, sequence_conv(): lax.all_to_all(sectioned[0], 'seq', split_axis=1, concat_axis=2, tiled=True)  95 us
    dot_general x16, matrix products, contract(): return jnp.einsum(pattern, first_op, second_op, precision=highest)  89.8 us
    all_to_all x2, waiting for transfers between devices, sequence_conv(): lax.all_to_all(sectioned[1], 'seq', split_axis=1, concat_axis=2, tiled=True)  88.2 us
    all_to_all x1, waiting for transfers between devices, sequence_conv(): lax.all_to_all(planes, 'seq', split_axis=2, concat_axis=1, tiled=True)  36.7 us
    all_to_all x1, waiting for transfers between devices, sequence_conv(): lax.all_to_all(sectioned[0], 'seq', split_axis=2, concat_axis=1, tiled=True)  34.6 us
    all_to_all x1, waiting for transfers between devices, sequence_conv(): lax.all_to_all(sectioned[1], 'seq', split_axis=2, concat_axis=1, tiled=True)  33.1 us
    all_gather x1, waiting for transfers between devices, on_device(): lax.all_gather(mixed, 'ch', axis=1, tiled=True)  31 us
    all_to_all x2, starting transfers between devices, sequence_conv(): lax.all_to_all(sectioned[1], 'seq', split_axis=1, concat_axis=2, tiled=True)  15.6 us
  transfers between devices with their start and end apart: 9, of which 8 were waited for; matrix products, arithmetic and copies ran while one was open for 8% of the time, Pallas kernels for 0%

commit v1 on v0

v1 whole, which is shorter than its diff:
```python
import math

import jax
import jax.numpy as jnp
import numpy as np
from jax import lax
from jax.sharding import PartitionSpec as P

high = lax.Precision.HIGH


def contract(pattern, first_op, second_op):
    return jnp.einsum(
        pattern, first_op, second_op, precision=high, preferred_element_type=jnp.float32
    )


def tables(seq_len, inner):
    total = 2 * seq_len
    outer = total // inner
    half = seq_len // inner
    k1 = np.arange(outer)[:, None]
    n1 = np.arange(half)[None, :]
    a1 = 2.0 * np.pi * ((k1 * n1) % outer) / outer
    n2 = np.arange(inner)[None, :]
    at = 2.0 * np.pi * ((k1 * n2) % total) / total
    m2 = np.arange(inner)
    a2 = 2.0 * np.pi * ((m2[:, None] * m2[None, :]) % inner) / inner
    f32 = lambda v: jnp.asarray(v, jnp.float32)
    return dict(
        c1=f32(np.cos(a1)),
        s1=f32(np.sin(a1)),
        tc=f32(np.cos(at)[:, :, None]),
        ts=f32(np.sin(at)[:, :, None]),
        c2=f32(np.cos(a2)),
        s2=f32(np.sin(a2)),
        c1i=f32(np.cos(a1).T / total),
        s1i=f32(np.sin(a1).T / total),
    )


def forward(signal, tb):
    br = contract("kn,nmc->kmc", tb["c1"], signal)
    bi = -contract("kn,nmc->kmc", tb["s1"], signal)
    tr, ti = tb["tc"], -tb["ts"]
    br, bi = br * tr - bi * ti, br * ti + bi * tr
    xr = contract("kmc,mj->kjc", br, tb["c2"]) + contract("kmc,mj->kjc", bi, tb["s2"])
    xi = contract("kmc,mj->kjc", bi, tb["c2"]) - contract("kmc,mj->kjc", br, tb["s2"])
    return xr, xi


def inverse(yr, yi, tb):
    zr = contract("kjc,jm->kmc", yr, tb["c2"]) - contract("kjc,jm->kmc", yi, tb["s2"])
    zi = contract("kjc,jm->kmc", yr, tb["s2"]) + contract("kjc,jm->kmc", yi, tb["c2"])
    tc, ts = tb["tc"], tb["ts"]
    zr, zi = zr * tc - zi * ts, zr * ts + zi * tc
    return contract("nk,kmc->nmc", tb["c1i"], zr) - contract("nk,kmc->nmc", tb["s1i"], zi)


def long_conv(mixed_in, long_filter, inner):
    seq_len, width = mixed_in.shape
    half = seq_len // inner
    tb = tables(seq_len, inner)
    xr, xi = forward(mixed_in.reshape(half, inner, width), tb)
    hr, hi = forward(long_filter.reshape(half, inner, width), tb)
    yr = xr * hr - xi * hi
    yi = xr * hi + xi * hr
    return inverse(yr, yi, tb).reshape(seq_len, width)


def short_conv(signal, taps):
    tap_count = taps.shape[0]
    widened = jnp.pad(signal, ((tap_count - 1, 0), (0, 0)))
    seq_len = signal.shape[0]
    summed = taps[0] * widened[tap_count - 1 :]
    for offset in range(1, tap_count):
        start = tap_count - 1 - offset
        summed = summed + taps[offset] * widened[start : start + seq_len]
    return summed


def on_device(out_gate, in_gate, values, short_filter, long_filter, skip_gain, out_weight):
    seq_count = lax.axis_size("seq")
    seq_index = lax.axis_index("seq")
    width = out_gate.shape[1] // seq_count
    stacked = jnp.stack([out_gate, in_gate, values])
    spread = lax.all_to_all(stacked, "seq", split_axis=2, concat_axis=1, tiled=True)
    filt = lax.all_to_all(long_filter, "seq", split_axis=1, concat_axis=0, tiled=True)
    start = seq_index * width
    taps = lax.dynamic_slice_in_dim(short_filter, start, width, axis=2)
    gain = lax.dynamic_slice_in_dim(skip_gain, start, width, axis=0)
    spread = spread.astype(jnp.float32)
    gate_late = short_conv(spread[0], taps[0])
    mixed_in = short_conv(spread[1], taps[1]) * short_conv(spread[2], taps[2])
    long_out = long_conv(mixed_in, filt, 192)
    filtered = long_out + gain * mixed_in
    mixed = (gate_late * filtered).astype(jnp.bfloat16)
    mixed = lax.all_to_all(mixed, "seq", split_axis=0, concat_axis=1, tiled=True)
    summed = jnp.dot(
        lax.all_gather(mixed, "ch", axis=1, tiled=True),
        out_weight,
        preferred_element_type=jnp.float32,
    )
    return summed.astype(jnp.bfloat16)


def solution(mesh):
    return jax.shard_map(
        on_device,
        mesh=mesh,
        in_specs=(
            P("seq", "ch"),
            P("seq", "ch"),
            P("seq", "ch"),
            P(None, None, "ch"),
            P("seq", "ch"),
            P("ch"),
            P(None, "ch"),
        ),
        out_specs=P("seq", "ch"),
        check_vma=False,
    )
```

time: 548 us -> 171 us (0.31)
  waiting for transfers between devices: 319 us -> 71.9 us
  matrix products: 95.5 us -> 29.1 us
  starting transfers between devices: 61.3 us -> 20.3 us
  local copies, waits for them, and re-layouts: 41.5 us -> 15.1 us
  blocking collectives: 0 us -> 18.3 us
  other arithmetic: 13.5 us -> 1.73 us
    all_to_all x7 -> x2, waiting for transfers between devices: 288 us -> 40.2 us  [the longest x1 23.4 us: on_device(): lax.all_to_all(stacked, 'seq', split_axis=2, concat_axis=1, tiled=True)]
    dot_general x16 -> x18, matrix products: 89.8 us -> 23.4 us  [contract(): jnp.einsum(pattern, first_op, second_op, precision=high, preferred_elemen...]
    all_to_all x7 -> x2, starting transfers between devices: 56.6 us -> 20.2 us  [the longest x1 11.9 us: on_device(): lax.all_to_all(long_filter, 'seq', split_axis=1, concat_axis=0, tiled=True)]
    all_to_all x0 -> x1, blocking collectives: none -> 18.3 us  [on_device(): lax.all_to_all(mixed, 'seq', split_axis=0, concat_axis=1, tiled=True)]
    add x3 -> x0, local copies, waits for them, and re-layouts: 10 us -> none  [the longest x2 7.65 us: complex_times(): first_op[0] * second_op[1] + first_op[1] * second_op[0]]
    sub x3 -> x1, local copies, waits for them, and re-layouts: 8.2 us -> 1.75 us  [inverse(): contract('nk,kmc->nmc', tb['c1i'], zr)]
    another operation x3 -> x1, local copies, waits for them, and re-layouts: 8.44 us -> 2.3 us  [on_device(): stacked = jnp.stack([out_gate, in_gate, values])]
    slice x3 -> x1, local copies, waits for them, and re-layouts: 6.23 us -> 0.15 us  [on_device(): gate_late = short_conv(spread[0], taps[0])]
  transfers between devices with their start and end apart: 9 -> 3, of which waited for: 8 -> 3; matrix products, arithmetic and copies ran while one was open for 8% -> 9% of each run, Pallas kernels for 0% -> 0%
where the time goes in v1:
time: 171 us; the launch traced here: 170 us
  waiting for transfers between devices  71.9 us (42%)
  matrix products  29.1 us (17%)
  starting transfers between devices  20.3 us (12%)
  blocking collectives  18.3 us (11%)
  local copies, waits for them, and re-layouts  15.1 us (9%)
  between operations  13.8 us (8%)
  other arithmetic  1.73 us (1%)
    all_gather x1, waiting for transfers between devices, on_device(): lax.all_gather(mixed, 'ch', axis=1, tiled=True)  31.7 us
    all_to_all x1, waiting for transfers between devices, on_device(): lax.all_to_all(stacked, 'seq', split_axis=2, concat_axis=1, tiled=True)  23.4 us
    dot_general x18, matrix products, contract(): jnp.einsum(pattern, first_op, second_op, precision=high, preferred_elemen...  23.4 us
    all_to_all x1, blocking collectives, on_device(): lax.all_to_all(mixed, 'seq', split_axis=0, concat_axis=1, tiled=True)  18.3 us
    all_to_all x1, waiting for transfers between devices, on_device(): lax.all_to_all(long_filter, 'seq', split_axis=1, concat_axis=0, tiled=True)  16.8 us
    all_to_all x1, starting transfers between devices, on_device(): lax.all_to_all(long_filter, 'seq', split_axis=1, concat_axis=0, tiled=True)  11.9 us
    all_to_all x1, starting transfers between devices, on_device(): lax.all_to_all(stacked, 'seq', split_axis=2, concat_axis=1, tiled=True)  8.36 us
    dot_general x1, matrix products, on_device(): jnp.dot(lax.all_gather(mixed, 'ch', axis=1, tiled=True), out_weight, pref...  5.7 us
  transfers between devices with their start and end apart: 3, of which 3 were waited for; matrix products, arithmetic and copies ran while one was open for 9% of the time, Pallas kernels for 0%

profile of v1, /device:TPU:1, one launch (start us, length us, event | category | flops | bytes accessed | tf_op | source)
XLA Modules:
  0.0 170.3 jit_solution(440597330835324851)
XLA Ops:
  6.5 2.4 %copy.57 = f32[384,512]{0,1:T(8,128)} copy(f32[384,512]{1,0:T(8,128)} %param.19) | data formatting | bytes 1572864 | tf_op args[4]
  8.9 11.9 %all-to-all-start.1 = ((f32[384,32,16]{0,2,1:T(8,128)}), f32[384,32,16]{0,2,1:T(8,128)S(1)}, u32[]{:S(2)}, u32[]{:S(2)}) async-start(f32[384,32,16]{0,2,1:T(8,128)} %bitcast.20), calls=%async_computation.1 | async-start | bytes 1572864 | tf_op jit(solution)/shard_map/all_to_all | solution.py:88
  21.0 2.3 %copy.50 = bf16[3,384,512]{1,0,2:T(4,128)(2,1)} copy(bf16[3,384,512]{2,1,0:T(8,128)(2,1)S(1)} %pad_maximum_fusion) | data formatting | bytes 2359296 | tf_op jit(solution)/shard_map/stack | solution.py:86
  23.3 16.8 %all-to-all-done.1 = f32[384,32,16]{0,2,1:T(8,128)S(1)} async-done(((f32[384,32,16]{0,2,1:T(8,128)}), f32[384,32,16]{0,2,1:T(8,128)S(1)}, u32[]{:S(2)}, u32[]{:S(2)}) %all-to-all-start.1) | async-done | bytes 786464 | tf_op jit(solution)/shard_map/all_to_all | solution.py:88
  40.1 8.4 %all-to-all-start = ((bf16[3,384,512]{1,0,2:T(4,128)(2,1)}), bf16[3,384,512]{1,0,2:T(4,128)(2,1)S(1)}, u32[]{:S(2)}, u32[]{:S(2)}) async-start(bf16[3,384,512]{1,0,2:T(4,128)(2,1)} %copy.50), calls=%async_computation | async-start | bytes 3145728 | tf_op jit(solution)/shard_map/all_to_all | solution.py:87
  50.1 1.1 copy.58
  51.3 1.4 reshape.45
  52.7 1.4 convolution_negate_fusion
  54.1 1.4 fusion.39
  57.5 2.1 %convolution_subtract_fusion = f32[128,16,192]{0,2,1:T(8,128)} fusion(f32[128,16,192]{0,2,1:T(8,128)S(1)} %fusion.23, f32[192,192,1]{0,1,2:T(8,128)S(1)} %copy-done.2, f32[128,192,16]{0,1,2:T(8,128)S(1)} %convolution_negate_fusion, f32[128,192,16]{0,1,2:T(8,128)S(1)} %fusion.39, f32[128,192]{0,1:T(8,128)S(1)} %copy-done.5, f32[128,192]{0,1:T(8,128)S(1)} %copy-done), kind=kOutput, calls=%fused_computation.28 | convolution fusion | flops 454557696 | bytes 6635520 | tf_op jit(solution)/shard_map/kmc,mj->kjc/dot_general | solution.py:13
  59.7 2.1 %convolution_add_fusion = f32[128,16,192]{0,2,1:T(8,128)} fusion(f32[128,16,192]{0,2,1:T(8,128)S(1)} %fusion.22, f32[192,192,1]{0,1,2:T(8,128)S(1)} %copy-done.2, f32[128,192,16]{0,1,2:T(8,128)S(1)} %convolution_negate_fusion, f32[128,192,16]{0,1,2:T(8,128)S(1)} %fusion.39, f32[128,192]{0,1:T(8,128)S(1)} %copy-done.5, f32[128,192]{0,1:T(8,128)S(1)} %copy-done), kind=kOutput, calls=%fused_computation.30 | convolution fusion | flops 454557696 | bytes 6635520 | tf_op jit(solution)/shard_map/kmc,mj->kjc/dot_general | solution.py:13
  61.8 23.4 %all-to-all-done = bf16[3,384,512]{1,0,2:T(4,128)(2,1)S(1)} async-done(((bf16[3,384,512]{1,0,2:T(4,128)(2,1)}), bf16[3,384,512]{1,0,2:T(4,128)(2,1)S(1)}, u32[]{:S(2)}, u32[]{:S(2)}) %all-to-all-start) | async-done | bytes 1179680 | tf_op jit(solution)/shard_map/all_to_all | solution.py:87
  87.2 1.4 convolution_negate_fusion.1
  88.7 1.4 fusion.38
  90.1 1.2 fusion.24
  94.1 1.5 multiply_subtract_fusion
  99.2 1.2 subtract_bitcast_fusion.1
  100.5 1.5 fusion.10
  102.0 1.6 subtract_bitcast_fusion
  103.6 1.7 %copy.61 = f32[64,192,16]{1,0,2:T(8,128)} copy(f32[64,192,16]{0,2,1:T(8,128)S(1)} %subtract_bitcast_fusion) | data formatting | bytes 1572864 | tf_op jit(solution)/shard_map/sub | solution.py:57
  105.4 1.7 reshape.46
  107.6 18.3 %all_to_all.44 = bf16[32,384,16]{1,2,0:T(8,128)(2,1)} all-to-all(bf16[32,384,16]{1,2,0:T(8,128)(2,1)S(1)} %bitcast.133), channel_id=1, replica_groups=mesh['seq'=32,'ch'=8] {'seq'}, dimensions={0} | all-to-all | bytes 786432 | tf_op jit(solution)/shard_map/all_to_all | solution.py:98
  126.0 31.7 %all-gather.2.cloned.1.call-done = bf16[384,4096]{0,1:T(8,128)(2,1)} async-done(((bf16[384,512]{0,1:T(8,128)(2,1)}), bf16[384,4096]{0,1:T(8,128)(2,1)}) %all-gather.2.cloned.1.call-update) | async-done | bytes 3145744 | tf_op jit(solution)/shard_map/all_gather | solution.py:100
  157.7 5.7 %convolution_convert_fusion = bf16[384,512]{1,0:T(8,128)(2,1)} fusion(bf16[384,4096]{0,1:T(8,128)(2,1)} %all-gather.2.cloned.1.call-done, bf16[4096,512]{1,0:T(8,128)(2,1)} %param.21), kind=kOutput, calls=%fused_computation.32 | convolution fusion | flops 1610809344 | bytes 7733248 | tf_op jit(solution)/shard_map/dot_general | solution.py:99
  (52 shorter events, 12.7 us)
Async XLA Ops:
  6.5 14.3 %copy-start.7 = (bf16[384,512]{1,0:T(8,128)(2,1)S(1)}, bf16[384,512]{1,0:T(8,128)(2,1)}, u32[]{:S(2)}) copy-start(bf16[384,512]{1,0:T(8,128)(2,1)} %param.17) | copy-start | bytes 1179652
  6.5 14.3 %copy-start.8 = (bf16[384,512]{1,0:T(8,128)(2,1)S(1)}, bf16[384,512]{1,0:T(8,128)(2,1)}, u32[]{:S(2)}) copy-start(bf16[384,512]{1,0:T(8,128)(2,1)} %param.16) | copy-start | bytes 1179652
  6.5 14.3 %copy-start.9 = (bf16[384,512]{1,0:T(8,128)(2,1)S(1)}, bf16[384,512]{1,0:T(8,128)(2,1)}, u32[]{:S(2)}) copy-start(bf16[384,512]{1,0:T(8,128)(2,1)} %param.15) | copy-start | bytes 1179652
  8.9 31.1 %all-to-all-start.1 = ((f32[384,32,16]{0,2,1:T(8,128)}), f32[384,32,16]{0,2,1:T(8,128)S(1)}, u32[]{:S(2)}, u32[]{:S(2)}) async-start(f32[384,32,16]{0,2,1:T(8,128)} %bitcast.20), calls=%async_computation.1 | async-start | bytes 1572864 | tf_op jit(solution)/shard_map/all_to_all | solution.py:88
  40.1 45.2 %all-to-all-start = ((bf16[3,384,512]{1,0,2:T(4,128)(2,1)}), bf16[3,384,512]{1,0,2:T(4,128)(2,1)S(1)}, u32[]{:S(2)}, u32[]{:S(2)}) async-start(bf16[3,384,512]{1,0,2:T(4,128)(2,1)} %copy.50), calls=%async_computation | async-start | bytes 3145728 | tf_op jit(solution)/shard_map/all_to_all | solution.py:87
  48.4 109.3 %all-gather.2.cloned.1.call-start = ((), (), s32[]{:S(2)}) async-start(), calls=%async_computation.3 | async-start | bytes 3538944 | tf_op jit(solution)/shard_map/all_gather | solution.py:100
  50.1 2.5 %copy-start.11 = (f32[128,64,1]{0,1,2:T(8,128)S(1)}, f32[128,64,1]{0,1,2:T(8,128)}, u32[]{:S(2)}) copy-start(f32[128,64,1]{0,1,2:T(8,128)} %constant.49) | copy-start | bytes 98308
  52.7 1.4 copy-start.10
  54.1 1.5 copy-start
  54.1 1.5 copy-start.1
  54.1 1.5 copy-start.5
  56.6 1.0 copy-start.2
  92.2 1.4 copy-start.3
  92.2 1.9 %copy-start.4 = (f32[128,16,192]{0,2,1:T(8,128)S(1)}, f32[128,16,192]{0,2,1:T(8,128)}, u32[]{:S(2)}) copy-start(f32[128,16,192]{0,2,1:T(8,128)} %convolution_add_fusion) | copy-start | bytes 4718596
  98.2 0.9 copy-start.12
  99.2 1.3 copy-start.14
  100.5 1.6 copy-start.13
  105.4 1.7 copy-start.6
Sparse Core Ops, SparseCore 0:
  126.1 31.5 all-gather.1

commit v2 on v1

v2 whole, which is shorter than its diff:
```python
import jax
import jax.numpy as jnp
import numpy as np
from jax import lax
from jax.sharding import PartitionSpec as P

high = lax.Precision.HIGH
LANES = 128


def contract(pattern, first_op, second_op):
    return jnp.einsum(
        pattern, first_op, second_op, precision=high, preferred_element_type=jnp.float32
    )


def tables(seq_len):
    total = 2 * seq_len
    outer = total // LANES
    half = seq_len // LANES
    k1 = np.arange(outer)[:, None]
    a1 = 2.0 * np.pi * ((k1 * np.arange(half)[None, :]) % outer) / outer
    at = 2.0 * np.pi * ((k1 * np.arange(LANES)[None, :]) % total) / total
    m2 = np.arange(LANES)
    a2 = 2.0 * np.pi * ((m2[:, None] * m2[None, :]) % LANES) / LANES
    c1, s1 = np.cos(a1), np.sin(a1)
    c2, s2 = np.cos(a2), np.sin(a2)
    f32 = lambda v: jnp.asarray(v, jnp.float32)
    return dict(
        first=f32(np.concatenate([c1, -s1], axis=0)),
        tc=f32(np.cos(at)[:, None, :]),
        ts=f32(np.sin(at)[:, None, :]),
        fwd2=f32(np.block([[c2, -s2], [s2, c2]])),
        inv2=f32(np.block([[c2, s2], [-s2, c2]])),
        last=f32(np.concatenate([c1.T, -s1.T], axis=1) / total),
    )


def forward(signal, tb):
    outer = tb["tc"].shape[0]
    both = contract("kn,ncm->kcm", tb["first"], signal)
    br, bi = both[:outer], both[outer:]
    tr, ti = tb["tc"], -tb["ts"]
    twisted = jnp.concatenate([br * tr - bi * ti, br * ti + bi * tr], axis=2)
    return contract("kcm,mj->kcj", twisted, tb["fwd2"])


def inverse(spectrum, tb):
    z = contract("kcj,jm->kcm", spectrum, tb["inv2"])
    zr, zi = z[:, :, :LANES], z[:, :, LANES:]
    tc, ts = tb["tc"], tb["ts"]
    stacked = jnp.concatenate([zr * tc - zi * ts, zr * ts + zi * tc], axis=0)
    return contract("nk,kcm->ncm", tb["last"], stacked)


def long_conv(mixed_in, long_filter):
    half = mixed_in.shape[0]
    tb = tables(half * LANES)
    xs = forward(mixed_in, tb)
    hs = forward(long_filter, tb)
    xr, xi = xs[:, :, :LANES], xs[:, :, LANES:]
    hr, hi = hs[:, :, :LANES], hs[:, :, LANES:]
    product = jnp.concatenate([xr * hr - xi * hi, xr * hi + xi * hr], axis=2)
    return inverse(product, tb)


def shift_seq(signal, distance):
    rows, width, lanes = signal.shape
    prev = jnp.concatenate([jnp.zeros((1, width, lanes), signal.dtype), signal[:-1]], axis=0)
    return jnp.concatenate(
        [prev[:, :, lanes - distance :], signal[:, :, : lanes - distance]], axis=2
    )


def short_conv(signal, taps):
    summed = taps[0][None, :, None] * signal
    for offset in range(1, taps.shape[0]):
        summed = summed + taps[offset][None, :, None] * shift_seq(signal, offset)
    return summed


def to_ncm(block):
    rows, width = block.shape
    return block.reshape(rows // LANES, LANES, width).transpose(0, 2, 1)


def on_device(out_gate, in_gate, values, short_filter, long_filter, skip_gain, out_weight):
    seq_count = lax.axis_size("seq")
    seq_index = lax.axis_index("seq")
    rows = out_gate.shape[0]
    width = out_gate.shape[1] // seq_count
    stacked = jnp.stack([to_ncm(out_gate), to_ncm(in_gate), to_ncm(values)])
    spread = lax.all_to_all(stacked, "seq", split_axis=2, concat_axis=1, tiled=True)
    filt = lax.all_to_all(to_ncm(long_filter), "seq", split_axis=1, concat_axis=0, tiled=True)
    start = seq_index * width
    taps = lax.dynamic_slice_in_dim(short_filter, start, width, axis=2)
    gain = lax.dynamic_slice_in_dim(skip_gain, start, width, axis=0)
    spread = spread.astype(jnp.float32)
    gate_late = short_conv(spread[0], taps[0])
    mixed_in = short_conv(spread[1], taps[1]) * short_conv(spread[2], taps[2])
    long_out = long_conv(mixed_in, filt)
    filtered = long_out + gain[None, :, None] * mixed_in
    mixed = (gate_late * filtered).astype(jnp.bfloat16)
    mixed = lax.all_to_all(mixed, "seq", split_axis=0, concat_axis=1, tiled=True)
    gathered = lax.all_gather(mixed, "ch", axis=1, tiled=True)
    summed = jnp.einsum(
        "ncm,co->nmo", gathered, out_weight, preferred_element_type=jnp.float32
    )
    return summed.reshape(rows, -1).astype(jnp.bfloat16)


def solution(mesh):
    return jax.shard_map(
        on_device,
        mesh=mesh,
        in_specs=(
            P("seq", "ch"),
            P("seq", "ch"),
            P("seq", "ch"),
            P(None, None, "ch"),
            P("seq", "ch"),
            P("ch"),
            P(None, "ch"),
        ),
        out_specs=P("seq", "ch"),
        check_vma=False,
    )
```

time: 171 us -> 180 us (1.053)
  waiting for transfers between devices: 71.9 us -> 87.4 us
  matrix products: 29.1 us -> 19.5 us
  other arithmetic: 1.73 us -> 4.42 us
    all_to_all x1, waiting for transfers between devices: 23.4 us -> 33.5 us  [on_device(): lax.all_to_all(stacked, 'seq', split_axis=2, concat_axis=1, tiled=True)]
    dot_general x18 -> x6, matrix products: 23.4 us -> 13.9 us  [contract(): jnp.einsum(pattern, first_op, second_op, precision=high, preferred_elemen...]
    all_to_all x1, waiting for transfers between devices: 16.8 us -> 22.1 us  [on_device(): lax.all_to_all(to_ncm(long_filter), 'seq', split_axis=1, concat_axis=0, t...]
    reshape x3 -> x0, local copies, waits for them, and re-layouts: 3.51 us -> none  [the longest x1 1.69 us: long_conv(): return inverse(yr, yi, tb).reshape(seq_len, width)]
    transpose x0 -> x1, local copies, waits for them, and re-layouts: none -> 2.55 us  [to_ncm(): return block.reshape(rows // LANES, LANES, width).transpose(0, 2, 1)]
    slice x0 -> x10, local copies, waits for them, and re-layouts: none -> 2.34 us  [the longest x6 1.61 us: shift_seq(): prev[:, :, lanes - distance:]]
    sub x0 -> x3, other arithmetic: none -> 1.87 us  [the longest x1 1.01 us: forward(): twisted = jnp.concatenate([br * tr - bi * ti, br * ti + bi * tr], axis=2)]
    unnamed x34 -> x29, local copies, waits for them, and re-layouts: 4.38 us -> 3.67 us
  transfers between devices with their start and end apart: 3 -> 3, of which waited for: 3 -> 3; matrix products, arithmetic and copies ran while one was open for 9% -> 3% of each run, Pallas kernels for 0% -> 0%
where the time goes in v2:
time: 180 us
  waiting for transfers between devices  87.4 us (49%)
  starting transfers between devices  20.6 us (11%)
  matrix products  19.5 us (11%)
  blocking collectives  18.2 us (10%)
  local copies, waits for them, and re-layouts  15.7 us (9%)
  between operations  13.8 us (8%)
  other arithmetic  4.42 us (2%)
    all_to_all x1, waiting for transfers between devices, on_device(): lax.all_to_all(stacked, 'seq', split_axis=2, concat_axis=1, tiled=True)  33.5 us
    all_gather x1, waiting for transfers between devices, on_device(): gathered = lax.all_gather(mixed, 'ch', axis=1, tiled=True)  31.7 us
    all_to_all x1, waiting for transfers between devices, on_device(): lax.all_to_all(to_ncm(long_filter), 'seq', split_axis=1, concat_axis=0, t...  22.1 us
    all_to_all x1, blocking collectives, on_device(): lax.all_to_all(mixed, 'seq', split_axis=0, concat_axis=1, tiled=True)  18.2 us
    dot_general x6, matrix products, contract(): jnp.einsum(pattern, first_op, second_op, precision=high, preferred_elemen...  13.9 us
    all_to_all x1, starting transfers between devices, on_device(): lax.all_to_all(to_ncm(long_filter), 'seq', split_axis=1, concat_axis=0, t...  11.9 us
    all_to_all x1, starting transfers between devices, on_device(): lax.all_to_all(stacked, 'seq', split_axis=2, concat_axis=1, tiled=True)  8.7 us
    dot_general x1, matrix products, on_device(): jnp.einsum('ncm,co->nmo', gathered, out_weight, preferred_element_type=jn...  5.68 us
  transfers between devices with their start and end apart: 3, of which 3 were waited for; matrix products, arithmetic and copies ran while one was open for 3% of the time, Pallas kernels for 0%

profile of v2, /device:TPU:1, one launch (start us, length us, event | category | flops | bytes accessed | tf_op | source)
XLA Modules:
  0.0 179.7 jit_solution(8522045096169225749)
XLA Ops:
  6.5 2.5 %copy.88 = f32[3,512,128]{2,0,1:T(4,128)} copy(f32[3,512,128]{1,2,0:T(8,128)} %bitcast.97) | data formatting | bytes 1572864 | tf_op jit(solution)/shard_map/transpose | solution.py:84
  9.1 11.9 %all-to-all-start.1 = ((f32[3,512,128]{2,0,1:T(4,128)}), f32[3,512,128]{2,0,1:T(4,128)S(1)}, u32[]{:S(2)}, u32[]{:S(2)}) async-start(f32[3,512,128]{2,0,1:T(4,128)} %copy.88), calls=%async_computation.1 | async-start | bytes 2097152 | tf_op jit(solution)/shard_map/all_to_all | solution.py:94
  21.1 2.3 %copy.69 = bf16[3,3,512,128]{3,1,0,2:T(4,128)(2,1)} copy(bf16[3,3,512,128]{2,3,1,0:T(8,128)(2,1)S(1)} %pad_maximum_fusion.3) | data formatting | bytes 2359296 | tf_op jit(solution)/shard_map/stack | solution.py:92
  23.4 22.1 %all-to-all-done.1 = f32[3,512,128]{2,0,1:T(4,128)S(1)} async-done(((f32[3,512,128]{2,0,1:T(4,128)}), f32[3,512,128]{2,0,1:T(4,128)S(1)}, u32[]{:S(2)}, u32[]{:S(2)}) %all-to-all-start.1) | async-done | bytes 786464 | tf_op jit(solution)/shard_map/all_to_all | solution.py:94
  45.6 8.7 %all-to-all-start = ((bf16[3,3,512,128]{3,1,0,2:T(4,128)(2,1)}), bf16[3,3,512,128]{3,1,0,2:T(4,128)(2,1)}, u32[]{:S(2)}, u32[]{:S(2)}) async-start(bf16[3,3,512,128]{3,1,0,2:T(4,128)(2,1)} %copy.69), calls=%async_computation | async-start | bytes 3145728 | tf_op jit(solution)/shard_map/all_to_all | solution.py:93
  54.4 0.8 dynamic_slice.7
  55.1 0.9 fusion.34
  56.1 1.5 fusion.31
  57.6 33.5 %all-to-all-done = bf16[3,3,512,128]{3,1,0,2:T(4,128)(2,1)} async-done(((bf16[3,3,512,128]{3,1,0,2:T(4,128)(2,1)}), bf16[3,3,512,128]{3,1,0,2:T(4,128)(2,1)}, u32[]{:S(2)}, u32[]{:S(2)}) %all-to-all-start) | async-done | bytes 1179680 | tf_op jit(solution)/shard_map/all_to_all | solution.py:93
  91.1 1.6 copy.70
  93.2 0.5 copy_bitcast_fusion
  97.0 1.5 fusion.28
  98.5 1.5 fusion.41
  100.0 1.0 multiply_subtract_fusion.3
  101.3 0.7 copy-done
  102.0 3.1 %fusion.10 = f32[192,16,256]{2,1,0:T(8,128)S(1)} fusion(f32[256,256,1]{1,0,2:T(8,128)S(1)} %copy-done, f32[192,16,256]{2,0,1:T(8,128)S(1)} %pad_maximum_fusion), kind=kOutput, calls=%fused_computation.13 | convolution fusion | flops 1207959552 | bytes 6553600 | tf_op jit(solution)/shard_map/kcm,mj->kcj/dot_general | solution.py:12
  105.4 3.0 %fusion.8 = f32[192,16,256]{2,1,0:T(8,128)S(1)} fusion(f32[256,256,1]{1,0,2:T(8,128)S(1)} %copy-done, f32[192,16,256]{2,0,1:T(8,128)S(1)} %pad_maximum_fusion.1), kind=kOutput, calls=%fused_computation.11 | convolution fusion | flops 1207959552 | bytes 6553600 | tf_op jit(solution)/shard_map/kcm,mj->kcj/dot_general | solution.py:12
  109.6 0.7 copy-done.5
  110.3 3.0 %fusion.6 = f32[192,16,256]{2,0,1:T(8,128)S(1)} fusion(f32[256,256,1]{1,0,2:T(8,128)S(1)} %copy-done.5, f32[192,16,256]{2,1,0:T(8,128)S(1)} %pad_maximum_fusion.2), kind=kOutput, calls=%fused_computation.9 | convolution fusion | flops 1207959552 | bytes 6553600 | tf_op jit(solution)/shard_map/kcj,jm->kcm/dot_general | solution.py:12
  114.2 1.8 %fusion.18 = bf16[96,16,128]{2,0,1:T(8,128)(2,1)S(1)} fusion(f32[96,384,1]{1,0,2:T(8,128)S(1)} %copy-done.8, f32[192,16,128]{2,0,1:T(8,128)S(1)} %get-tuple-element.8, f32[192,16,128]{2,0,1:T(8,128)S(1)} %get-tuple-element.7, f32[96,16,127]{2,0,1:T(8,128)S(1)} %copy.120, f32[96,16,1]{2,0,1:T(8,128)S(1)} %pad_slice_fusion.5, f32[96,16,126]{2,0,1:T(8,128)S(1)} %copy.121, ...), kind=kOutput, calls=%fused_computation.26 | convolution fusion | flops 455933952 | bytes 6832384 | tf_op jit(solution)/shard_map/nk,kcm->ncm/dot_general | solution.py:12
  116.2 18.2 %all_to_all.45 = bf16[96,16,128]{2,1,0:T(8,128)(2,1)S(1)} all-to-all(bf16[96,16,128]{2,1,0:T(8,128)(2,1)S(1)} %copy.94), channel_id=1, replica_groups=mesh['seq'=32,'ch'=8] {'seq'}, dimensions={0} | all-to-all | bytes 786432 | tf_op jit(solution)/shard_map/all_to_all | solution.py:104
  134.4 0.9 copy.96
  135.4 31.7 %all-gather.2.cloned.1.call-done = bf16[3,4096,128]{1,2,0:T(8,128)(2,1)} async-done(((bf16[3,512,128]{1,2,0:T(8,128)(2,1)}), bf16[3,4096,128]{1,2,0:T(8,128)(2,1)}) %all-gather.2.cloned.1.call-update) | async-done | bytes 3145744 | tf_op jit(solution)/shard_map/all_gather | solution.py:105
  167.1 5.7 %fusion.21 = bf16[3,128,512]{2,1,0:T(8,128)(2,1)} fusion(bf16[3,4096,128]{1,2,0:T(8,128)(2,1)} %all-gather.2.cloned.1.call-done, bf16[4096,512]{1,0:T(8,128)(2,1)} %param.19), kind=kOutput, calls=%fused_computation.27 | convolution fusion | flops 1610809344 | bytes 7733248 | tf_op jit(solution)/shard_map/ncm,co->nmo/dot_general | solution.py:106
  (51 shorter events, 6.8 us)
Async XLA Ops:
  6.5 14.4 %copy-start.2 = (bf16[384,512]{1,0:T(8,128)(2,1)S(1)}, bf16[384,512]{1,0:T(8,128)(2,1)}, u32[]{:S(2)}) copy-start(bf16[384,512]{1,0:T(8,128)(2,1)} %param.15) | copy-start | bytes 1179652
  6.5 14.4 %copy-start.3 = (bf16[384,512]{1,0:T(8,128)(2,1)S(1)}, bf16[384,512]{1,0:T(8,128)(2,1)}, u32[]{:S(2)}) copy-start(bf16[384,512]{1,0:T(8,128)(2,1)} %param.14) | copy-start | bytes 1179652
  6.5 14.4 %copy-start.4 = (bf16[384,512]{1,0:T(8,128)(2,1)S(1)}, bf16[384,512]{1,0:T(8,128)(2,1)}, u32[]{:S(2)}) copy-start(bf16[384,512]{1,0:T(8,128)(2,1)} %param.13) | copy-start | bytes 1179652
  9.1 36.5 %all-to-all-start.1 = ((f32[3,512,128]{2,0,1:T(4,128)}), f32[3,512,128]{2,0,1:T(4,128)S(1)}, u32[]{:S(2)}, u32[]{:S(2)}) async-start(f32[3,512,128]{2,0,1:T(4,128)} %copy.88), calls=%async_computation.1 | async-start | bytes 2097152 | tf_op jit(solution)/shard_map/all_to_all | solution.py:94
  45.6 45.5 %all-to-all-start = ((bf16[3,3,512,128]{3,1,0,2:T(4,128)(2,1)}), bf16[3,3,512,128]{3,1,0,2:T(4,128)(2,1)}, u32[]{:S(2)}, u32[]{:S(2)}) async-start(bf16[3,3,512,128]{3,1,0,2:T(4,128)(2,1)} %copy.69), calls=%async_computation | async-start | bytes 3145728 | tf_op jit(solution)/shard_map/all_to_all | solution.py:93
  54.3 1.8 %copy-start.7 = (f32[384,96,1]{0,1,2:T(8,128)S(1)}, f32[384,96,1]{0,1,2:T(8,128)}, u32[]{:S(2)}) copy-start(f32[384,96,1]{0,1,2:T(8,128)} %constant.48) | copy-start | bytes 442372
  54.3 112.8 %all-gather.2.cloned.1.call-start = ((), (), s32[]{:S(2)}) async-start(), calls=%async_computation.3 | async-start | bytes 3538944 | tf_op jit(solution)/shard_map/all_gather | solution.py:105
  97.0 1.5 copy-start.6
  98.5 1.5 copy-start.1
  98.5 1.5 copy-start.9
  101.0 1.0 copy-start
  109.4 1.0 copy-start.5
  110.3 3.0 %copy-start.10 = (f32[192,128]{1,0:T(8,128)S(1)}, f32[192,128]{1,0:T(8,128)}, u32[]{:S(2)}) copy-start(f32[192,128]{1,0:T(8,128)} %constant.44) | copy-start | bytes 294916
  113.3 0.9 copy-start.8
Sparse Core Ops, SparseCore 0:
  135.5 31.5 all-gather.1

commit v3 on v2

--- a/solution.py
+++ b/solution.py
@@ -1,11 +1,78 @@
+import functools
+
 import jax
 import jax.numpy as jnp
 import numpy as np
 from jax import lax
+from jax.experimental import pallas as pl
+from jax.experimental.pallas import tpu as pltpu
 from jax.sharding import PartitionSpec as P
 
 high = lax.Precision.HIGH
 LANES = 128
+MESH = pl.DeviceIdType.MESH
+
+
+def exchange_kernel(group, count, *refs):
+    sources, targets = refs[:count], refs[count : 2 * count]
+    send_sem, recv_sem, local_sem = refs[2 * count :]
+    me = lax.axis_index("seq")
+    ch = lax.axis_index("ch")
+    barrier = pltpu.get_barrier_semaphore()
+    for step in range(1, group):
+        peer = lax.rem(me + step, group)
+        pl.semaphore_signal(barrier, inc=1, device_id=(peer, ch), device_id_type=MESH)
+    pl.semaphore_wait(barrier, group - 1)
+    locals_ = []
+    for a in range(count):
+        cp = pltpu.make_async_copy(sources[a].at[me], targets[a].at[me], local_sem.at[a])
+        cp.start()
+        locals_.append(cp)
+    sent = []
+    for step in range(1, group):
+        peer = lax.rem(me + step, group)
+        for a in range(count):
+            cp = pltpu.make_async_remote_copy(
+                src_ref=sources[a].at[peer],
+                dst_ref=targets[a].at[me],
+                send_sem=send_sem.at[a, step],
+                recv_sem=recv_sem.at[a, step],
+                device_id=(peer, ch),
+                device_id_type=MESH,
+            )
+            cp.start()
+            sent.append(cp)
+    for cp in locals_:
+        cp.wait()
+    for cp in sent:
+        cp.wait_send()
+    for step in range(1, group):
+        origin = lax.rem(me + group - step, group)
+        for a in range(count):
+            pltpu.make_async_remote_copy(
+                src_ref=sources[a].at[origin],
+                dst_ref=targets[a].at[origin],
+                send_sem=send_sem.at[a, step],
+                recv_sem=recv_sem.at[a, step],
+                device_id=(origin, ch),
+                device_id_type=MESH,
+            ).wait_recv()
+
+
+def exchange(arrays, group, tag):
+    count = len(arrays)
+    return pl.pallas_call(
+        functools.partial(exchange_kernel, group, count),
+        out_shape=[jax.ShapeDtypeStruct(a.shape, a.dtype) for a in arrays],
+        in_specs=[pl.BlockSpec(memory_space=pl.ANY)] * count,
+        out_specs=[pl.BlockSpec(memory_space=pl.ANY)] * count,
+        scratch_shapes=[
+            pltpu.SemaphoreType.DMA((count, group)),
+            pltpu.SemaphoreType.DMA((count, group)),
+            pltpu.SemaphoreType.DMA((count,)),
+        ],
+        compiler_params=pltpu.CompilerParams(collective_id=tag, has_side_effects=True),
+    )(*arrays)
 
 
 def contract(pattern, first_op, second_op):
@@ -89,9 +156,15 @@
     seq_index = lax.axis_index("seq")
     rows = out_gate.shape[0]
     width = out_gate.shape[1] // seq_count
-    stacked = jnp.stack([to_ncm(out_gate), to_ncm(in_gate), to_ncm(values)])
-    spread = lax.all_to_all(stacked, "seq", split_axis=2, concat_axis=1, tiled=True)
-    filt = lax.all_to_all(to_ncm(long_filter), "seq", split_axis=1, concat_axis=0, tiled=True)
+    half = rows // LANES
+
+    def by_target(block):
+        return to_ncm(block).reshape(half, seq_count, width, LANES).transpose(1, 0, 2, 3)
+
+    stacked = jnp.stack([by_target(out_gate), by_target(in_gate), by_target(values)], axis=1)
+    spread, filt = exchange([stacked, by_target(long_filter)], seq_count, 0)
+    spread = spread.transpose(1, 0, 2, 3, 4).reshape(3, seq_count * half, width, LANES)
+    filt = filt.reshape(seq_count * half, width, LANES)
     start = seq_index * width
     taps = lax.dynamic_slice_in_dim(short_filter, start, width, axis=2)
     gain = lax.dynamic_slice_in_dim(skip_gain, start, width, axis=0)
@@ -101,7 +174,8 @@
     long_out = long_conv(mixed_in, filt)
     filtered = long_out + gain[None, :, None] * mixed_in
     mixed = (gate_late * filtered).astype(jnp.bfloat16)
-    mixed = lax.all_to_all(mixed, "seq", split_axis=0, concat_axis=1, tiled=True)
+    (mixed,) = exchange([mixed.reshape(seq_count, half, width, LANES)], seq_count, 1)
+    mixed = mixed.transpose(1, 0, 2, 3).reshape(half, seq_count * width, LANES)
     gathered = lax.all_gather(mixed, "ch", axis=1, tiled=True)
     summed = jnp.einsum(
         "ncm,co->nmo", gathered, out_weight, preferred_element_type=jnp.float32

time: 180 us -> 168 us (0.933)
  Pallas kernels: 0 us -> 69 us
  waiting for transfers between devices: 87.4 us -> 32.5 us
  starting transfers between devices: 20.6 us -> 0.01 us
  blocking collectives: 18.2 us -> 0 us
  local copies, waits for them, and re-layouts: 15.7 us -> 23.2 us
  other arithmetic: 4.42 us -> 9.45 us
    pallas_call x0 -> x2, Pallas kernels: none -> 69 us  [exchange(): pl.pallas_call(functools.partial(exchange_kernel, group, count), out_shap...]
    all_to_all x2 -> x0, waiting for transfers between devices: 55.7 us -> none  [the longest x1 33.5 us: on_device(): lax.all_to_all(stacked, 'seq', split_axis=2, concat_axis=1, tiled=True)]
    all_to_all x2 -> x0, starting transfers between devices: 20.6 us -> none  [the longest x1 11.9 us: on_device(): lax.all_to_all(to_ncm(long_filter), 'seq', split_axis=1, concat_axis=0, t...]
    all_to_all x1 -> x0, blocking collectives: 18.2 us -> none  [on_device(): lax.all_to_all(mixed, 'seq', split_axis=0, concat_axis=1, tiled=True)]
    slice x6, local copies, waits for them, and re-layouts: 1.61 us -> 6.06 us  [shift_seq(): prev[:, :, lanes - distance:]]
    unnamed x29 -> x31, local copies, waits for them, and re-layouts: 3.67 us -> 7.93 us
    all_to_all x4 -> x0, local copies, waits for them, and re-layouts: 2.58 us -> none  [the longest x1 1.58 us: on_device(): lax.all_to_all(stacked, 'seq', split_axis=2, concat_axis=1, tiled=True)]
    mul x1, other arithmetic: 1.49 us -> 4 us  [on_device(): mixed_in = short_conv(spread[1], taps[1]) * short_conv(spread[2], taps[2])]
  transfers between devices with their start and end apart: 3 -> 1, of which waited for: 3 -> 1; matrix products, arithmetic and copies ran while one was open for 3% -> 0% of each run, Pallas kernels for 0% -> 0%
where the time goes in v3:
time: 168 us
  Pallas kernels  69 us (41%)
  waiting for transfers between devices  32.5 us (19%)
  local copies, waits for them, and re-layouts  23.2 us (14%)
  matrix products  20 us (12%)
  between operations  13.7 us (8%)
  other arithmetic  9.45 us (6%)
    pallas_call x2, Pallas kernels, exchange(): pl.pallas_call(functools.partial(exchange_kernel, group, count), out_shap...  69 us
    all_gather x1, waiting for transfers between devices, on_device(): gathered = lax.all_gather(mixed, 'ch', axis=1, tiled=True)  32.5 us
    dot_general x6, matrix products, contract(): jnp.einsum(pattern, first_op, second_op, precision=high, preferred_elemen...  14.3 us
    unnamed x31, local copies, waits for them, and re-layouts  7.93 us
    slice x6, local copies, waits for them, and re-layouts, shift_seq(): prev[:, :, lanes - distance:]  6.06 us
    dot_general x1, matrix products, on_device(): jnp.einsum('ncm,co->nmo', gathered, out_weight, preferred_element_type=jn...  5.68 us
    mul x1, other arithmetic, on_device(): mixed_in = short_conv(spread[1], taps[1]) * short_conv(spread[2], taps[2])  4 us
  transfers between devices with their start and end apart: 1, of which 1 were waited for; matrix products, arithmetic and copies ran while one was open for 0% of the time, Pallas kernels for 0%

profile of v3, /device:TPU:1, one launch (start us, length us, event | category | flops | bytes accessed | tf_op | source)
XLA Modules:
  0.0 167.9 jit_solution(6978648913723611979)
XLA Ops:
  6.5 1.3 copy.58
  7.9 1.2 copy.56
  10.7 1.2 pad_maximum_fusion.3.refs_0_
  11.9 55.3 %shard_map.127 = (bf16[32,3,3,16,128]{4,3,2,1,0:T(8,128)(2,1)}, f32[32,3,16,128]{3,2,1,0:T(8,128)}) custom-call(bf16[32,3,3,16,128]{4,3,2,1,0:T(8,128)(2,1)} %pad_maximum_fusion.3.refs_0_, f32[32,3,16,128]{3,2,1,0:T(8,128)} %bitcast.110), custom_call_target="tpu_custom_call" | custom-call | tf_op jit(solution)/shard_map/pallas_call | solution.py:64
  67.1 1.4 convert_bitcast_fusion
  69.5 1.2 pad_slice_fusion
  70.6 1.2 pad_slice_fusion.1
  72.0 1.1 pad_slice_fusion.2
  73.2 1.2 pad_slice_fusion.3
  74.9 1.1 pad_slice_fusion.5
  76.0 1.1 copy.106
  78.3 1.2 copy.108
  79.5 1.1 copy.109
  81.5 4.0 %fusion.28 = f32[96,16,128]{2,0,1:T(8,128)S(1)} fusion(f32[96,16,127]{2,0,1:T(8,128)} %copy.106, f32[96,16,1]{2,0,1:T(8,128)} %pad_slice_fusion.3, f32[96,16,126]{2,0,1:T(8,128)} %copy.107, f32[96,16,2]{2,0,1:T(8,128)} %pad_slice_fusion.2, f32[96,16,127]{2,0,1:T(8,128)} %copy.108, f32[96,16,1]{2,0,1:T(8,128)} %pad_slice_fusion.1, f32[96,16,126]{2,0,1:T(8,128)} %copy.109, ...), kind=kLoop, calls=%fused_computation.36 | loop fusion | flops 2949120 | bytes 5505408 | tf_op jit(solution)/shard_map/mul | solution.py:173
  85.5 1.5 fusion.41
  87.0 1.5 fusion.31
  88.5 1.3 multiply_subtract_fusion.3
  90.8 3.2 %fusion.10 = f32[192,16,256]{2,1,0:T(8,128)S(1)} fusion(f32[256,256,1]{1,0,2:T(8,128)S(1)} %copy-done.1, f32[192,16,256]{2,0,1:T(8,128)S(1)} %pad_maximum_fusion), kind=kOutput, calls=%fused_computation.13 | convolution fusion | flops 1207959552 | bytes 6553600 | tf_op jit(solution)/shard_map/kcm,mj->kcj/dot_general | solution.py:79
  94.2 3.0 %fusion.8 = f32[192,16,256]{2,1,0:T(8,128)S(1)} fusion(f32[256,256,1]{1,0,2:T(8,128)S(1)} %copy-done.1, f32[192,16,256]{2,0,1:T(8,128)S(1)} %pad_maximum_fusion.1), kind=kOutput, calls=%fused_computation.11 | convolution fusion | flops 1207959552 | bytes 6553600 | tf_op jit(solution)/shard_map/kcm,mj->kcj/dot_general | solution.py:79
  99.8 3.0 %fusion.6 = f32[192,16,256]{2,0,1:T(8,128)S(1)} fusion(f32[256,256,1]{1,0,2:T(8,128)S(1)} %copy-done.7, f32[192,16,256]{2,1,0:T(8,128)S(1)} %pad_maximum_fusion.2), kind=kOutput, calls=%fused_computation.9 | convolution fusion | flops 1207959552 | bytes 6553600 | tf_op jit(solution)/shard_map/kcj,jm->kcm/dot_general | solution.py:79
  104.0 2.2 %fusion.18 = bf16[96,16,128]{2,0,1:T(8,128)(2,1)S(1)} fusion(f32[96,384,1]{1,0,2:T(8,128)S(1)} %copy-done.8, f32[192,16,128]{2,0,1:T(8,128)S(1)} %get-tuple-element.12, f32[192,16,128]{2,0,1:T(8,128)S(1)} %get-tuple-element.11, f32[96,16,127]{2,0,1:T(8,128)S(1)} %copy.110, f32[96,16,1]{2,0,1:T(8,128)S(1)} %copy-done, f32[96,16,126]{2,0,1:T(8,128)S(1)} %copy.111, ...), kind=kOutput, calls=%fused_computation.26 | convolution fusion | flops 455933952 | bytes 6832384 | tf_op jit(solution)/shard_map/nk,kcm->ncm/dot_general | solution.py:79
  107.1 13.8 %shard_map.128 = bf16[32,3,16,128]{3,2,1,0:T(8,128)(2,1)} custom-call(bf16[32,3,16,128]{3,2,1,0:T(8,128)(2,1)} %bitcast.112), custom_call_target="tpu_custom_call" | custom-call | tf_op jit(solution)/shard_map/pallas_call | solution.py:64
  122.9 32.5 %all-gather.2.cloned.1.call-done = bf16[3,4096,128]{1,2,0:T(8,128)(2,1)} async-done(((bf16[3,512,128]{1,2,0:T(8,128)(2,1)}), bf16[3,4096,128]{1,2,0:T(8,128)(2,1)}) %all-gather.2.cloned.1.call-update) | async-done | bytes 3145744 | tf_op jit(solution)/shard_map/all_gather | solution.py:179
  155.4 5.7 %fusion.21 = bf16[3,128,512]{2,1,0:T(8,128)(2,1)} fusion(bf16[3,4096,128]{1,2,0:T(8,128)(2,1)} %all-gather.2.cloned.1.call-done, bf16[4096,512]{1,0:T(8,128)(2,1)} %param.19), kind=kOutput, calls=%fused_computation.27 | convolution fusion | flops 1610809344 | bytes 7733248 | tf_op jit(solution)/shard_map/ncm,co->nmo/dot_general | solution.py:180
  (49 shorter events, 13.0 us)
Async XLA Ops:
  6.5 2.5 %copy-start.6 = (bf16[384,512]{1,0:T(8,128)(2,1)S(1)}, bf16[384,512]{1,0:T(8,128)(2,1)}, u32[]{:S(2)}) copy-start(bf16[384,512]{1,0:T(8,128)(2,1)} %param.13) | copy-start | bytes 1179652
  6.5 148.8 %all-gather.2.cloned.1.call-start = ((), (), s32[]{:S(2)}) async-start(), calls=%async_computation | async-start | bytes 3538944 | tf_op jit(solution)/shard_map/all_gather | solution.py:179
  6.5 2.8 %copy-start.2 = (f32[384,512]{1,0:T(8,128)S(1)}, f32[384,512]{1,0:T(8,128)}, u32[]{:S(2)}) copy-start(f32[384,512]{1,0:T(8,128)} %param.17) | copy-start | bytes 2359300
  81.5 4.0 %copy-start.4 = (f32[384,96,1]{0,1,2:T(8,128)S(1)}, f32[384,96,1]{0,1,2:T(8,128)}, u32[]{:S(2)}) copy-start(f32[384,96,1]{0,1,2:T(8,128)} %constant.43) | copy-start | bytes 442372
  85.5 1.5 copy-start.3
  87.0 1.5 copy-start.5
  87.0 1.5 copy-start.9
  89.8 1.0 copy-start.1
  98.9 1.0 copy-start.7
  99.8 3.0 %copy-start.10 = (f32[192,128]{1,0:T(8,128)S(1)}, f32[192,128]{1,0:T(8,128)}, u32[]{:S(2)}) copy-start(f32[192,128]{1,0:T(8,128)} %constant.41) | copy-start | bytes 294916
  102.9 1.1 copy-start
  102.9 1.1 copy-start.8
Sparse Core Ops, SparseCore 0:
  123.0 32.3 all-gather.1

commit v4 on v3

--- a/solution.py
+++ b/solution.py
@@ -161,17 +161,17 @@
     def by_target(block):
         return to_ncm(block).reshape(half, seq_count, width, LANES).transpose(1, 0, 2, 3)
 
-    stacked = jnp.stack([by_target(out_gate), by_target(in_gate), by_target(values)], axis=1)
-    spread, filt = exchange([stacked, by_target(long_filter)], seq_count, 0)
-    spread = spread.transpose(1, 0, 2, 3, 4).reshape(3, seq_count * half, width, LANES)
-    filt = filt.reshape(seq_count * half, width, LANES)
+    planes = [out_gate, in_gate, values, long_filter.astype(jnp.bfloat16)]
+    stacked = jnp.stack([by_target(plane) for plane in planes], axis=1)
+    (spread,) = exchange([stacked], seq_count, 0)
+    spread = spread.transpose(1, 0, 2, 3, 4).reshape(len(planes), seq_count * half, width, LANES)
     start = seq_index * width
     taps = lax.dynamic_slice_in_dim(short_filter, start, width, axis=2)
     gain = lax.dynamic_slice_in_dim(skip_gain, start, width, axis=0)
     spread = spread.astype(jnp.float32)
     gate_late = short_conv(spread[0], taps[0])
     mixed_in = short_conv(spread[1], taps[1]) * short_conv(spread[2], taps[2])
-    long_out = long_conv(mixed_in, filt)
+    long_out = long_conv(mixed_in, spread[3])
     filtered = long_out + gain[None, :, None] * mixed_in
     mixed = (gate_late * filtered).astype(jnp.bfloat16)
     (mixed,) = exchange([mixed.reshape(seq_count, half, width, LANES)], seq_count, 1)

time: 168 us -> 159 us (0.946)
  Pallas kernels: 69 us -> 59.7 us
  local copies, waits for them, and re-layouts: 23.2 us -> 21.4 us
  other arithmetic: 9.45 us -> 11.2 us
    pallas_call x2, Pallas kernels: 69 us -> 59.7 us  [exchange(): pl.pallas_call(functools.partial(exchange_kernel, group, count), out_shap...]
    transpose x4, local copies, waits for them, and re-layouts: 3 us -> 0.88 us  [to_ncm(): return block.reshape(rows // LANES, LANES, width).transpose(0, 2, 1)]
where the time goes in v4:
time: 159 us
  Pallas kernels  59.7 us (38%)
  waiting for transfers between devices  33.4 us (21%)
  local copies, waits for them, and re-layouts  21.4 us (13%)
  matrix products  19.3 us (12%)
  between operations  13.7 us (9%)
  other arithmetic  11.2 us (7%)
    pallas_call x2, Pallas kernels, exchange(): pl.pallas_call(functools.partial(exchange_kernel, group, count), out_shap...  59.7 us
    all_gather x1, waiting for transfers between devices, on_device(): gathered = lax.all_gather(mixed, 'ch', axis=1, tiled=True)  33.4 us
    dot_general x6, matrix products, contract(): jnp.einsum(pattern, first_op, second_op, precision=high, preferred_elemen...  13.6 us
    unnamed x31, local copies, waits for them, and re-layouts  7.98 us
    slice x6, local copies, waits for them, and re-layouts, shift_seq(): prev[:, :, lanes - distance:]  6.05 us
    dot_general x1, matrix products, on_device(): jnp.einsum('ncm,co->nmo', gathered, out_weight, preferred_element_type=jn...  5.68 us
    mul x1, other arithmetic, on_device(): mixed_in = short_conv(spread[1], taps[1]) * short_conv(spread[2], taps[2])  4 us
  transfers between devices with their start and end apart: 1, of which 1 were waited for; matrix products, arithmetic and copies ran while one was open for 0% of the time, Pallas kernels for 0%

profile of v4, /device:TPU:1, one launch (start us, length us, event | category | flops | bytes accessed | tf_op | source)
XLA Modules:
  0.0 158.7 jit_solution(7121929995035317084)
XLA Ops:
  6.5 1.3 convert_element_type.18
  9.0 1.3 pad_maximum_fusion.3.refs_0_
  10.4 46.1 %shard_map.127 = bf16[32,4,3,16,128]{4,3,2,1,0:T(8,128)(2,1)} custom-call(bf16[32,4,3,16,128]{4,3,2,1,0:T(8,128)(2,1)} %pad_maximum_fusion.3.refs_0_), custom_call_target="tpu_custom_call" | custom-call | tf_op jit(solution)/shard_map/pallas_call | solution.py:64
  56.5 1.8 %bitcast_convert_fusion = f32[4,32,3,16,128]{4,3,2,0,1:T(8,128)S(1)} fusion(bf16[32,4,3,16,128]{4,3,2,1,0:T(8,128)(2,1)} %shard_map.127), kind=kLoop, calls=%fused_computation.71 | loop fusion | flops 786432 | bytes 4718592 | tf_op jit(solution)/shard_map/convert_element_type | solution.py:171
  59.3 1.2 pad_slice_fusion
  60.4 1.2 pad_slice_fusion.1
  61.9 1.2 pad_slice_fusion.2
  63.0 1.2 pad_slice_fusion.3
  64.7 1.1 pad_slice_fusion.5
  65.8 1.1 copy.106
  67.0 1.2 copy.107
  68.1 1.1 copy.108
  69.3 1.2 copy.109
  72.4 4.0 %fusion.28 = f32[96,16,128]{2,0,1:T(8,128)S(1)} fusion(f32[96,16,127]{2,0,1:T(8,128)} %copy.106, f32[96,16,1]{2,0,1:T(8,128)} %pad_slice_fusion.3, f32[96,16,126]{2,0,1:T(8,128)} %copy.107, f32[96,16,2]{2,0,1:T(8,128)} %pad_slice_fusion.2, f32[96,16,127]{2,0,1:T(8,128)} %copy.108, f32[96,16,1]{2,0,1:T(8,128)} %pad_slice_fusion.1, f32[96,16,126]{2,0,1:T(8,128)} %copy.109, ...), kind=kLoop, calls=%fused_computation.35 | loop fusion | flops 2949120 | bytes 5505408 | tf_op jit(solution)/shard_map/mul | solution.py:173
  76.4 1.5 fusion.41
  77.9 1.0 fusion.31
  79.0 1.3 multiply_subtract_fusion.3
  81.2 3.2 %fusion.10 = f32[192,16,256]{2,1,0:T(8,128)S(1)} fusion(f32[256,256,1]{1,0,2:T(8,128)S(1)} %copy-done.1, f32[192,16,256]{2,0,1:T(8,128)S(1)} %pad_maximum_fusion), kind=kOutput, calls=%fused_computation.13 | convolution fusion | flops 1207959552 | bytes 6553600 | tf_op jit(solution)/shard_map/kcm,mj->kcj/dot_general | solution.py:79
  84.6 3.0 %fusion.8 = f32[192,16,256]{2,1,0:T(8,128)S(1)} fusion(f32[256,256,1]{1,0,2:T(8,128)S(1)} %copy-done.1, f32[192,16,256]{2,0,1:T(8,128)S(1)} %pad_maximum_fusion.1), kind=kOutput, calls=%fused_computation.11 | convolution fusion | flops 1207959552 | bytes 6553600 | tf_op jit(solution)/shard_map/kcm,mj->kcj/dot_general | solution.py:79
  90.3 3.0 %fusion.6 = f32[192,16,256]{2,0,1:T(8,128)S(1)} fusion(f32[256,256,1]{1,0,2:T(8,128)S(1)} %copy-done.7, f32[192,16,256]{2,1,0:T(8,128)S(1)} %pad_maximum_fusion.2), kind=kOutput, calls=%fused_computation.9 | convolution fusion | flops 1207959552 | bytes 6553600 | tf_op jit(solution)/shard_map/kcj,jm->kcm/dot_general | solution.py:79
  94.5 2.0 %fusion.18 = bf16[96,16,128]{2,0,1:T(8,128)(2,1)S(1)} fusion(f32[96,384,1]{1,0,2:T(8,128)S(1)} %copy-done.8, f32[192,16,128]{2,0,1:T(8,128)S(1)} %get-tuple-element.8, f32[192,16,128]{2,0,1:T(8,128)S(1)} %get-tuple-element.7, f32[96,16,127]{2,0,1:T(8,128)S(1)} %copy.110, f32[96,16,1]{2,0,1:T(8,128)S(1)} %copy-done, f32[96,16,126]{2,0,1:T(8,128)S(1)} %copy.111, ...), kind=kOutput, calls=%fused_computation.26 | convolution fusion | flops 455933952 | bytes 6832384 | tf_op jit(solution)/shard_map/nk,kcm->ncm/dot_general | solution.py:79
  97.4 13.5 %shard_map.128 = bf16[32,3,16,128]{3,2,1,0:T(8,128)(2,1)} custom-call(bf16[32,3,16,128]{3,2,1,0:T(8,128)(2,1)} %bitcast.111), custom_call_target="tpu_custom_call" | custom-call | tf_op jit(solution)/shard_map/pallas_call | solution.py:64
  112.8 33.4 %all-gather.2.cloned.1.call-done = bf16[3,4096,128]{1,2,0:T(8,128)(2,1)} async-done(((bf16[3,512,128]{1,2,0:T(8,128)(2,1)}), bf16[3,4096,128]{1,2,0:T(8,128)(2,1)}) %all-gather.2.cloned.1.call-update) | async-done | bytes 3145744 | tf_op jit(solution)/shard_map/all_gather | solution.py:179
  146.2 5.7 %fusion.21 = bf16[3,128,512]{2,1,0:T(8,128)(2,1)} fusion(bf16[3,4096,128]{1,2,0:T(8,128)(2,1)} %all-gather.2.cloned.1.call-done, bf16[4096,512]{1,0:T(8,128)(2,1)} %param.19), kind=kOutput, calls=%fused_computation.27 | convolution fusion | flops 1610809344 | bytes 7733248 | tf_op jit(solution)/shard_map/ncm,co->nmo/dot_general | solution.py:180
  (50 shorter events, 12.6 us)
Async XLA Ops:
  6.5 1.5 copy-start.4
  6.5 1.7 %copy-start.5 = (bf16[384,512]{1,0:T(8,128)(2,1)S(1)}, bf16[384,512]{1,0:T(8,128)(2,1)}, u32[]{:S(2)}) copy-start(bf16[384,512]{1,0:T(8,128)(2,1)} %param.13) | copy-start | bytes 1179652
  6.5 139.7 %all-gather.2.cloned.1.call-start = ((), (), s32[]{:S(2)}) async-start(), calls=%async_computation | async-start | bytes 3538944 | tf_op jit(solution)/shard_map/all_gather | solution.py:179
  6.5 2.0 %copy-start.6 = (bf16[384,512]{1,0:T(8,128)(2,1)S(1)}, bf16[384,512]{1,0:T(8,128)(2,1)}, u32[]{:S(2)}) copy-start(bf16[384,512]{1,0:T(8,128)(2,1)} %param.14) | copy-start | bytes 1179652
  72.4 4.0 %copy-start.2 = (f32[384,96,1]{0,1,2:T(8,128)S(1)}, f32[384,96,1]{0,1,2:T(8,128)}, u32[]{:S(2)}) copy-start(f32[384,96,1]{0,1,2:T(8,128)} %constant.43) | copy-start | bytes 442372
  77.9 1.1 copy-start.3
  77.9 1.1 copy-start.9
  80.3 1.0 copy-start.1
  89.3 1.0 copy-start.7
  90.3 3.0 %copy-start.10 = (f32[192,128]{1,0:T(8,128)S(1)}, f32[192,128]{1,0:T(8,128)}, u32[]{:S(2)}) copy-start(f32[192,128]{1,0:T(8,128)} %constant.41) | copy-start | bytes 294916
  93.3 1.1 copy-start
  93.3 1.1 copy-start.8
Sparse Core Ops, SparseCore 0:
  113.0 33.1 all-gather.1

commit v5 on v4

--- a/solution.py
+++ b/solution.py
@@ -73,6 +73,117 @@
         ],
         compiler_params=pltpu.CompilerParams(collective_id=tag, has_side_effects=True),
     )(*arrays)
+
+
+def return_kernel(group, chans, source, target, send_sem, recv_sem, pass_sem, got_sem, fwd_sem, local_sem):
+    me = lax.axis_index("seq")
+    ch = lax.axis_index("ch")
+    sibling = ch + 1 - 2 * lax.rem(ch, 2)
+    across = [lax.rem(ch + 2 * hop, chans) for hop in range(1, chans // 2)]
+    barrier = pltpu.get_barrier_semaphore()
+    for step in range(1, group):
+        peer = lax.rem(me + step, group)
+        pl.semaphore_signal(barrier, inc=1, device_id=(peer, ch), device_id_type=MESH)
+    for peer_ch in across + [sibling]:
+        pl.semaphore_signal(barrier, inc=1, device_id=(me, peer_ch), device_id_type=MESH)
+    pl.semaphore_wait(barrier, group - 1 + len(across) + 1)
+    local = pltpu.make_async_copy(source.at[me], target.at[ch, me], local_sem.at[0])
+    local.start()
+    sent = []
+    for step in range(1, group):
+        peer = lax.rem(me + step, group)
+        cp = pltpu.make_async_remote_copy(
+            src_ref=source.at[peer],
+            dst_ref=target.at[ch, me],
+            send_sem=send_sem.at[step],
+            recv_sem=recv_sem.at[step],
+            device_id=(peer, ch),
+            device_id_type=MESH,
+        )
+        cp.start()
+        sent.append(cp)
+    local.wait()
+    for step in range(1, group):
+        origin = lax.rem(me + group - step, group)
+        pltpu.make_async_remote_copy(
+            src_ref=source.at[origin],
+            dst_ref=target.at[ch, origin],
+            send_sem=send_sem.at[step],
+            recv_sem=recv_sem.at[step],
+            device_id=(origin, ch),
+            device_id_type=MESH,
+        ).wait_recv()
+    passed = []
+    for slot, peer_ch in enumerate(across + [sibling]):
+        cp = pltpu.make_async_remote_copy(
+            src_ref=target.at[ch],
+            dst_ref=target.at[ch],
+            send_sem=pass_sem.at[slot],
+            recv_sem=got_sem.at[ch],
+            device_id=(me, peer_ch),
+            device_id_type=MESH,
+        )
+        cp.start()
+        passed.append(cp)
+    forwarded = []
+    for hop in range(1, chans // 2):
+        origin = lax.rem(ch + chans - 2 * hop, chans)
+        pltpu.make_async_remote_copy(
+            src_ref=target.at[origin],
+            dst_ref=target.at[origin],
+            send_sem=pass_sem.at[0],
+            recv_sem=got_sem.at[origin],
+            device_id=(me, origin),
+            device_id_type=MESH,
+        ).wait_recv()
+        cp = pltpu.make_async_remote_copy(
+            src_ref=target.at[origin],
+            dst_ref=target.at[origin],
+            send_sem=fwd_sem.at[hop],
+            recv_sem=got_sem.at[origin],
+            device_id=(me, sibling),
+            device_id_type=MESH,
+        )
+        cp.start()
+        forwarded.append(cp)
+    for cp in sent + passed + forwarded:
+        cp.wait_send()
+    for hop in range(1, chans // 2):
+        origin = lax.rem(sibling + chans - 2 * hop, chans)
+        pltpu.make_async_remote_copy(
+            src_ref=target.at[origin],
+            dst_ref=target.at[origin],
+            send_sem=pass_sem.at[0],
+            recv_sem=got_sem.at[origin],
+            device_id=(me, origin),
+            device_id_type=MESH,
+        ).wait_recv()
+    pltpu.make_async_remote_copy(
+        src_ref=target.at[sibling],
+        dst_ref=target.at[sibling],
+        send_sem=pass_sem.at[0],
+        recv_sem=got_sem.at[sibling],
+        device_id=(me, sibling),
+        device_id_type=MESH,
+    ).wait_recv()
+
+
+def return_and_gather(block, group, chans, tag):
+    return pl.pallas_call(
+        functools.partial(return_kernel, group, chans),
+        out_shape=jax.ShapeDtypeStruct((chans,) + block.shape, block.dtype),
+        in_specs=[pl.BlockSpec(memory_space=pl.ANY)],
+        out_specs=pl.BlockSpec(memory_space=pl.ANY),
+        scratch_shapes=[
+            pltpu.SemaphoreType.DMA((group,)),
+            pltpu.SemaphoreType.DMA((group,)),
+            pltpu.SemaphoreType.DMA((chans // 2,)),
+            pltpu.SemaphoreType.DMA((chans,)),
+            pltpu.SemaphoreType.DMA((chans // 2,)),
+            pltpu.SemaphoreType.DMA((1,)),
+        ],
+        compiler_params=pltpu.CompilerParams(collective_id=tag, has_side_effects=True),
+    )(block)
 
 
 def contract(pattern, first_op, second_op):
@@ -174,9 +285,9 @@
     long_out = long_conv(mixed_in, spread[3])
     filtered = long_out + gain[None, :, None] * mixed_in
     mixed = (gate_late * filtered).astype(jnp.bfloat16)
-    (mixed,) = exchange([mixed.reshape(seq_count, half, width, LANES)], seq_count, 1)
-    mixed = mixed.transpose(1, 0, 2, 3).reshape(half, seq_count * width, LANES)
-    gathered = lax.all_gather(mixed, "ch", axis=1, tiled=True)
+    chans = lax.axis_size("ch")
+    gathered = return_and_gather(mixed.reshape(seq_count, half, width, LANES), seq_count, chans, 1)
+    gathered = gathered.transpose(2, 0, 1, 3, 4).reshape(half, chans * seq_count * width, LANES)
     summed = jnp.einsum(
         "ncm,co->nmo", gathered, out_weight, preferred_element_type=jnp.float32
     )

time: 159 us -> 130 us (0.82)
  waiting for transfers between devices: 33.4 us -> 0 us
  Pallas kernels: 59.7 us -> 83.6 us
  between operations: 13.7 us -> 0.4 us
  local copies, waits for them, and re-layouts: 21.4 us -> 16.8 us
  other arithmetic: 11.2 us -> 8.75 us
    pallas_call x0 -> x1, Pallas kernels: none -> 37.5 us  [return_and_gather(): pl.pallas_call(functools.partial(return_kernel, group, chans), out_shape=...]
    all_gather x1 -> x0, waiting for transfers between devices: 33.4 us -> none  [on_device(): gathered = lax.all_gather(mixed, 'ch', axis=1, tiled=True)]
    pallas_call x2 -> x1, Pallas kernels: 59.7 us -> 46.1 us  [exchange(): pl.pallas_call(functools.partial(exchange_kernel, group, count), out_shap...]
    slice x6, local copies, waits for them, and re-layouts: 6.05 us -> 1.61 us  [shift_seq(): prev[:, :, lanes - distance:]]
    unnamed x31 -> x29, local copies, waits for them, and re-layouts: 7.98 us -> 4.16 us
    dot_general x0 -> x1, local copies, waits for them, and re-layouts: none -> 2.86 us  [on_device(): jnp.einsum('ncm,co->nmo', gathered, out_weight, preferred_element_type=jn...]
    mul x1, other arithmetic: 4 us -> 1.56 us  [on_device(): mixed_in = short_conv(spread[1], taps[1]) * short_conv(spread[2], taps[2])]
    transpose x1, local copies, waits for them, and re-layouts: 1.02 us -> 2.76 us  [on_device(): gathered.transpose(2, 0, 1, 3, 4)]
  transfers between devices with their start and end apart: 1 -> 0, of which waited for: 1 -> 0; matrix products, arithmetic and copies ran while one was open for 0% -> 0% of each run, Pallas kernels for 0% -> 0%
where the time goes in v5:
time: 130 us; the launch traced here: 129 us
  Pallas kernels  83.6 us (64%)
  matrix products  19.6 us (15%)
  local copies, waits for them, and re-layouts  16.8 us (13%)
  other arithmetic  8.75 us (7%)
    pallas_call x1, Pallas kernels, exchange(): pl.pallas_call(functools.partial(exchange_kernel, group, count), out_shap...  46.1 us
    pallas_call x1, Pallas kernels, return_and_gather(): pl.pallas_call(functools.partial(return_kernel, group, chans), out_shape=...  37.5 us
    dot_general x6, matrix products, contract(): jnp.einsum(pattern, first_op, second_op, precision=high, preferred_elemen...  13.9 us
    dot_general x1, matrix products, on_device(): jnp.einsum('ncm,co->nmo', gathered, out_weight, preferred_element_type=jn...  5.68 us
    unnamed x29, local copies, waits for them, and re-layouts  4.16 us
    dot_general x1, local copies, waits for them, and re-layouts, on_device(): jnp.einsum('ncm,co->nmo', gathered, out_weight, preferred_element_type=jn...  2.86 us
    transpose x1, local copies, waits for them, and re-layouts, on_device(): gathered.transpose(2, 0, 1, 3, 4)  2.76 us

profile of v5, /device:TPU:1, one launch (start us, length us, event | category | flops | bytes accessed | tf_op | source)
XLA Modules:
  0.0 129.2 jit_solution(6264311186746353718)
XLA Ops:
  0.0 0.9 fusion.29
  0.9 1.2 convert_element_type.15
  3.8 1.4 %pad_maximum_fusion.3.refs_0_ = bf16[32,4,3,16,128]{4,3,2,1,0:T(8,128)(2,1)} fusion(bf16[32,1,3,16,128]{4,3,2,1,0:T(8,128)(2,1)S(1)} %get-tuple-element.30, bf16[32,1,3,16,128]{4,3,2,1,0:T(8,128)(2,1)S(1)} %get-tuple-element.31, bf16[32,1,3,16,128]{4,3,2,1,0:T(8,128)(2,1)S(1)} %get-tuple-element.32, bf16[32,1,3,16,128]{4,3,2,1,0:T(8,128)(2,1)S(1)} %get-tuple-element.33), kind=kLoop, calls=%fused_computation.13 | loop fusion | flops 2359296 | bytes 3145728 | tf_op jit(solution)/shard_map/stack | solution.py:276
  5.1 46.1 %shard_map.127 = bf16[32,4,3,16,128]{4,3,2,1,0:T(8,128)(2,1)} custom-call(bf16[32,4,3,16,128]{4,3,2,1,0:T(8,128)(2,1)} %pad_maximum_fusion.3.refs_0_), custom_call_target="tpu_custom_call" | custom-call | tf_op jit(solution)/shard_map/pallas_call | solution.py:64
  51.3 1.8 %bitcast_convert_fusion = f32[4,32,3,16,128]{4,3,2,0,1:T(8,128)S(1)} fusion(bf16[32,4,3,16,128]{4,3,2,1,0:T(8,128)(2,1)} %shard_map.127), kind=kLoop, calls=%fused_computation.69 | loop fusion | flops 786432 | bytes 4718592 | tf_op jit(solution)/shard_map/convert_element_type | solution.py:282
  56.4 1.6 %fusion.23 = f32[96,16,128]{2,0,1:T(8,128)S(1)} fusion(f32[96,16,127]{2,0,1:T(8,128)S(1)} %copy.106, f32[96,16,1]{2,0,1:T(8,128)S(1)} %pad_slice_fusion.3, f32[96,16,126]{2,0,1:T(8,128)S(1)} %copy.107, f32[96,16,2]{2,0,1:T(8,128)S(1)} %pad_slice_fusion.2, f32[96,16,127]{2,0,1:T(8,128)S(1)} %copy.108, f32[96,16,1]{2,0,1:T(8,128)S(1)} %pad_slice_fusion.1, ...), kind=kLoop, calls=%fused_computation.33 | loop fusion | flops 2949120 | bytes 5505408 | tf_op jit(solution)/shard_map/mul | solution.py:284
  58.0 1.5 %fusion.36 = f32[384,16,128]{2,0,1:T(8,128)S(1)} fusion(f32[384,96,1]{0,1,2:T(8,128)S(1)} %copy-done.1, f32[96,16,128]{2,0,1:T(8,128)S(1)} %fusion.23), kind=kOutput, calls=%fused_computation.72 | convolution fusion | flops 452984832 | bytes 4079616 | tf_op jit(solution)/shard_map/kn,ncm->kcm/dot_general | solution.py:190
  59.5 1.0 slice.210
  60.5 1.0 fusion.26
  61.6 1.3 multiply_subtract_fusion.3
  63.1 0.7 copy-done
  63.8 3.2 %fusion.8 = f32[192,16,256]{2,1,0:T(8,128)S(1)} fusion(f32[256,256,1]{1,0,2:T(8,128)S(1)} %copy-done, f32[192,16,256]{2,0,1:T(8,128)S(1)} %pad_maximum_fusion), kind=kOutput, calls=%fused_computation.11 | convolution fusion | flops 1207959552 | bytes 6553600 | tf_op jit(solution)/shard_map/kcm,mj->kcj/dot_general | solution.py:190
  67.2 3.0 %fusion.6 = f32[192,16,256]{2,1,0:T(8,128)S(1)} fusion(f32[256,256,1]{1,0,2:T(8,128)S(1)} %copy-done, f32[192,16,256]{2,0,1:T(8,128)S(1)} %pad_maximum_fusion.1), kind=kOutput, calls=%fused_computation.9 | convolution fusion | flops 1207959552 | bytes 6553600 | tf_op jit(solution)/shard_map/kcm,mj->kcj/dot_general | solution.py:190
  70.2 0.4 multiply_subtract_fusion.1
  70.9 0.7 copy-done.6
  71.6 3.0 %fusion.4 = f32[192,16,256]{2,0,1:T(8,128)S(1)} fusion(f32[256,256,1]{1,0,2:T(8,128)S(1)} %copy-done.6, f32[192,16,256]{2,1,0:T(8,128)S(1)} %pad_maximum_fusion.2), kind=kOutput, calls=%fused_computation.7 | convolution fusion | flops 1207959552 | bytes 6553600 | tf_op jit(solution)/shard_map/kcj,jm->kcm/dot_general | solution.py:190
  74.7 0.4 multiply_subtract_fusion
  76.5 0.8 dynamic_slice.7
  77.2 2.3 %fusion.16 = bf16[96,16,128]{2,0,1:T(8,128)(2,1)S(1)} fusion(f32[96,384,1]{1,0,2:T(8,128)S(1)} %copy-done.7, f32[192,16,128]{2,0,1:T(8,128)S(1)} %get-tuple-element.8, f32[192,16,128]{2,0,1:T(8,128)S(1)} %get-tuple-element.7, f32[96,16,127]{2,0,1:T(8,128)S(1)} %copy.110, f32[96,16,1]{2,0,1:T(8,128)S(1)} %pad_slice_fusion.5, f32[96,16,126]{2,0,1:T(8,128)S(1)} %copy.111, ...), kind=kOutput, calls=%fused_computation.24 | convolution fusion | flops 455933952 | bytes 6832384 | tf_op jit(solution)/shard_map/nk,kcm->ncm/dot_general | solution.py:190
  79.5 0.9 copy.80
  80.4 37.5 %shard_map.128 = bf16[8,32,3,16,128]{4,3,2,1,0:T(8,128)(2,1)} custom-call(bf16[32,3,16,128]{3,2,1,0:T(8,128)(2,1)} %bitcast.112), custom_call_target="tpu_custom_call" | custom-call | tf_op jit(solution)/shard_map/pallas_call | solution.py:172
  117.9 2.8 %copy.81 = bf16[3,8,32,16,128]{4,3,2,1,0:T(8,128)(2,1)S(1)} copy(bf16[3,8,32,16,128]{4,3,0,2,1:T(8,128)(2,1)} %bitcast.100) | data formatting | bytes 6291456 | tf_op jit(solution)/shard_map/transpose | solution.py:290
  120.7 2.9 %copy.82 = bf16[3,128,4096]{2,1,0:T(8,128)(2,1)} copy(bf16[3,128,4096]{1,2,0:T(8,128)(2,1)S(1)} %bitcast.101) | data formatting | bytes 6291456 | tf_op jit(solution)/shard_map/ncm,co->nmo/dot_general | solution.py:291
  123.5 5.7 %convolution_convert_fusion = bf16[384,512]{1,0:T(8,128)(2,1)} fusion(bf16[384,4096]{1,0:T(8,128)(2,1)} %bitcast.110, bf16[4096,512]{1,0:T(8,128)(2,1)} %param.19), kind=kOutput, calls=%fused_computation.25 | convolution fusion | flops 1610809344 | bytes 7733248 | tf_op jit(solution)/shard_map/ncm,co->nmo/dot_general | solution.py:291
  (45 shorter events, 6.9 us)
Async XLA Ops:
  0.0 2.4 %copy-start.3 = (bf16[384,512]{1,0:T(8,128)(2,1)S(1)}, bf16[384,512]{1,0:T(8,128)(2,1)}, u32[]{:S(2)}) copy-start(bf16[384,512]{1,0:T(8,128)(2,1)} %param.15) | copy-start | bytes 1179652
  2.1 1.0 copy-start.4
  2.4 1.0 copy-start.5
  56.4 1.6 %copy-start.1 = (f32[384,96,1]{0,1,2:T(8,128)S(1)}, f32[384,96,1]{0,1,2:T(8,128)}, u32[]{:S(2)}) copy-start(f32[384,96,1]{0,1,2:T(8,128)} %constant.43) | copy-start | bytes 442372
  60.5 1.1 copy-start.2
  60.5 1.1 copy-start.8
  62.9 1.0 copy-start
  70.6 1.0 copy-start.6
  71.6 3.0 %copy-start.9 = (f32[192,128]{1,0:T(8,128)S(1)}, f32[192,128]{1,0:T(8,128)}, u32[]{:S(2)}) copy-start(f32[192,128]{1,0:T(8,128)} %constant.41) | copy-start | bytes 294916
  75.9 1.3 %copy-start.7 = (f32[96,384,1]{1,0,2:T(8,128)S(1)}, f32[96,384,1]{1,0,2:T(8,128)}, u32[]{:S(2)}) copy-start(f32[96,384,1]{1,0,2:T(8,128)} %constant.42) | copy-start | bytes 442372

commit v6 on v5

--- a/solution.py
+++ b/solution.py
@@ -87,14 +87,14 @@
     for peer_ch in across + [sibling]:
         pl.semaphore_signal(barrier, inc=1, device_id=(me, peer_ch), device_id_type=MESH)
     pl.semaphore_wait(barrier, group - 1 + len(across) + 1)
-    local = pltpu.make_async_copy(source.at[me], target.at[ch, me], local_sem.at[0])
+    local = pltpu.make_async_copy(source.at[me], target.at[:, ch, me], local_sem.at[0])
     local.start()
     sent = []
     for step in range(1, group):
         peer = lax.rem(me + step, group)
         cp = pltpu.make_async_remote_copy(
             src_ref=source.at[peer],
-            dst_ref=target.at[ch, me],
+            dst_ref=target.at[:, ch, me],
             send_sem=send_sem.at[step],
             recv_sem=recv_sem.at[step],
             device_id=(peer, ch),
@@ -107,7 +107,7 @@
         origin = lax.rem(me + group - step, group)
         pltpu.make_async_remote_copy(
             src_ref=source.at[origin],
-            dst_ref=target.at[ch, origin],
+            dst_ref=target.at[:, ch, origin],
             send_sem=send_sem.at[step],
             recv_sem=recv_sem.at[step],
             device_id=(origin, ch),
@@ -116,8 +116,8 @@
     passed = []
     for slot, peer_ch in enumerate(across + [sibling]):
         cp = pltpu.make_async_remote_copy(
-            src_ref=target.at[ch],
-            dst_ref=target.at[ch],
+            src_ref=target.at[:, ch],
+            dst_ref=target.at[:, ch],
             send_sem=pass_sem.at[slot],
             recv_sem=got_sem.at[ch],
             device_id=(me, peer_ch),
@@ -129,16 +129,16 @@
     for hop in range(1, chans // 2):
         origin = lax.rem(ch + chans - 2 * hop, chans)
         pltpu.make_async_remote_copy(
-            src_ref=target.at[origin],
-            dst_ref=target.at[origin],
+            src_ref=target.at[:, origin],
+            dst_ref=target.at[:, origin],
             send_sem=pass_sem.at[0],
             recv_sem=got_sem.at[origin],
             device_id=(me, origin),
             device_id_type=MESH,
         ).wait_recv()
         cp = pltpu.make_async_remote_copy(
-            src_ref=target.at[origin],
-            dst_ref=target.at[origin],
+            src_ref=target.at[:, origin],
+            dst_ref=target.at[:, origin],
             send_sem=fwd_sem.at[hop],
             recv_sem=got_sem.at[origin],
             device_id=(me, sibling),
@@ -151,16 +151,16 @@
     for hop in range(1, chans // 2):
         origin = lax.rem(sibling + chans - 2 * hop, chans)
         pltpu.make_async_remote_copy(
-            src_ref=target.at[origin],
-            dst_ref=target.at[origin],
+            src_ref=target.at[:, origin],
+            dst_ref=target.at[:, origin],
             send_sem=pass_sem.at[0],
             recv_sem=got_sem.at[origin],
             device_id=(me, origin),
             device_id_type=MESH,
         ).wait_recv()
     pltpu.make_async_remote_copy(
-        src_ref=target.at[sibling],
-        dst_ref=target.at[sibling],
+        src_ref=target.at[:, sibling],
+        dst_ref=target.at[:, sibling],
         send_sem=pass_sem.at[0],
         recv_sem=got_sem.at[sibling],
         device_id=(me, sibling),
@@ -171,7 +171,9 @@
 def return_and_gather(block, group, chans, tag):
     return pl.pallas_call(
         functools.partial(return_kernel, group, chans),
-        out_shape=jax.ShapeDtypeStruct((chans,) + block.shape, block.dtype),
+        out_shape=jax.ShapeDtypeStruct(
+            (block.shape[1], chans, block.shape[0]) + block.shape[2:], block.dtype
+        ),
         in_specs=[pl.BlockSpec(memory_space=pl.ANY)],
         out_specs=pl.BlockSpec(memory_space=pl.ANY),
         scratch_shapes=[
@@ -287,7 +289,7 @@
     mixed = (gate_late * filtered).astype(jnp.bfloat16)
     chans = lax.axis_size("ch")
     gathered = return_and_gather(mixed.reshape(seq_count, half, width, LANES), seq_count, chans, 1)
-    gathered = gathered.transpose(2, 0, 1, 3, 4).reshape(half, chans * seq_count * width, LANES)
+    gathered = gathered.reshape(half, chans * seq_count * width, LANES)
     summed = jnp.einsum(
         "ncm,co->nmo", gathered, out_weight, preferred_element_type=jnp.float32
     )

time: 130 us -> 126 us (0.969)
  local copies, waits for them, and re-layouts: 16.8 us -> 14.4 us
  matrix products: 19.6 us -> 18.3 us
    reshape x0 -> x1, local copies, waits for them, and re-layouts: none -> 3.2 us  [on_device(): gathered = gathered.reshape(half, chans * seq_count * width, LANES)]
    dot_general x1 -> x0, local copies, waits for them, and re-layouts: 2.86 us -> none  [on_device(): jnp.einsum('ncm,co->nmo', gathered, out_weight, preferred_element_type=jn...]
    transpose x1 -> x0, local copies, waits for them, and re-layouts: 2.76 us -> none  [on_device(): gathered.transpose(2, 0, 1, 3, 4)]
where the time goes in v6:
time: 126 us
  Pallas kernels  83.6 us (66%)
  matrix products  18.3 us (15%)
  local copies, waits for them, and re-layouts  14.4 us (11%)
  other arithmetic  9.08 us (7%)
    pallas_call x1, Pallas kernels, exchange(): pl.pallas_call(functools.partial(exchange_kernel, group, count), out_shap...  46.1 us
    pallas_call x1, Pallas kernels, return_and_gather(): pl.pallas_call(functools.partial(return_kernel, group, chans), out_shape=...  37.5 us
    dot_general x6, matrix products, contract(): jnp.einsum(pattern, first_op, second_op, precision=high, preferred_elemen...  13.6 us
    dot_general x1, matrix products, on_device(): jnp.einsum('ncm,co->nmo', gathered, out_weight, preferred_element_type=jn...  4.78 us
    unnamed x29, local copies, waits for them, and re-layouts  4.16 us
    reshape x1, local copies, waits for them, and re-layouts, on_device(): gathered = gathered.reshape(half, chans * seq_count * width, LANES)  3.2 us

profile of v6, /device:TPU:1, one launch (start us, length us, event | category | flops | bytes accessed | tf_op | source)
XLA Modules:
  0.0 125.8 jit_solution(17603284648541581434)
XLA Ops:
  0.0 0.9 fusion.29
  0.9 1.2 convert_element_type.15
  2.7 0.4 copy-done.4
  3.8 1.4 %pad_maximum_fusion.3.refs_0_ = bf16[32,4,3,16,128]{4,3,2,1,0:T(8,128)(2,1)} fusion(bf16[32,1,3,16,128]{4,3,2,1,0:T(8,128)(2,1)S(1)} %get-tuple-element.30, bf16[32,1,3,16,128]{4,3,2,1,0:T(8,128)(2,1)S(1)} %get-tuple-element.31, bf16[32,1,3,16,128]{4,3,2,1,0:T(8,128)(2,1)S(1)} %get-tuple-element.32, bf16[32,1,3,16,128]{4,3,2,1,0:T(8,128)(2,1)S(1)} %get-tuple-element.33), kind=kLoop, calls=%fused_computation.13 | loop fusion | flops 2359296 | bytes 3145728 | tf_op jit(solution)/shard_map/stack | solution.py:278
  5.1 46.1 %shard_map.127 = bf16[32,4,3,16,128]{4,3,2,1,0:T(8,128)(2,1)} custom-call(bf16[32,4,3,16,128]{4,3,2,1,0:T(8,128)(2,1)} %pad_maximum_fusion.3.refs_0_), custom_call_target="tpu_custom_call" | custom-call | tf_op jit(solution)/shard_map/pallas_call | solution.py:64
  51.3 1.8 %bitcast_convert_fusion = f32[4,32,3,16,128]{4,3,2,0,1:T(8,128)S(1)} fusion(bf16[32,4,3,16,128]{4,3,2,1,0:T(8,128)(2,1)} %shard_map.127), kind=kLoop, calls=%fused_computation.69 | loop fusion | flops 786432 | bytes 4718592 | tf_op jit(solution)/shard_map/convert_element_type | solution.py:284
  56.4 1.9 %fusion.23 = f32[96,16,128]{2,0,1:T(8,128)S(1)} fusion(f32[96,16,127]{2,0,1:T(8,128)S(1)} %copy.104, f32[96,16,1]{2,0,1:T(8,128)S(1)} %pad_slice_fusion.3, f32[96,16,126]{2,0,1:T(8,128)S(1)} %copy.105, f32[96,16,2]{2,0,1:T(8,128)S(1)} %pad_slice_fusion.2, f32[96,16,127]{2,0,1:T(8,128)S(1)} %copy.106, f32[96,16,1]{2,0,1:T(8,128)S(1)} %pad_slice_fusion.1, ...), kind=kLoop, calls=%fused_computation.33 | loop fusion | flops 2949120 | bytes 5505408 | tf_op jit(solution)/shard_map/mul | solution.py:286
  58.3 1.5 %fusion.36 = f32[384,16,128]{2,0,1:T(8,128)S(1)} fusion(f32[384,96,1]{0,1,2:T(8,128)S(1)} %copy-done.1, f32[96,16,128]{2,0,1:T(8,128)S(1)} %fusion.23), kind=kOutput, calls=%fused_computation.72 | convolution fusion | flops 452984832 | bytes 4079616 | tf_op jit(solution)/shard_map/kn,ncm->kcm/dot_general | solution.py:192
  59.8 1.0 slice.210
  60.8 1.0 fusion.26
  61.9 1.3 %multiply_subtract_fusion.3 = (f32[192,16,128]{2,0,1:T(8,128)S(1)}, f32[192,16,128]{2,0,1:T(8,128)S(1)}, f32[192,16,128]{2,0,1:T(8,128)S(1)}, f32[192,16,128]{2,0,1:T(8,128)S(1)}) fusion(f32[384,16,128]{2,0,1:T(8,128)S(1)} %fusion.36, f32[192,128]{1,0:T(8,128)S(1)} %copy-done.8, f32[192,128]{1,0:T(8,128)S(1)} %copy-done.2, f32[384,16,128]{2,0,1:T(8,128)S(1)} %fusion.26), kind=kLoop, calls=%fused_computation.21 | loop fusion | flops 4718592 | bytes 12779520 | tf_op jit(solution)/shard_map/sub | solution.py:224
  63.4 0.7 copy-done
  64.1 3.2 %fusion.8 = f32[192,16,256]{2,1,0:T(8,128)S(1)} fusion(f32[256,256,1]{1,0,2:T(8,128)S(1)} %copy-done, f32[192,16,256]{2,0,1:T(8,128)S(1)} %pad_maximum_fusion), kind=kOutput, calls=%fused_computation.11 | convolution fusion | flops 1207959552 | bytes 6553600 | tf_op jit(solution)/shard_map/kcm,mj->kcj/dot_general | solution.py:192
  67.6 3.0 %fusion.6 = f32[192,16,256]{2,1,0:T(8,128)S(1)} fusion(f32[256,256,1]{1,0,2:T(8,128)S(1)} %copy-done, f32[192,16,256]{2,0,1:T(8,128)S(1)} %pad_maximum_fusion.1), kind=kOutput, calls=%fused_computation.9 | convolution fusion | flops 1207959552 | bytes 6553600 | tf_op jit(solution)/shard_map/kcm,mj->kcj/dot_general | solution.py:192
  70.6 0.4 multiply_subtract_fusion.1
  71.3 0.7 copy-done.6
  72.0 3.0 %fusion.4 = f32[192,16,256]{2,0,1:T(8,128)S(1)} fusion(f32[256,256,1]{1,0,2:T(8,128)S(1)} %copy-done.6, f32[192,16,256]{2,1,0:T(8,128)S(1)} %pad_maximum_fusion.2), kind=kOutput, calls=%fused_computation.7 | convolution fusion | flops 1207959552 | bytes 6553600 | tf_op jit(solution)/shard_map/kcj,jm->kcm/dot_general | solution.py:192
  75.0 0.5 multiply_subtract_fusion
  76.8 0.8 dynamic_slice.7
  77.5 1.9 %fusion.16 = bf16[96,16,128]{2,0,1:T(8,128)(2,1)S(1)} fusion(f32[96,384,1]{1,0,2:T(8,128)S(1)} %copy-done.7, f32[192,16,128]{2,0,1:T(8,128)S(1)} %get-tuple-element.8, f32[192,16,128]{2,0,1:T(8,128)S(1)} %get-tuple-element.7, f32[96,16,127]{2,0,1:T(8,128)S(1)} %copy.108, f32[96,16,1]{2,0,1:T(8,128)S(1)} %pad_slice_fusion.5, f32[96,16,126]{2,0,1:T(8,128)S(1)} %copy.109, ...), kind=kOutput, calls=%fused_computation.24 | convolution fusion | flops 455933952 | bytes 6832384 | tf_op jit(solution)/shard_map/nk,kcm->ncm/dot_general | solution.py:192
  79.4 0.9 copy.79
  80.3 37.5 %shard_map.128 = bf16[3,8,32,16,128]{4,3,2,1,0:T(8,128)(2,1)} custom-call(bf16[32,3,16,128]{3,2,1,0:T(8,128)(2,1)} %bitcast.110), custom_call_target="tpu_custom_call" | custom-call | tf_op jit(solution)/shard_map/pallas_call | solution.py:172
  117.8 3.2 %copy.80 = bf16[3,4096,128]{1,2,0:T(8,128)(2,1)S(1)} copy(bf16[3,4096,128]{2,1,0:T(8,128)(2,1)} %bitcast.99) | data formatting | bytes 6291456 | tf_op jit(solution)/shard_map/reshape | solution.py:292
  121.0 4.8 %convolution_convert_fusion = bf16[384,512]{1,0:T(8,128)(2,1)} fusion(bf16[384,4096]{1,0:T(8,128)(2,1)S(1)} %bitcast.108, bf16[4096,512]{1,0:T(8,128)(2,1)} %param.19), kind=kOutput, calls=%fused_computation.25 | convolution fusion | flops 1610809344 | bytes 7733248 | tf_op jit(solution)/shard_map/ncm,co->nmo/dot_general | solution.py:293
  (44 shorter events, 6.5 us)
Async XLA Ops:
  0.0 2.4 %copy-start.3 = (bf16[384,512]{1,0:T(8,128)(2,1)S(1)}, bf16[384,512]{1,0:T(8,128)(2,1)}, u32[]{:S(2)}) copy-start(bf16[384,512]{1,0:T(8,128)(2,1)} %param.15) | copy-start | bytes 1179652
  2.1 1.0 copy-start.4
  2.4 1.0 copy-start.5
  56.4 1.9 %copy-start.1 = (f32[384,96,1]{0,1,2:T(8,128)S(1)}, f32[384,96,1]{0,1,2:T(8,128)}, u32[]{:S(2)}) copy-start(f32[384,96,1]{0,1,2:T(8,128)} %constant.43) | copy-start | bytes 442372
  60.8 1.1 copy-start.2
  60.8 1.1 copy-start.8
  63.2 1.0 copy-start
  71.0 1.0 copy-start.6
  72.0 3.0 %copy-start.9 = (f32[192,128]{1,0:T(8,128)S(1)}, f32[192,128]{1,0:T(8,128)}, u32[]{:S(2)}) copy-start(f32[192,128]{1,0:T(8,128)} %constant.41) | copy-start | bytes 294916
  76.2 1.3 %copy-start.7 = (f32[96,384,1]{1,0,2:T(8,128)S(1)}, f32[96,384,1]{1,0,2:T(8,128)}, u32[]{:S(2)}) copy-start(f32[96,384,1]{1,0,2:T(8,128)} %constant.42) | copy-start | bytes 442372

commit v7 on v4

--- a/solution.py
+++ b/solution.py
@@ -75,6 +75,119 @@
     )(*arrays)
 
 
+def return_kernel(group, chans, source, target, send_sem, recv_sem, pass_sem, got_sem, fwd_sem, local_sem):
+    me = lax.axis_index("seq")
+    ch = lax.axis_index("ch")
+    half = source.shape[1]
+    sibling = ch + 1 - 2 * lax.rem(ch, 2)
+    across = [lax.rem(ch + 2 * hop, chans) for hop in range(1, chans // 2)]
+    barrier = pltpu.get_barrier_semaphore()
+    for step in range(1, group):
+        peer = lax.rem(me + step, group)
+        pl.semaphore_signal(barrier, inc=1, device_id=(peer, ch), device_id_type=MESH)
+    for peer_ch in across + [sibling]:
+        pl.semaphore_signal(barrier, inc=1, device_id=(me, peer_ch), device_id_type=MESH)
+    pl.semaphore_wait(barrier, group - 1 + len(across) + 1)
+
+    def incoming(part, slot, peer_ch):
+        return pltpu.make_async_remote_copy(
+            src_ref=target.at[part, slot],
+            dst_ref=target.at[part, slot],
+            send_sem=pass_sem.at[part, 0],
+            recv_sem=got_sem.at[part, slot],
+            device_id=(me, peer_ch),
+            device_id_type=MESH,
+        )
+
+    sent = []
+    locals_ = []
+    for part in range(half):
+        cp = pltpu.make_async_copy(
+            source.at[me, part], target.at[part, ch, me], local_sem.at[part]
+        )
+        cp.start()
+        locals_.append(cp)
+        for step in range(1, group):
+            peer = lax.rem(me + step, group)
+            cp = pltpu.make_async_remote_copy(
+                src_ref=source.at[peer, part],
+                dst_ref=target.at[part, ch, me],
+                send_sem=send_sem.at[part, step],
+                recv_sem=recv_sem.at[part, step],
+                device_id=(peer, ch),
+                device_id_type=MESH,
+            )
+            cp.start()
+            sent.append(cp)
+    passed = []
+    for part in range(half):
+        locals_[part].wait()
+        for step in range(1, group):
+            origin = lax.rem(me + group - step, group)
+            pltpu.make_async_remote_copy(
+                src_ref=source.at[origin, part],
+                dst_ref=target.at[part, ch, origin],
+                send_sem=send_sem.at[part, step],
+                recv_sem=recv_sem.at[part, step],
+                device_id=(origin, ch),
+                device_id_type=MESH,
+            ).wait_recv()
+        for slot, peer_ch in enumerate(across + [sibling]):
+            cp = pltpu.make_async_remote_copy(
+                src_ref=target.at[part, ch],
+                dst_ref=target.at[part, ch],
+                send_sem=pass_sem.at[part, slot],
+                recv_sem=got_sem.at[part, ch],
+                device_id=(me, peer_ch),
+                device_id_type=MESH,
+            )
+            cp.start()
+            passed.append(cp)
+    forwarded = []
+    for part in range(half):
+        for hop in range(1, chans // 2):
+            origin = lax.rem(ch + chans - 2 * hop, chans)
+            incoming(part, origin, origin).wait_recv()
+            cp = pltpu.make_async_remote_copy(
+                src_ref=target.at[part, origin],
+                dst_ref=target.at[part, origin],
+                send_sem=fwd_sem.at[part, hop],
+                recv_sem=got_sem.at[part, origin],
+                device_id=(me, sibling),
+                device_id_type=MESH,
+            )
+            cp.start()
+            forwarded.append(cp)
+    for cp in sent + passed + forwarded:
+        cp.wait_send()
+    for part in range(half):
+        for hop in range(1, chans // 2):
+            origin = lax.rem(sibling + chans - 2 * hop, chans)
+            incoming(part, origin, origin).wait_recv()
+        incoming(part, sibling, sibling).wait_recv()
+
+
+def return_and_gather(block, group, chans, tag):
+    half = block.shape[1]
+    return pl.pallas_call(
+        functools.partial(return_kernel, group, chans),
+        out_shape=jax.ShapeDtypeStruct(
+            (half, chans, block.shape[0]) + block.shape[2:], block.dtype
+        ),
+        in_specs=[pl.BlockSpec(memory_space=pl.ANY)],
+        out_specs=pl.BlockSpec(memory_space=pl.ANY),
+        scratch_shapes=[
+            pltpu.SemaphoreType.DMA((half, group)),
+            pltpu.SemaphoreType.DMA((half, group)),
+            pltpu.SemaphoreType.DMA((half, chans // 2)),
+            pltpu.SemaphoreType.DMA((half, chans)),
+            pltpu.SemaphoreType.DMA((half, chans // 2)),
+            pltpu.SemaphoreType.DMA((half,)),
+        ],
+        compiler_params=pltpu.CompilerParams(collective_id=tag, has_side_effects=True),
+    )(block)
+
+
 def contract(pattern, first_op, second_op):
     return jnp.einsum(
         pattern, first_op, second_op, precision=high, preferred_element_type=jnp.float32
@@ -174,9 +287,9 @@
     long_out = long_conv(mixed_in, spread[3])
     filtered = long_out + gain[None, :, None] * mixed_in
     mixed = (gate_late * filtered).astype(jnp.bfloat16)
-    (mixed,) = exchange([mixed.reshape(seq_count, half, width, LANES)], seq_count, 1)
-    mixed = mixed.transpose(1, 0, 2, 3).reshape(half, seq_count * width, LANES)
-    gathered = lax.all_gather(mixed, "ch", axis=1, tiled=True)
+    chans = lax.axis_size("ch")
+    gathered = return_and_gather(mixed.reshape(seq_count, half, width, LANES), seq_count, chans, 1)
+    gathered = gathered.reshape(half, chans * seq_count * width, LANES)
     summed = jnp.einsum(
         "ncm,co->nmo", gathered, out_weight, preferred_element_type=jnp.float32
     )

time: 159 us -> 124 us (0.78)
  waiting for transfers between devices: 33.4 us -> 0 us
  Pallas kernels: 59.7 us -> 81.4 us
  between operations: 13.7 us -> 0.4 us
  local copies, waits for them, and re-layouts: 21.4 us -> 14.4 us
  other arithmetic: 11.2 us -> 9.08 us
    pallas_call x0 -> x1, Pallas kernels: none -> 35.2 us  [return_and_gather(): pl.pallas_call(functools.partial(return_kernel, group, chans), out_shape=...]
    all_gather x1 -> x0, waiting for transfers between devices: 33.4 us -> none  [on_device(): gathered = lax.all_gather(mixed, 'ch', axis=1, tiled=True)]
    pallas_call x2 -> x1, Pallas kernels: 59.7 us -> 46.1 us  [exchange(): pl.pallas_call(functools.partial(exchange_kernel, group, count), out_shap...]
    slice x6, local copies, waits for them, and re-layouts: 6.05 us -> 1.61 us  [shift_seq(): prev[:, :, lanes - distance:]]
    unnamed x31 -> x29, local copies, waits for them, and re-layouts: 7.98 us -> 4.16 us
    reshape x1, local copies, waits for them, and re-layouts: 0.93 us -> 3.2 us  [on_device(): gathered = gathered.reshape(half, chans * seq_count * width, LANES)]
    mul x1, other arithmetic: 4 us -> 1.88 us  [on_device(): mixed_in = short_conv(spread[1], taps[1]) * short_conv(spread[2], taps[2])]
  transfers between devices with their start and end apart: 1 -> 0, of which waited for: 1 -> 0; matrix products, arithmetic and copies ran while one was open for 0% -> 0% of each run, Pallas kernels for 0% -> 0%
where the time goes in v7:
time: 124 us
  Pallas kernels  81.4 us (66%)
  matrix products  18.4 us (15%)
  local copies, waits for them, and re-layouts  14.4 us (12%)
  other arithmetic  9.08 us (7%)
    pallas_call x1, Pallas kernels, exchange(): pl.pallas_call(functools.partial(exchange_kernel, group, count), out_shap...  46.1 us
    pallas_call x1, Pallas kernels, return_and_gather(): pl.pallas_call(functools.partial(return_kernel, group, chans), out_shape=...  35.2 us
    dot_general x6, matrix products, contract(): jnp.einsum(pattern, first_op, second_op, precision=high, preferred_elemen...  13.6 us
    dot_general x1, matrix products, on_device(): jnp.einsum('ncm,co->nmo', gathered, out_weight, preferred_element_type=jn...  4.78 us
    unnamed x29, local copies, waits for them, and re-layouts  4.16 us
    reshape x1, local copies, waits for them, and re-layouts, on_device(): gathered = gathered.reshape(half, chans * seq_count * width, LANES)  3.2 us

profile of v7, /device:TPU:1, one launch (start us, length us, event | category | flops | bytes accessed | tf_op | source)
XLA Modules:
  0.0 123.5 jit_solution(1237363261073995474)
XLA Ops:
  0.0 0.9 fusion.29
  0.9 1.2 convert_element_type.15
  2.7 0.4 copy-done.4
  3.8 1.4 %pad_maximum_fusion.3.refs_0_ = bf16[32,4,3,16,128]{4,3,2,1,0:T(8,128)(2,1)} fusion(bf16[32,1,3,16,128]{4,3,2,1,0:T(8,128)(2,1)S(1)} %get-tuple-element.30, bf16[32,1,3,16,128]{4,3,2,1,0:T(8,128)(2,1)S(1)} %get-tuple-element.31, bf16[32,1,3,16,128]{4,3,2,1,0:T(8,128)(2,1)S(1)} %get-tuple-element.32, bf16[32,1,3,16,128]{4,3,2,1,0:T(8,128)(2,1)S(1)} %get-tuple-element.33), kind=kLoop, calls=%fused_computation.13 | loop fusion | flops 2359296 | bytes 3145728 | tf_op jit(solution)/shard_map/stack | solution.py:278
  5.1 46.1 %shard_map.127 = bf16[32,4,3,16,128]{4,3,2,1,0:T(8,128)(2,1)} custom-call(bf16[32,4,3,16,128]{4,3,2,1,0:T(8,128)(2,1)} %pad_maximum_fusion.3.refs_0_), custom_call_target="tpu_custom_call" | custom-call | tf_op jit(solution)/shard_map/pallas_call | solution.py:64
  51.3 1.8 %bitcast_convert_fusion = f32[4,32,3,16,128]{4,3,2,0,1:T(8,128)S(1)} fusion(bf16[32,4,3,16,128]{4,3,2,1,0:T(8,128)(2,1)} %shard_map.127), kind=kLoop, calls=%fused_computation.69 | loop fusion | flops 786432 | bytes 4718592 | tf_op jit(solution)/shard_map/convert_element_type | solution.py:284
  56.4 1.9 %fusion.23 = f32[96,16,128]{2,0,1:T(8,128)S(1)} fusion(f32[96,16,127]{2,0,1:T(8,128)S(1)} %copy.104, f32[96,16,1]{2,0,1:T(8,128)S(1)} %pad_slice_fusion.3, f32[96,16,126]{2,0,1:T(8,128)S(1)} %copy.105, f32[96,16,2]{2,0,1:T(8,128)S(1)} %pad_slice_fusion.2, f32[96,16,127]{2,0,1:T(8,128)S(1)} %copy.106, f32[96,16,1]{2,0,1:T(8,128)S(1)} %pad_slice_fusion.1, ...), kind=kLoop, calls=%fused_computation.33 | loop fusion | flops 2949120 | bytes 5505408 | tf_op jit(solution)/shard_map/mul | solution.py:286
  58.3 1.5 %fusion.36 = f32[384,16,128]{2,0,1:T(8,128)S(1)} fusion(f32[384,96,1]{0,1,2:T(8,128)S(1)} %copy-done.1, f32[96,16,128]{2,0,1:T(8,128)S(1)} %fusion.23), kind=kOutput, calls=%fused_computation.72 | convolution fusion | flops 452984832 | bytes 4079616 | tf_op jit(solution)/shard_map/kn,ncm->kcm/dot_general | solution.py:192
  59.8 1.0 slice.210
  60.8 1.0 fusion.26
  61.9 1.3 %multiply_subtract_fusion.3 = (f32[192,16,128]{2,0,1:T(8,128)S(1)}, f32[192,16,128]{2,0,1:T(8,128)S(1)}, f32[192,16,128]{2,0,1:T(8,128)S(1)}, f32[192,16,128]{2,0,1:T(8,128)S(1)}) fusion(f32[384,16,128]{2,0,1:T(8,128)S(1)} %fusion.36, f32[192,128]{1,0:T(8,128)S(1)} %copy-done.8, f32[192,128]{1,0:T(8,128)S(1)} %copy-done.2, f32[384,16,128]{2,0,1:T(8,128)S(1)} %fusion.26), kind=kLoop, calls=%fused_computation.21 | loop fusion | flops 4718592 | bytes 12779520 | tf_op jit(solution)/shard_map/sub | solution.py:224
  63.4 0.7 copy-done
  64.1 3.2 %fusion.8 = f32[192,16,256]{2,1,0:T(8,128)S(1)} fusion(f32[256,256,1]{1,0,2:T(8,128)S(1)} %copy-done, f32[192,16,256]{2,0,1:T(8,128)S(1)} %pad_maximum_fusion), kind=kOutput, calls=%fused_computation.11 | convolution fusion | flops 1207959552 | bytes 6553600 | tf_op jit(solution)/shard_map/kcm,mj->kcj/dot_general | solution.py:192
  67.6 3.0 %fusion.6 = f32[192,16,256]{2,1,0:T(8,128)S(1)} fusion(f32[256,256,1]{1,0,2:T(8,128)S(1)} %copy-done, f32[192,16,256]{2,0,1:T(8,128)S(1)} %pad_maximum_fusion.1), kind=kOutput, calls=%fused_computation.9 | convolution fusion | flops 1207959552 | bytes 6553600 | tf_op jit(solution)/shard_map/kcm,mj->kcj/dot_general | solution.py:192
  70.6 0.4 multiply_subtract_fusion.1
  71.3 0.7 copy-done.6
  72.0 3.0 %fusion.4 = f32[192,16,256]{2,0,1:T(8,128)S(1)} fusion(f32[256,256,1]{1,0,2:T(8,128)S(1)} %copy-done.6, f32[192,16,256]{2,1,0:T(8,128)S(1)} %pad_maximum_fusion.2), kind=kOutput, calls=%fused_computation.7 | convolution fusion | flops 1207959552 | bytes 6553600 | tf_op jit(solution)/shard_map/kcj,jm->kcm/dot_general | solution.py:192
  75.0 0.5 multiply_subtract_fusion
  76.8 0.8 dynamic_slice.7
  77.5 1.9 %fusion.16 = bf16[96,16,128]{2,0,1:T(8,128)(2,1)S(1)} fusion(f32[96,384,1]{1,0,2:T(8,128)S(1)} %copy-done.7, f32[192,16,128]{2,0,1:T(8,128)S(1)} %get-tuple-element.8, f32[192,16,128]{2,0,1:T(8,128)S(1)} %get-tuple-element.7, f32[96,16,127]{2,0,1:T(8,128)S(1)} %copy.108, f32[96,16,1]{2,0,1:T(8,128)S(1)} %pad_slice_fusion.5, f32[96,16,126]{2,0,1:T(8,128)S(1)} %copy.109, ...), kind=kOutput, calls=%fused_computation.24 | convolution fusion | flops 455933952 | bytes 6832384 | tf_op jit(solution)/shard_map/nk,kcm->ncm/dot_general | solution.py:192
  79.4 0.9 copy.79
  80.3 35.2 %shard_map.128 = bf16[3,8,32,16,128]{4,3,2,1,0:T(8,128)(2,1)} custom-call(bf16[32,3,16,128]{3,2,1,0:T(8,128)(2,1)} %bitcast.110), custom_call_target="tpu_custom_call" | custom-call | tf_op jit(solution)/shard_map/pallas_call | solution.py:172
  115.6 3.2 %copy.80 = bf16[3,4096,128]{1,2,0:T(8,128)(2,1)S(1)} copy(bf16[3,4096,128]{2,1,0:T(8,128)(2,1)} %bitcast.99) | data formatting | bytes 6291456 | tf_op jit(solution)/shard_map/reshape | solution.py:292
  118.8 4.8 %convolution_convert_fusion = bf16[384,512]{1,0:T(8,128)(2,1)} fusion(bf16[384,4096]{1,0:T(8,128)(2,1)S(1)} %bitcast.108, bf16[4096,512]{1,0:T(8,128)(2,1)} %param.19), kind=kOutput, calls=%fused_computation.25 | convolution fusion | flops 1610809344 | bytes 7733248 | tf_op jit(solution)/shard_map/ncm,co->nmo/dot_general | solution.py:293
  (44 shorter events, 6.5 us)
Async XLA Ops:
  0.0 2.4 %copy-start.3 = (bf16[384,512]{1,0:T(8,128)(2,1)S(1)}, bf16[384,512]{1,0:T(8,128)(2,1)}, u32[]{:S(2)}) copy-start(bf16[384,512]{1,0:T(8,128)(2,1)} %param.15) | copy-start | bytes 1179652
  2.1 1.0 copy-start.4
  2.4 1.0 copy-start.5
  56.4 1.9 %copy-start.1 = (f32[384,96,1]{0,1,2:T(8,128)S(1)}, f32[384,96,1]{0,1,2:T(8,128)}, u32[]{:S(2)}) copy-start(f32[384,96,1]{0,1,2:T(8,128)} %constant.43) | copy-start | bytes 442372
  60.8 1.1 copy-start.2
  60.8 1.1 copy-start.8
  63.2 1.0 copy-start
  71.0 1.0 copy-start.6
  72.0 3.0 %copy-start.9 = (f32[192,128]{1,0:T(8,128)S(1)}, f32[192,128]{1,0:T(8,128)}, u32[]{:S(2)}) copy-start(f32[192,128]{1,0:T(8,128)} %constant.41) | copy-start | bytes 294916
  76.2 1.3 %copy-start.7 = (f32[96,384,1]{1,0,2:T(8,128)S(1)}, f32[96,384,1]{1,0,2:T(8,128)}, u32[]{:S(2)}) copy-start(f32[96,384,1]{1,0,2:T(8,128)} %constant.42) | copy-start | bytes 442372

commit v8 on v7

--- a/solution.py
+++ b/solution.py
@@ -274,7 +274,8 @@
     def by_target(block):
         return to_ncm(block).reshape(half, seq_count, width, LANES).transpose(1, 0, 2, 3)
 
-    planes = [out_gate, in_gate, values, long_filter.astype(jnp.bfloat16)]
+    gate_in = lax.all_to_all(to_ncm(out_gate), "seq", split_axis=1, concat_axis=0, tiled=True)
+    planes = [in_gate, values, long_filter.astype(jnp.bfloat16)]
     stacked = jnp.stack([by_target(plane) for plane in planes], axis=1)
     (spread,) = exchange([stacked], seq_count, 0)
     spread = spread.transpose(1, 0, 2, 3, 4).reshape(len(planes), seq_count * half, width, LANES)
@@ -282,9 +283,9 @@
     taps = lax.dynamic_slice_in_dim(short_filter, start, width, axis=2)
     gain = lax.dynamic_slice_in_dim(skip_gain, start, width, axis=0)
     spread = spread.astype(jnp.float32)
-    gate_late = short_conv(spread[0], taps[0])
-    mixed_in = short_conv(spread[1], taps[1]) * short_conv(spread[2], taps[2])
-    long_out = long_conv(mixed_in, spread[3])
+    mixed_in = short_conv(spread[0], taps[1]) * short_conv(spread[1], taps[2])
+    long_out = long_conv(mixed_in, spread[2])
+    gate_late = short_conv(gate_in.astype(jnp.float32), taps[0])
     filtered = long_out + gain[None, :, None] * mixed_in
     mixed = (gate_late * filtered).astype(jnp.bfloat16)
     chans = lax.axis_size("ch")

time: 124 us -> 141 us (1.14)
  starting transfers between devices: 0 us -> 12.1 us
  local copies, waits for them, and re-layouts: 14.4 us -> 24.1 us
  Pallas kernels: 81.4 us -> 74.9 us
  other arithmetic: 9.08 us -> 10.8 us
    all_to_all x0 -> x1, starting transfers between devices: none -> 12.1 us  [on_device(): lax.all_to_all(to_ncm(out_gate), 'seq', split_axis=1, concat_axis=0, tile...]
    pallas_call x1, Pallas kernels: 46.1 us -> 37.9 us  [exchange(): pl.pallas_call(functools.partial(exchange_kernel, group, count), out_shap...]
    unnamed x29 -> x33, local copies, waits for them, and re-layouts: 4.16 us -> 8.37 us
    slice x6, local copies, waits for them, and re-layouts: 1.61 us -> 4.31 us  [shift_seq(): prev[:, :, lanes - distance:]]
    transpose x4, local copies, waits for them, and re-layouts: 0.87 us -> 2.78 us  [to_ncm(): return block.reshape(rows // LANES, LANES, width).transpose(0, 2, 1)]
    mul x1, other arithmetic: 1.88 us -> 3.77 us  [on_device(): mixed_in = short_conv(spread[0], taps[1]) * short_conv(spread[1], taps[2])]
    pallas_call x1, Pallas kernels: 35.2 us -> 37.1 us  [return_and_gather(): pl.pallas_call(functools.partial(return_kernel, group, chans), out_shape=...]
    sub x1, other arithmetic: 0.46 us -> 2.11 us  [inverse(): stacked = jnp.concatenate([zr * tc - zi * ts, zr * ts + zi * tc], axis=0)]
  transfers between devices with their start and end apart: 0 -> 1, of which waited for: 0 -> 0; matrix products, arithmetic and copies ran while one was open for 0% -> 25% of each run, Pallas kernels for 0% -> 27%
where the time goes in v8:
time: 141 us
  Pallas kernels  74.9 us (53%)
  local copies, waits for them, and re-layouts  24.1 us (17%)
  matrix products  18.3 us (13%)
  starting transfers between devices  12.1 us (9%)
  other arithmetic  10.8 us (8%)
    pallas_call x1, Pallas kernels, exchange(): pl.pallas_call(functools.partial(exchange_kernel, group, count), out_shap...  37.9 us
    pallas_call x1, Pallas kernels, return_and_gather(): pl.pallas_call(functools.partial(return_kernel, group, chans), out_shape=...  37.1 us
    dot_general x6, matrix products, contract(): jnp.einsum(pattern, first_op, second_op, precision=high, preferred_elemen...  13.6 us
    all_to_all x1, starting transfers between devices, on_device(): lax.all_to_all(to_ncm(out_gate), 'seq', split_axis=1, concat_axis=0, tile...  12.1 us
    unnamed x33, local copies, waits for them, and re-layouts  8.37 us
    dot_general x1, matrix products, on_device(): jnp.einsum('ncm,co->nmo', gathered, out_weight, preferred_element_type=jn...  4.72 us
    slice x6, local copies, waits for them, and re-layouts, shift_seq(): prev[:, :, lanes - distance:]  4.31 us
    mul x1, other arithmetic, on_device(): mixed_in = short_conv(spread[0], taps[1]) * short_conv(spread[1], taps[2])  3.77 us
  transfers between devices with their start and end apart: 1, of which 0 were waited for; matrix products, arithmetic and copies ran while one was open for 25% of the time, Pallas kernels for 27%

profile of v8, /device:TPU:1, one launch (start us, length us, event | category | flops | bytes accessed | tf_op | source)
XLA Modules:
  0.0 140.7 jit_solution(9893414896826979459)
XLA Ops:
  0.0 2.1 %copy.78 = bf16[3,512,128]{2,0,1:T(4,128)(2,1)} copy(bf16[3,512,128]{1,2,0:T(8,128)(2,1)} %bitcast.113) | data formatting | bytes 786432 | tf_op jit(solution)/shard_map/transpose | solution.py:264
  2.1 12.1 %all-to-all-start = ((bf16[3,512,128]{2,0,1:T(4,128)(2,1)}), bf16[3,512,128]{2,0,1:T(4,128)(2,1)}, u32[]{:S(2)}, u32[]{:S(2)}) async-start(bf16[3,512,128]{2,0,1:T(4,128)(2,1)} %copy.78), calls=%async_computation | async-start | bytes 1048576 | tf_op jit(solution)/shard_map/all_to_all | solution.py:277
  15.7 1.1 pad_maximum_fusion.3.refs_0_
  16.8 37.9 %shard_map.127 = bf16[32,3,3,16,128]{4,3,2,1,0:T(8,128)(2,1)} custom-call(bf16[32,3,3,16,128]{4,3,2,1,0:T(8,128)(2,1)} %pad_maximum_fusion.3.refs_0_), custom_call_target="tpu_custom_call" | custom-call | tf_op jit(solution)/shard_map/pallas_call | solution.py:64
  54.7 1.4 %bitcast_convert_fusion = f32[3,32,3,16,128]{4,3,2,0,1:T(8,128)S(1)} fusion(bf16[32,3,3,16,128]{4,3,2,1,0:T(8,128)(2,1)} %shard_map.127), kind=kLoop, calls=%fused_computation.68 | loop fusion | flops 589824 | bytes 3538944 | tf_op jit(solution)/shard_map/convert_element_type | solution.py:285
  57.1 1.2 pad_slice_fusion.1
  58.6 1.1 pad_slice_fusion.2
  59.7 1.2 pad_slice_fusion.3
  60.9 1.1 copy.127
  62.0 1.1 copy.128
  63.2 1.1 copy.129
  64.3 1.1 copy.130
  67.4 3.8 %fusion.23 = f32[96,16,128]{2,0,1:T(8,128)S(1)} fusion(f32[96,16,127]{2,0,1:T(8,128)} %copy.127, f32[96,16,1]{2,0,1:T(8,128)} %pad_slice_fusion.3, f32[96,16,126]{2,0,1:T(8,128)} %copy.128, f32[96,16,2]{2,0,1:T(8,128)} %pad_slice_fusion.2, f32[96,16,127]{2,0,1:T(8,128)} %copy.129, f32[96,16,1]{2,0,1:T(8,128)} %pad_slice_fusion.1, f32[96,16,126]{2,0,1:T(8,128)} %copy.130, ...), kind=kLoop, calls=%fused_computation.33 | loop fusion | flops 2949120 | bytes 5505408 | tf_op jit(solution)/shard_map/mul | solution.py:286
  71.2 1.5 %fusion.36 = f32[384,16,128]{2,0,1:T(8,128)S(1)} fusion(f32[384,96,1]{0,1,2:T(8,128)S(1)} %copy-done.4, f32[96,16,128]{2,0,1:T(8,128)S(1)} %fusion.23), kind=kOutput, calls=%fused_computation.71 | convolution fusion | flops 452984832 | bytes 4079616 | tf_op jit(solution)/shard_map/kn,ncm->kcm/dot_general | solution.py:192
  73.7 1.1 multiply_subtract_fusion.3
  75.8 3.2 %fusion.8 = f32[192,16,256]{2,1,0:T(8,128)S(1)} fusion(f32[256,256,1]{1,0,2:T(8,128)S(1)} %copy-done.2, f32[192,16,256]{2,0,1:T(8,128)S(1)} %pad_maximum_fusion), kind=kOutput, calls=%fused_computation.11 | convolution fusion | flops 1207959552 | bytes 6553600 | tf_op jit(solution)/shard_map/kcm,mj->kcj/dot_general | solution.py:192
  79.3 3.0 %fusion.6 = f32[192,16,256]{2,1,0:T(8,128)S(1)} fusion(f32[256,256,1]{1,0,2:T(8,128)S(1)} %copy-done.2, f32[192,16,256]{2,0,1:T(8,128)S(1)} %pad_maximum_fusion.1), kind=kOutput, calls=%fused_computation.9 | convolution fusion | flops 1207959552 | bytes 6553600 | tf_op jit(solution)/shard_map/kcm,mj->kcj/dot_general | solution.py:192
  83.7 3.0 %fusion.4 = f32[192,16,256]{2,0,1:T(8,128)S(1)} fusion(f32[256,256,1]{1,0,2:T(8,128)S(1)} %copy-done.8, f32[192,16,256]{2,1,0:T(8,128)S(1)} %pad_maximum_fusion.2), kind=kOutput, calls=%fused_computation.7 | convolution fusion | flops 1207959552 | bytes 6553600 | tf_op jit(solution)/shard_map/kcj,jm->kcm/dot_general | solution.py:192
  86.8 2.1 %multiply_subtract_fusion = (f32[192,16,128]{2,0,1:T(8,128)}, f32[192,16,128]{2,0,1:T(8,128)}) fusion(f32[192,16,256]{2,0,1:T(8,128)S(1)} %fusion.4, f32[192,128]{1,0:T(8,128)S(1)} %copy-done.11, f32[192,128]{1,0:T(8,128)S(1)} %copy-done.5), kind=kLoop, calls=%fused_computation.14 | loop fusion | flops 2359296 | bytes 6488064 | tf_op jit(solution)/shard_map/sub | solution.py:232
  88.9 1.1 copy.79
  92.9 1.9 %fusion.16 = bf16[96,16,128]{2,0,1:T(8,128)(2,1)S(1)} fusion(f32[96,384,1]{1,0,2:T(8,128)S(1)} %copy-done.9, f32[192,16,128]{2,0,1:T(8,128)S(1)} %copy-done.1, f32[192,16,128]{2,0,1:T(8,128)S(1)} %copy-done, f32[96,16,127]{2,0,1:T(8,128)S(1)} %copy.131, f32[96,16,1]{2,0,1:T(8,128)S(1)} %pad_slice_fusion.5, f32[96,16,126]{2,0,1:T(8,128)S(1)} %copy.133, ...), kind=kOutput, calls=%fused_computation.23 | convolution fusion | flops 455933952 | bytes 6832384 | tf_op jit(solution)/shard_map/nk,kcm->ncm/dot_general | solution.py:192
  95.7 37.1 %shard_map.128 = bf16[3,8,32,16,128]{4,3,2,1,0:T(8,128)(2,1)} custom-call(bf16[32,3,16,128]{3,2,1,0:T(8,128)(2,1)} %bitcast.108), custom_call_target="tpu_custom_call" | custom-call | tf_op jit(solution)/shard_map/pallas_call | solution.py:172
  132.8 3.2 %copy.106 = bf16[3,4096,128]{1,2,0:T(8,128)(2,1)S(1)} copy(bf16[3,4096,128]{2,1,0:T(8,128)(2,1)} %bitcast.91) | data formatting | bytes 6291456 | tf_op jit(solution)/shard_map/reshape | solution.py:293
  136.0 4.7 %convolution_convert_fusion = bf16[384,512]{1,0:T(8,128)(2,1)} fusion(bf16[384,4096]{1,0:T(8,128)(2,1)S(1)} %bitcast.104, bf16[4096,512]{1,0:T(8,128)(2,1)} %param.19), kind=kOutput, calls=%fused_computation.24 | convolution fusion | flops 1610809344 | bytes 7733248 | tf_op jit(solution)/shard_map/ncm,co->nmo/dot_general | solution.py:294
  (54 shorter events, 12.0 us)
Async XLA Ops:
  0.0 14.3 %copy-start.3 = (f32[384,512]{1,0:T(8,128)S(1)}, f32[384,512]{1,0:T(8,128)}, u32[]{:S(2)}) copy-start(f32[384,512]{1,0:T(8,128)} %param.17) | copy-start | bytes 2359300
  2.1 12.4 %copy-start.6 = (bf16[384,512]{1,0:T(8,128)(2,1)S(1)}, bf16[384,512]{1,0:T(8,128)(2,1)}, u32[]{:S(2)}) copy-start(bf16[384,512]{1,0:T(8,128)(2,1)} %param.15) | copy-start | bytes 1179652
  2.1 86.7 %all-to-all-start = ((bf16[3,512,128]{2,0,1:T(4,128)(2,1)}), bf16[3,512,128]{2,0,1:T(4,128)(2,1)}, u32[]{:S(2)}, u32[]{:S(2)}) async-start(bf16[3,512,128]{2,0,1:T(4,128)(2,1)} %copy.78), calls=%async_computation | async-start | bytes 1048576 | tf_op jit(solution)/shard_map/all_to_all | solution.py:277
  14.3 1.0 copy-start.7
  67.4 3.8 %copy-start.4 = (f32[384,96,1]{0,1,2:T(8,128)S(1)}, f32[384,96,1]{0,1,2:T(8,128)}, u32[]{:S(2)}) copy-start(f32[384,96,1]{0,1,2:T(8,128)} %constant.43) | copy-start | bytes 442372
  72.6 1.1 copy-start.5
  72.6 1.1 copy-start.10
  74.8 1.0 copy-start.2
  82.7 1.0 copy-start.8
  83.7 3.0 %copy-start.11 = (f32[192,128]{1,0:T(8,128)S(1)}, f32[192,128]{1,0:T(8,128)}, u32[]{:S(2)}) copy-start(f32[192,128]{1,0:T(8,128)} %constant.41) | copy-start | bytes 294916
  90.7 0.9 copy-start.9
  91.0 1.4 %copy-start = (f32[192,16,128]{2,0,1:T(8,128)S(1)}, f32[192,16,128]{2,0,1:T(8,128)}, u32[]{:S(2)}) copy-start(f32[192,16,128]{2,0,1:T(8,128)} %get-tuple-element.7) | copy-start | bytes 4718596
  91.0 1.9 %copy-start.1 = (f32[192,16,128]{2,0,1:T(8,128)S(1)}, f32[192,16,128]{2,0,1:T(8,128)}, u32[]{:S(2)}) copy-start(f32[192,16,128]{2,0,1:T(8,128)} %get-tuple-element.8) | copy-start | bytes 4718596

commit v9 on v7

--- a/solution.py
+++ b/solution.py
@@ -18,11 +18,6 @@
     send_sem, recv_sem, local_sem = refs[2 * count :]
     me = lax.axis_index("seq")
     ch = lax.axis_index("ch")
-    barrier = pltpu.get_barrier_semaphore()
-    for step in range(1, group):
-        peer = lax.rem(me + step, group)
-        pl.semaphore_signal(barrier, inc=1, device_id=(peer, ch), device_id_type=MESH)
-    pl.semaphore_wait(barrier, group - 1)
     locals_ = []
     for a in range(count):
         cp = pltpu.make_async_copy(sources[a].at[me], targets[a].at[me], local_sem.at[a])
@@ -71,7 +66,7 @@
             pltpu.SemaphoreType.DMA((count, group)),
             pltpu.SemaphoreType.DMA((count,)),
         ],
-        compiler_params=pltpu.CompilerParams(collective_id=tag, has_side_effects=True),
+        compiler_params=pltpu.CompilerParams(has_side_effects=True),
     )(*arrays)
 
 
@@ -81,13 +76,6 @@
     half = source.shape[1]
     sibling = ch + 1 - 2 * lax.rem(ch, 2)
     across = [lax.rem(ch + 2 * hop, chans) for hop in range(1, chans // 2)]
-    barrier = pltpu.get_barrier_semaphore()
-    for step in range(1, group):
-        peer = lax.rem(me + step, group)
-        pl.semaphore_signal(barrier, inc=1, device_id=(peer, ch), device_id_type=MESH)
-    for peer_ch in across + [sibling]:
-        pl.semaphore_signal(barrier, inc=1, device_id=(me, peer_ch), device_id_type=MESH)
-    pl.semaphore_wait(barrier, group - 1 + len(across) + 1)
 
     def incoming(part, slot, peer_ch):
         return pltpu.make_async_remote_copy(
@@ -184,7 +172,7 @@
             pltpu.SemaphoreType.DMA((half, chans // 2)),
             pltpu.SemaphoreType.DMA((half,)),
         ],
-        compiler_params=pltpu.CompilerParams(collective_id=tag, has_side_effects=True),
+        compiler_params=pltpu.CompilerParams(has_side_effects=True),
     )(block)
 
 

time: 124 us -> 140 us (1.13)
  Pallas kernels: 81.4 us -> 97.9 us
    pallas_call x1, Pallas kernels: 46.1 us -> 55 us  [exchange(): pl.pallas_call(functools.partial(exchange_kernel, group, count), out_shap...]
    pallas_call x1, Pallas kernels: 35.2 us -> 42.8 us  [return_and_gather(): pl.pallas_call(functools.partial(return_kernel, group, chans), out_shape=...]
where the time goes in v9:
time: 140 us
  Pallas kernels  97.9 us (70%)
  matrix products  17.9 us (13%)
  local copies, waits for them, and re-layouts  14.4 us (10%)
  other arithmetic  9.25 us (7%)
    pallas_call x1, Pallas kernels, exchange(): pl.pallas_call(functools.partial(exchange_kernel, group, count), out_shap...  55 us
    pallas_call x1, Pallas kernels, return_and_gather(): pl.pallas_call(functools.partial(return_kernel, group, chans), out_shape=...  42.8 us
    dot_general x6, matrix products, contract(): jnp.einsum(pattern, first_op, second_op, precision=high, preferred_elemen...  13.2 us
    dot_general x1, matrix products, on_device(): jnp.einsum('ncm,co->nmo', gathered, out_weight, preferred_element_type=jn...  4.78 us
    unnamed x29, local copies, waits for them, and re-layouts  4.16 us
    reshape x1, local copies, waits for them, and re-layouts, on_device(): gathered = gathered.reshape(half, chans * seq_count * width, LANES)  3.2 us

profile of v9, /device:TPU:1, one launch (start us, length us, event | category | flops | bytes accessed | tf_op | source)
XLA Modules:
  0.0 139.9 jit_solution(18118176327975929829)
XLA Ops:
  0.0 0.9 fusion.29
  0.9 1.2 convert_element_type.15
  3.8 1.4 pad_maximum_fusion.3.refs_0_
  5.1 55.0 %shard_map.127 = bf16[32,4,3,16,128]{4,3,2,1,0:T(8,128)(2,1)} custom-call(bf16[32,4,3,16,128]{4,3,2,1,0:T(8,128)(2,1)} %pad_maximum_fusion.3.refs_0_), custom_call_target="tpu_custom_call" | custom-call | tf_op jit(solution)/shard_map/pallas_call | solution.py:59
  60.2 1.8 %bitcast_convert_fusion = f32[4,32,3,16,128]{4,3,2,0,1:T(8,128)S(1)} fusion(bf16[32,4,3,16,128]{4,3,2,1,0:T(8,128)(2,1)} %shard_map.127), kind=kLoop, calls=%fused_computation.69 | loop fusion | flops 786432 | bytes 4718592 | tf_op jit(solution)/shard_map/convert_element_type | solution.py:272
  65.3 1.9 %fusion.23 = f32[96,16,128]{2,0,1:T(8,128)S(1)} fusion(f32[96,16,127]{2,0,1:T(8,128)S(1)} %copy.104, f32[96,16,1]{2,0,1:T(8,128)S(1)} %pad_slice_fusion.3, f32[96,16,126]{2,0,1:T(8,128)S(1)} %copy.105, f32[96,16,2]{2,0,1:T(8,128)S(1)} %pad_slice_fusion.2, f32[96,16,127]{2,0,1:T(8,128)S(1)} %copy.106, f32[96,16,1]{2,0,1:T(8,128)S(1)} %pad_slice_fusion.1, ...), kind=kLoop, calls=%fused_computation.33 | loop fusion | flops 2949120 | bytes 5505408 | tf_op jit(solution)/shard_map/mul | solution.py:274
  67.2 1.5 %fusion.36 = f32[384,16,128]{2,0,1:T(8,128)S(1)} fusion(f32[384,96,1]{0,1,2:T(8,128)S(1)} %copy-done.1, f32[96,16,128]{2,0,1:T(8,128)S(1)} %fusion.23), kind=kOutput, calls=%fused_computation.72 | convolution fusion | flops 452984832 | bytes 4079616 | tf_op jit(solution)/shard_map/kn,ncm->kcm/dot_general | solution.py:180
  68.7 1.0 slice.210
  69.7 1.0 fusion.26
  70.8 1.3 multiply_subtract_fusion.3
  72.3 0.7 copy-done
  73.0 3.0 %fusion.8 = f32[192,16,256]{2,1,0:T(8,128)S(1)} fusion(f32[256,256,1]{1,0,2:T(8,128)S(1)} %copy-done, f32[192,16,256]{2,0,1:T(8,128)S(1)} %pad_maximum_fusion), kind=kOutput, calls=%fused_computation.11 | convolution fusion | flops 1207959552 | bytes 6553600 | tf_op jit(solution)/shard_map/kcm,mj->kcj/dot_general | solution.py:180
  76.1 0.4 pad_maximum_fusion.1
  76.5 3.0 %fusion.6 = f32[192,16,256]{2,1,0:T(8,128)S(1)} fusion(f32[256,256,1]{1,0,2:T(8,128)S(1)} %copy-done, f32[192,16,256]{2,0,1:T(8,128)S(1)} %pad_maximum_fusion.1), kind=kOutput, calls=%fused_computation.9 | convolution fusion | flops 1207959552 | bytes 6553600 | tf_op jit(solution)/shard_map/kcm,mj->kcj/dot_general | solution.py:180
  79.5 0.4 multiply_subtract_fusion.1
  80.2 0.7 copy-done.6
  80.9 3.0 %fusion.4 = f32[192,16,256]{2,0,1:T(8,128)S(1)} fusion(f32[256,256,1]{1,0,2:T(8,128)S(1)} %copy-done.6, f32[192,16,256]{2,1,0:T(8,128)S(1)} %pad_maximum_fusion.2), kind=kOutput, calls=%fused_computation.7 | convolution fusion | flops 1207959552 | bytes 6553600 | tf_op jit(solution)/shard_map/kcj,jm->kcm/dot_general | solution.py:180
  83.9 0.5 multiply_subtract_fusion
  85.7 0.8 dynamic_slice.7
  86.4 1.7 %fusion.16 = bf16[96,16,128]{2,0,1:T(8,128)(2,1)S(1)} fusion(f32[96,384,1]{1,0,2:T(8,128)S(1)} %copy-done.7, f32[192,16,128]{2,0,1:T(8,128)S(1)} %get-tuple-element.8, f32[192,16,128]{2,0,1:T(8,128)S(1)} %get-tuple-element.7, f32[96,16,127]{2,0,1:T(8,128)S(1)} %copy.108, f32[96,16,1]{2,0,1:T(8,128)S(1)} %pad_slice_fusion.5, f32[96,16,126]{2,0,1:T(8,128)S(1)} %copy.109, ...), kind=kOutput, calls=%fused_computation.24 | convolution fusion | flops 455933952 | bytes 6832384 | tf_op jit(solution)/shard_map/nk,kcm->ncm/dot_general | solution.py:180
  88.1 0.9 copy.79
  89.0 42.8 %shard_map.128 = bf16[3,8,32,16,128]{4,3,2,1,0:T(8,128)(2,1)} custom-call(bf16[32,3,16,128]{3,2,1,0:T(8,128)(2,1)} %bitcast.110), custom_call_target="tpu_custom_call" | custom-call | tf_op jit(solution)/shard_map/pallas_call | solution.py:160
  131.9 3.2 %copy.80 = bf16[3,4096,128]{1,2,0:T(8,128)(2,1)S(1)} copy(bf16[3,4096,128]{2,1,0:T(8,128)(2,1)} %bitcast.99) | data formatting | bytes 6291456 | tf_op jit(solution)/shard_map/reshape | solution.py:280
  135.1 4.8 %convolution_convert_fusion = bf16[384,512]{1,0:T(8,128)(2,1)} fusion(bf16[384,4096]{1,0:T(8,128)(2,1)S(1)} %bitcast.108, bf16[4096,512]{1,0:T(8,128)(2,1)} %param.19), kind=kOutput, calls=%fused_computation.25 | convolution fusion | flops 1610809344 | bytes 7733248 | tf_op jit(solution)/shard_map/ncm,co->nmo/dot_general | solution.py:281
  (44 shorter events, 6.6 us)
Async XLA Ops:
  0.0 2.4 %copy-start.3 = (bf16[384,512]{1,0:T(8,128)(2,1)S(1)}, bf16[384,512]{1,0:T(8,128)(2,1)}, u32[]{:S(2)}) copy-start(bf16[384,512]{1,0:T(8,128)(2,1)} %param.15) | copy-start | bytes 1179652
  2.1 1.0 copy-start.4
  2.4 1.0 copy-start.5
  65.3 1.9 %copy-start.1 = (f32[384,96,1]{0,1,2:T(8,128)S(1)}, f32[384,96,1]{0,1,2:T(8,128)}, u32[]{:S(2)}) copy-start(f32[384,96,1]{0,1,2:T(8,128)} %constant.43) | copy-start | bytes 442372
  69.7 1.1 copy-start.2
  69.7 1.1 copy-start.8
  72.1 1.0 copy-start
  79.9 1.0 copy-start.6
  80.9 3.0 %copy-start.9 = (f32[192,128]{1,0:T(8,128)S(1)}, f32[192,128]{1,0:T(8,128)}, u32[]{:S(2)}) copy-start(f32[192,128]{1,0:T(8,128)} %constant.41) | copy-start | bytes 294916
  85.1 1.3 copy-start.7

commit v10 on v7

--- a/solution.py
+++ b/solution.py
@@ -13,66 +13,70 @@
 MESH = pl.DeviceIdType.MESH
 
 
-def exchange_kernel(group, count, *refs):
-    sources, targets = refs[:count], refs[count : 2 * count]
-    send_sem, recv_sem, local_sem = refs[2 * count :]
+def exchange_kernel(group, source, target, send_sem, recv_sem, local_sem):
     me = lax.axis_index("seq")
     ch = lax.axis_index("ch")
+    half = source.shape[1]
+    width = target.shape[2]
     barrier = pltpu.get_barrier_semaphore()
     for step in range(1, group):
         peer = lax.rem(me + step, group)
         pl.semaphore_signal(barrier, inc=1, device_id=(peer, ch), device_id_type=MESH)
     pl.semaphore_wait(barrier, group - 1)
-    locals_ = []
-    for a in range(count):
-        cp = pltpu.make_async_copy(sources[a].at[me], targets[a].at[me], local_sem.at[a])
-        cp.start()
-        locals_.append(cp)
+
+    def piece(ref_src, peer, origin):
+        return (
+            ref_src.at[:, :, pl.ds(peer * width, width)],
+            target.at[:, pl.ds(origin * half, half)],
+        )
+
+    src, dst = piece(source, me, me)
+    local = pltpu.make_async_copy(src, dst, local_sem.at[0])
+    local.start()
     sent = []
     for step in range(1, group):
         peer = lax.rem(me + step, group)
-        for a in range(count):
-            cp = pltpu.make_async_remote_copy(
-                src_ref=sources[a].at[peer],
-                dst_ref=targets[a].at[me],
-                send_sem=send_sem.at[a, step],
-                recv_sem=recv_sem.at[a, step],
-                device_id=(peer, ch),
-                device_id_type=MESH,
-            )
-            cp.start()
-            sent.append(cp)
-    for cp in locals_:
-        cp.wait()
+        src, dst = piece(source, peer, me)
+        cp = pltpu.make_async_remote_copy(
+            src_ref=src,
+            dst_ref=dst,
+            send_sem=send_sem.at[step],
+            recv_sem=recv_sem.at[step],
+            device_id=(peer, ch),
+            device_id_type=MESH,
+        )
+        cp.start()
+        sent.append(cp)
+    local.wait()
     for cp in sent:
         cp.wait_send()
     for step in range(1, group):
         origin = lax.rem(me + group - step, group)
-        for a in range(count):
-            pltpu.make_async_remote_copy(
-                src_ref=sources[a].at[origin],
-                dst_ref=targets[a].at[origin],
-                send_sem=send_sem.at[a, step],
-                recv_sem=recv_sem.at[a, step],
-                device_id=(origin, ch),
-                device_id_type=MESH,
-            ).wait_recv()
-
-
-def exchange(arrays, group, tag):
-    count = len(arrays)
+        src, dst = piece(source, me, origin)
+        pltpu.make_async_remote_copy(
+            src_ref=src,
+            dst_ref=dst,
+            send_sem=send_sem.at[step],
+            recv_sem=recv_sem.at[step],
+            device_id=(origin, ch),
+            device_id_type=MESH,
+        ).wait_recv()
+
+
+def exchange(stacked, group, tag):
+    planes, half, full, lanes = stacked.shape
     return pl.pallas_call(
-        functools.partial(exchange_kernel, group, count),
-        out_shape=[jax.ShapeDtypeStruct(a.shape, a.dtype) for a in arrays],
-        in_specs=[pl.BlockSpec(memory_space=pl.ANY)] * count,
-        out_specs=[pl.BlockSpec(memory_space=pl.ANY)] * count,
+        functools.partial(exchange_kernel, group),
+        out_shape=jax.ShapeDtypeStruct((planes, group * half, full // group, lanes), stacked.dtype),
+        in_specs=[pl.BlockSpec(memory_space=pl.ANY)],
+        out_specs=pl.BlockSpec(memory_space=pl.ANY),
         scratch_shapes=[
-            pltpu.SemaphoreType.DMA((count, group)),
-            pltpu.SemaphoreType.DMA((count, group)),
-            pltpu.SemaphoreType.DMA((count,)),
+            pltpu.SemaphoreType.DMA((group,)),
+            pltpu.SemaphoreType.DMA((group,)),
+            pltpu.SemaphoreType.DMA((1,)),
         ],
         compiler_params=pltpu.CompilerParams(collective_id=tag, has_side_effects=True),
-    )(*arrays)
+    )(stacked)
 
 
 def return_kernel(group, chans, source, target, send_sem, recv_sem, pass_sem, got_sem, fwd_sem, local_sem):
@@ -236,8 +240,9 @@
 def long_conv(mixed_in, long_filter):
     half = mixed_in.shape[0]
     tb = tables(half * LANES)
-    xs = forward(mixed_in, tb)
-    hs = forward(long_filter, tb)
+    width = mixed_in.shape[1]
+    both = forward(jnp.concatenate([mixed_in, long_filter], axis=1), tb)
+    xs, hs = both[:, :width], both[:, width:]
     xr, xi = xs[:, :, :LANES], xs[:, :, LANES:]
     hr, hi = hs[:, :, :LANES], hs[:, :, LANES:]
     product = jnp.concatenate([xr * hr - xi * hi, xr * hi + xi * hr], axis=2)
@@ -271,13 +276,9 @@
     width = out_gate.shape[1] // seq_count
     half = rows // LANES
 
-    def by_target(block):
-        return to_ncm(block).reshape(half, seq_count, width, LANES).transpose(1, 0, 2, 3)
-
     planes = [out_gate, in_gate, values, long_filter.astype(jnp.bfloat16)]
-    stacked = jnp.stack([by_target(plane) for plane in planes], axis=1)
-    (spread,) = exchange([stacked], seq_count, 0)
-    spread = spread.transpose(1, 0, 2, 3, 4).reshape(len(planes), seq_count * half, width, LANES)
+    stacked = jnp.stack([to_ncm(plane) for plane in planes])
+    spread = exchange(stacked, seq_count, 0)
     start = seq_index * width
     taps = lax.dynamic_slice_in_dim(short_filter, start, width, axis=2)
     gain = lax.dynamic_slice_in_dim(skip_gain, start, width, axis=0)

time: 124 us -> 121 us (0.976)
  local copies, waits for them, and re-layouts: 14.4 us -> 12.1 us
    reshape x0 -> x4, local copies, waits for them, and re-layouts: none -> 2.87 us  [to_ncm(): return block.reshape(rows // LANES, LANES, width).transpose(0, 2, 1)]
    unnamed x29 -> x16, local copies, waits for them, and re-layouts: 4.16 us -> 2.4 us
    convert_element_type x0 -> x1, other arithmetic: none -> 1.67 us  [on_device(): mixed = (gate_late * filtered).astype(jnp.bfloat16)]
    dot_general x6 -> x4, matrix products: 13.6 us -> 12.5 us  [contract(): jnp.einsum(pattern, first_op, second_op, precision=high, preferred_elemen...]
where the time goes in v10:
time: 121 us
  Pallas kernels  81.4 us (67%)
  matrix products  17.3 us (14%)
  local copies, waits for them, and re-layouts  12.1 us (10%)
  other arithmetic  9.8 us (8%)
    pallas_call x1, Pallas kernels, exchange(): pl.pallas_call(functools.partial(exchange_kernel, group), out_shape=jax.S...  46.1 us
    pallas_call x1, Pallas kernels, return_and_gather(): pl.pallas_call(functools.partial(return_kernel, group, chans), out_shape=...  35.2 us
    dot_general x4, matrix products, contract(): jnp.einsum(pattern, first_op, second_op, precision=high, preferred_elemen...  12.5 us
    dot_general x1, matrix products, on_device(): jnp.einsum('ncm,co->nmo', gathered, out_weight, preferred_element_type=jn...  4.78 us
    reshape x1, local copies, waits for them, and re-layouts, on_device(): gathered = gathered.reshape(half, chans * seq_count * width, LANES)  3.2 us
    reshape x4, local copies, waits for them, and re-layouts, to_ncm(): return block.reshape(rows // LANES, LANES, width).transpose(0, 2, 1)  2.87 us

profile of v10, /device:TPU:1, one launch (start us, length us, event | category | flops | bytes accessed | tf_op | source)
XLA Modules:
  0.0 120.8 jit_solution(9433945673386317327)
XLA Ops:
  0.0 0.9 fusion.20
  0.9 1.2 convert_element_type.12
  2.3 1.2 %copy.18 = bf16[3,128,512]{1,2,0:T(8,128)(2,1)S(1)} copy(bf16[3,128,512]{2,1,0:T(8,128)(2,1)} %bitcast.89) | data formatting | bytes 786432 | tf_op jit(solution)/shard_map/reshape | solution.py:269
  3.6 1.2 %copy.19 = bf16[3,128,512]{1,2,0:T(8,128)(2,1)S(1)} copy(bf16[3,128,512]{2,1,0:T(8,128)(2,1)} %bitcast.90) | data formatting | bytes 786432 | tf_op jit(solution)/shard_map/reshape | solution.py:269
  5.0 1.4 %pad_maximum_fusion.2.source = bf16[4,3,512,128]{3,2,1,0:T(8,128)(2,1)} fusion(bf16[1,3,512,128]{3,2,1,0:T(8,128)(2,1)S(1)} %bitcast.83, bf16[1,3,512,128]{3,2,1,0:T(8,128)(2,1)S(1)} %bitcast.86, bf16[1,3,512,128]{3,2,1,0:T(8,128)(2,1)S(1)} %bitcast.85, bf16[1,3,512,128]{3,2,1,0:T(8,128)(2,1)S(1)} %bitcast.84), kind=kLoop, calls=%fused_computation.12 | loop fusion | flops 2359296 | bytes 3145728 | tf_op jit(solution)/shard_map/stack | solution.py:280
  6.4 46.1 %shard_map.127 = bf16[4,96,16,128]{3,2,1,0:T(8,128)(2,1)} custom-call(bf16[4,3,512,128]{3,2,1,0:T(8,128)(2,1)} %pad_maximum_fusion.2.source), custom_call_target="tpu_custom_call" | custom-call | tf_op jit(solution)/shard_map/pallas_call | solution.py:68
  52.6 1.7 %convert_element_type.13 = f32[4,96,16,128]{3,2,1,0:T(8,128)S(1)} convert(bf16[4,96,16,128]{3,2,1,0:T(8,128)(2,1)} %shard_map.127) | non-fusion elementwise | flops 786432 | bytes 4718592 | tf_op jit(solution)/shard_map/convert_element_type | solution.py:285
  54.4 0.5 pad_slice_fusion
  54.9 0.5 pad_slice_fusion.1
  55.7 0.9 fusion.16
  56.9 0.7 copy-done.5
  57.6 3.1 %fusion.8 = f32[384,32,128]{2,0,1:T(8,128)S(1)} fusion(f32[384,96,1]{0,1,2:T(8,128)S(1)} %copy-done.5, f32[96,32,128]{2,1,0:T(8,128)S(1)} %pad_maximum_fusion.3), kind=kOutput, calls=%fused_computation.14 | convolution fusion | flops 905969664 | bytes 8011776 | tf_op jit(solution)/shard_map/kn,ncm->kcm/dot_general | solution.py:196
  60.6 1.3 %multiply_subtract_fusion = (f32[192,32,128]{2,0,1:T(8,128)S(1)}, f32[192,32,128]{2,0,1:T(8,128)S(1)}) fusion(f32[384,32,128]{2,0,1:T(8,128)S(1)} %fusion.8, f32[192,128]{1,0:T(8,128)S(1)} %copy-done.6, f32[192,128]{1,0:T(8,128)S(1)} %copy-done), kind=kLoop, calls=%fused_computation.11 | loop fusion | flops 4718592 | bytes 12779520 | tf_op jit(solution)/shard_map/sub | solution.py:228
  61.9 0.5 pad_maximum_fusion
  62.9 6.0 %fusion = f32[192,32,256]{2,1,0:T(8,128)S(1)} fusion(f32[256,256,1]{1,0,2:T(8,128)S(1)} %copy-done.3, f32[192,32,256]{2,0,1:T(8,128)S(1)} %pad_maximum_fusion), kind=kOutput, calls=%fused_computation.1 | convolution fusion | flops 2415919104 | bytes 12845056 | tf_op jit(solution)/shard_map/kcm,mj->kcj/dot_general | solution.py:196
  69.3 0.5 copy-done.2
  69.8 1.4 %fusion.2 = f32[192,16,256]{2,1,0:T(8,128)S(1)} fusion(f32[256,256,1]{1,0,2:T(8,128)S(1)} %copy-done.2, f32[192,16,128]{2,1,0:T(8,128)S(1)} %get-tuple-element.8, f32[192,16,128]{2,1,0:T(8,128)S(1)} %get-tuple-element.7), kind=kOutput, calls=%fused_computation.3 | convolution fusion | flops 1208745984 | bytes 6553600 | tf_op jit(solution)/shard_map/kcj,jm->kcm/dot_general | solution.py:196
  71.9 0.7 copy-done.4
  72.6 2.0 %fusion.6 = f32[96,16,128]{2,0,1:T(8,128)S(1)} fusion(f32[96,384,1]{1,0,2:T(8,128)S(1)} %copy-done.4, f32[384,16,128]{2,1,0:T(8,128)S(1)} %pad_maximum_fusion.1), kind=kOutput, calls=%fused_computation.8 | convolution fusion | flops 452984832 | bytes 4079616 | tf_op jit(solution)/shard_map/nk,kcm->ncm/dot_general | solution.py:196
  74.6 0.8 dynamic_slice.7
  75.9 1.7 %fusion.13 = bf16[96,16,128]{2,1,0:T(8,128)(2,1)} fusion(f32[96,16,127]{2,1,0:T(8,128)S(1)} %bitcast.80, f32[96,16,1]{2,1,0:T(8,128)S(1)} %pad_slice_fusion.5, f32[96,16,126]{2,1,0:T(8,128)S(1)} %bitcast.81, f32[96,16,2]{2,1,0:T(8,128)S(1)} %pad_slice_fusion.4, f32[96,16,128]{2,0,1:T(8,128)S(1)} %fusion.6, f32[96,16,128]{2,1,0:T(8,128)S(1)} %fusion.16, ...), kind=kLoop, calls=%fused_computation.29 | loop fusion | flops 2162688 | bytes 4325632 | tf_op jit(solution)/shard_map/convert_element_type | solution.py:290
  77.6 35.2 %shard_map.128 = bf16[3,8,32,16,128]{4,3,2,1,0:T(8,128)(2,1)} custom-call(bf16[32,3,16,128]{3,2,1,0:T(8,128)(2,1)} %bitcast.88), custom_call_target="tpu_custom_call" | custom-call | tf_op jit(solution)/shard_map/pallas_call | solution.py:176
  112.8 3.2 %copy.26 = bf16[3,4096,128]{1,2,0:T(8,128)(2,1)S(1)} copy(bf16[3,4096,128]{2,1,0:T(8,128)(2,1)} %bitcast.75) | data formatting | bytes 6291456 | tf_op jit(solution)/shard_map/reshape | solution.py:293
  116.0 4.8 %convolution_convert_fusion = bf16[384,512]{1,0:T(8,128)(2,1)} fusion(bf16[384,4096]{1,0:T(8,128)(2,1)S(1)} %bitcast.82, bf16[4096,512]{1,0:T(8,128)(2,1)} %param.19), kind=kOutput, calls=%fused_computation.20 | convolution fusion | flops 1610809344 | bytes 7733248 | tf_op jit(solution)/shard_map/ncm,co->nmo/dot_general | solution.py:294
  (23 shorter events, 3.0 us)
Async XLA Ops:
  0.0 4.8 %copy-start.1 = (bf16[384,512]{1,0:T(8,128)(2,1)S(1)}, bf16[384,512]{1,0:T(8,128)(2,1)}, u32[]{:S(2)}) copy-start(bf16[384,512]{1,0:T(8,128)(2,1)} %param.15) | copy-start | bytes 1179652
  56.6 0.9 copy-start.5
  57.5 3.1 %copy-start = (f32[192,128]{1,0:T(8,128)S(1)}, f32[192,128]{1,0:T(8,128)}, u32[]{:S(2)}) copy-start(f32[192,128]{1,0:T(8,128)} %constant.38) | copy-start | bytes 294916
  57.6 3.1 %copy-start.6 = (f32[192,128]{1,0:T(8,128)S(1)}, f32[192,128]{1,0:T(8,128)}, u32[]{:S(2)}) copy-start(f32[192,128]{1,0:T(8,128)} %constant.40) | copy-start | bytes 294916
  61.9 1.0 copy-start.3
  68.9 1.0 copy-start.2
  69.8 1.5 %copy-start.7 = (f32[192,128]{1,0:T(8,128)S(1)}, f32[192,128]{1,0:T(8,128)}, u32[]{:S(2)}) copy-start(f32[192,128]{1,0:T(8,128)} %constant.41) | copy-start | bytes 294916
  71.7 0.9 copy-start.4

commit v11 on v10

--- a/solution.py
+++ b/solution.py
@@ -11,6 +11,29 @@
 high = lax.Precision.HIGH
 LANES = 128
 MESH = pl.DeviceIdType.MESH
+
+
+def peer_offsets(group, inner=8):
+    if group % inner:
+        inner = group
+    outer = group // inner
+    dist = lambda d, n: min(d, n - d)
+    seen, order = set(), []
+    cands = [(dx, dz) for dx in range(outer) for dz in range(inner) if dx or dz]
+    cands.sort(key=lambda o: (-(dist(o[0], outer) + dist(o[1], inner)), o))
+    for dx, dz in cands:
+        for off in ((dx, dz), ((outer - dx) % outer, (inner - dz) % inner)):
+            if off not in seen:
+                seen.add(off)
+                order.append(off)
+    return inner, order
+
+
+def shifted_peer(me, off, inner, group, sign):
+    outer = group // inner
+    x, z = me // inner, lax.rem(me, inner)
+    dx, dz = off
+    return lax.rem(x + sign * dx + outer, outer) * inner + lax.rem(z + sign * dz + inner, inner)
 
 
 def exchange_kernel(group, source, target, send_sem, recv_sem, local_sem):
@@ -33,9 +56,10 @@
     src, dst = piece(source, me, me)
     local = pltpu.make_async_copy(src, dst, local_sem.at[0])
     local.start()
+    inner, offsets = peer_offsets(group)
     sent = []
-    for step in range(1, group):
-        peer = lax.rem(me + step, group)
+    for step, off in enumerate(offsets, start=1):
+        peer = shifted_peer(me, off, inner, group, 1)
         src, dst = piece(source, peer, me)
         cp = pltpu.make_async_remote_copy(
             src_ref=src,
@@ -50,8 +74,8 @@
     local.wait()
     for cp in sent:
         cp.wait_send()
-    for step in range(1, group):
-        origin = lax.rem(me + group - step, group)
+    for step, off in enumerate(offsets, start=1):
+        origin = shifted_peer(me, off, inner, group, -1)
         src, dst = piece(source, me, origin)
         pltpu.make_async_remote_copy(
             src_ref=src,
@@ -103,6 +127,7 @@
             device_id_type=MESH,
         )
 
+    inner, offsets = peer_offsets(group)
     sent = []
     locals_ = []
     for part in range(half):
@@ -111,8 +136,8 @@
         )
         cp.start()
         locals_.append(cp)
-        for step in range(1, group):
-            peer = lax.rem(me + step, group)
+        for step, off in enumerate(offsets, start=1):
+            peer = shifted_peer(me, off, inner, group, 1)
             cp = pltpu.make_async_remote_copy(
                 src_ref=source.at[peer, part],
                 dst_ref=target.at[part, ch, me],
@@ -126,8 +151,8 @@
     passed = []
     for part in range(half):
         locals_[part].wait()
-        for step in range(1, group):
-            origin = lax.rem(me + group - step, group)
+        for step, off in enumerate(offsets, start=1):
+            origin = shifted_peer(me, off, inner, group, -1)
             pltpu.make_async_remote_copy(
                 src_ref=source.at[origin, part],
                 dst_ref=target.at[part, ch, origin],

time: 121 us -> 121 us (level)
  no operation moved by 1% of the time
where the time goes in v11:
time: 121 us; the launch traced here: 120 us
  Pallas kernels  80.9 us (67%)
  matrix products  17.3 us (14%)
  local copies, waits for them, and re-layouts  12.1 us (10%)
  other arithmetic  9.8 us (8%)
    pallas_call x1, Pallas kernels, exchange(): pl.pallas_call(functools.partial(exchange_kernel, group), out_shape=jax.S...  46.3 us
    pallas_call x1, Pallas kernels, return_and_gather(): pl.pallas_call(functools.partial(return_kernel, group, chans), out_shape=...  34.6 us
    dot_general x4, matrix products, contract(): jnp.einsum(pattern, first_op, second_op, precision=high, preferred_elemen...  12.5 us
    dot_general x1, matrix products, on_device(): jnp.einsum('ncm,co->nmo', gathered, out_weight, preferred_element_type=jn...  4.78 us
    reshape x1, local copies, waits for them, and re-layouts, on_device(): gathered = gathered.reshape(half, chans * seq_count * width, LANES)  3.2 us
    reshape x4, local copies, waits for them, and re-layouts, to_ncm(): return block.reshape(rows // LANES, LANES, width).transpose(0, 2, 1)  2.87 us

profile of v11, /device:TPU:1, one launch (start us, length us, event | category | flops | bytes accessed | tf_op | source)
XLA Modules:
  0.0 120.4 jit_solution(12411536940192585271)
XLA Ops:
  0.0 0.9 fusion.20
  0.9 1.2 convert_element_type.12
  2.3 1.2 %copy.18 = bf16[3,128,512]{1,2,0:T(8,128)(2,1)S(1)} copy(bf16[3,128,512]{2,1,0:T(8,128)(2,1)} %bitcast.89) | data formatting | bytes 786432 | tf_op jit(solution)/shard_map/reshape | solution.py:294
  3.6 1.2 %copy.19 = bf16[3,128,512]{1,2,0:T(8,128)(2,1)S(1)} copy(bf16[3,128,512]{2,1,0:T(8,128)(2,1)} %bitcast.90) | data formatting | bytes 786432 | tf_op jit(solution)/shard_map/reshape | solution.py:294
  5.0 1.4 %pad_maximum_fusion.2.source = bf16[4,3,512,128]{3,2,1,0:T(8,128)(2,1)} fusion(bf16[1,3,512,128]{3,2,1,0:T(8,128)(2,1)S(1)} %bitcast.83, bf16[1,3,512,128]{3,2,1,0:T(8,128)(2,1)S(1)} %bitcast.86, bf16[1,3,512,128]{3,2,1,0:T(8,128)(2,1)S(1)} %bitcast.85, bf16[1,3,512,128]{3,2,1,0:T(8,128)(2,1)S(1)} %bitcast.84), kind=kLoop, calls=%fused_computation.12 | loop fusion | flops 2359296 | bytes 3145728 | tf_op jit(solution)/shard_map/stack | solution.py:305
  6.4 46.3 %shard_map.127 = bf16[4,96,16,128]{3,2,1,0:T(8,128)(2,1)} custom-call(bf16[4,3,512,128]{3,2,1,0:T(8,128)(2,1)} %pad_maximum_fusion.2.source), custom_call_target="tpu_custom_call" | custom-call | tf_op jit(solution)/shard_map/pallas_call | solution.py:92
  52.7 1.7 %convert_element_type.13 = f32[4,96,16,128]{3,2,1,0:T(8,128)S(1)} convert(bf16[4,96,16,128]{3,2,1,0:T(8,128)(2,1)} %shard_map.127) | non-fusion elementwise | flops 786432 | bytes 4718592 | tf_op jit(solution)/shard_map/convert_element_type | solution.py:310
  54.5 0.5 pad_slice_fusion
  55.1 0.5 pad_slice_fusion.1
  55.8 0.9 fusion.16
  57.0 0.7 copy-done.5
  57.7 3.1 %fusion.8 = f32[384,32,128]{2,0,1:T(8,128)S(1)} fusion(f32[384,96,1]{0,1,2:T(8,128)S(1)} %copy-done.5, f32[96,32,128]{2,1,0:T(8,128)S(1)} %pad_maximum_fusion.3), kind=kOutput, calls=%fused_computation.14 | convolution fusion | flops 905969664 | bytes 8011776 | tf_op jit(solution)/shard_map/kn,ncm->kcm/dot_general | solution.py:221
  60.8 1.3 %multiply_subtract_fusion = (f32[192,32,128]{2,0,1:T(8,128)S(1)}, f32[192,32,128]{2,0,1:T(8,128)S(1)}) fusion(f32[384,32,128]{2,0,1:T(8,128)S(1)} %fusion.8, f32[192,128]{1,0:T(8,128)S(1)} %copy-done.6, f32[192,128]{1,0:T(8,128)S(1)} %copy-done), kind=kLoop, calls=%fused_computation.11 | loop fusion | flops 4718592 | bytes 12779520 | tf_op jit(solution)/shard_map/sub | solution.py:253
  62.0 0.5 pad_maximum_fusion
  63.0 6.0 %fusion = f32[192,32,256]{2,1,0:T(8,128)S(1)} fusion(f32[256,256,1]{1,0,2:T(8,128)S(1)} %copy-done.3, f32[192,32,256]{2,0,1:T(8,128)S(1)} %pad_maximum_fusion), kind=kOutput, calls=%fused_computation.1 | convolution fusion | flops 2415919104 | bytes 12845056 | tf_op jit(solution)/shard_map/kcm,mj->kcj/dot_general | solution.py:221
  69.4 0.5 copy-done.2
  70.0 1.4 %fusion.2 = f32[192,16,256]{2,1,0:T(8,128)S(1)} fusion(f32[256,256,1]{1,0,2:T(8,128)S(1)} %copy-done.2, f32[192,16,128]{2,1,0:T(8,128)S(1)} %get-tuple-element.8, f32[192,16,128]{2,1,0:T(8,128)S(1)} %get-tuple-element.7), kind=kOutput, calls=%fused_computation.3 | convolution fusion | flops 1208745984 | bytes 6553600 | tf_op jit(solution)/shard_map/kcj,jm->kcm/dot_general | solution.py:221
  72.1 0.7 copy-done.4
  72.8 2.0 %fusion.6 = f32[96,16,128]{2,0,1:T(8,128)S(1)} fusion(f32[96,384,1]{1,0,2:T(8,128)S(1)} %copy-done.4, f32[384,16,128]{2,1,0:T(8,128)S(1)} %pad_maximum_fusion.1), kind=kOutput, calls=%fused_computation.8 | convolution fusion | flops 452984832 | bytes 4079616 | tf_op jit(solution)/shard_map/nk,kcm->ncm/dot_general | solution.py:221
  74.8 0.8 dynamic_slice.7
  76.1 1.7 %fusion.13 = bf16[96,16,128]{2,1,0:T(8,128)(2,1)} fusion(f32[96,16,127]{2,1,0:T(8,128)S(1)} %bitcast.80, f32[96,16,1]{2,1,0:T(8,128)S(1)} %pad_slice_fusion.5, f32[96,16,126]{2,1,0:T(8,128)S(1)} %bitcast.81, f32[96,16,2]{2,1,0:T(8,128)S(1)} %pad_slice_fusion.4, f32[96,16,128]{2,0,1:T(8,128)S(1)} %fusion.6, f32[96,16,128]{2,1,0:T(8,128)S(1)} %fusion.16, ...), kind=kLoop, calls=%fused_computation.29 | loop fusion | flops 2162688 | bytes 4325632 | tf_op jit(solution)/shard_map/convert_element_type | solution.py:315
  77.7 34.6 %shard_map.128 = bf16[3,8,32,16,128]{4,3,2,1,0:T(8,128)(2,1)} custom-call(bf16[32,3,16,128]{3,2,1,0:T(8,128)(2,1)} %bitcast.88), custom_call_target="tpu_custom_call" | custom-call | tf_op jit(solution)/shard_map/pallas_call | solution.py:201
  112.4 3.2 %copy.26 = bf16[3,4096,128]{1,2,0:T(8,128)(2,1)S(1)} copy(bf16[3,4096,128]{2,1,0:T(8,128)(2,1)} %bitcast.75) | data formatting | bytes 6291456 | tf_op jit(solution)/shard_map/reshape | solution.py:318
  115.6 4.8 %convolution_convert_fusion = bf16[384,512]{1,0:T(8,128)(2,1)} fusion(bf16[384,4096]{1,0:T(8,128)(2,1)S(1)} %bitcast.82, bf16[4096,512]{1,0:T(8,128)(2,1)} %param.19), kind=kOutput, calls=%fused_computation.20 | convolution fusion | flops 1610809344 | bytes 7733248 | tf_op jit(solution)/shard_map/ncm,co->nmo/dot_general | solution.py:319
  (23 shorter events, 3.0 us)
Async XLA Ops:
  0.0 4.8 %copy-start.1 = (bf16[384,512]{1,0:T(8,128)(2,1)S(1)}, bf16[384,512]{1,0:T(8,128)(2,1)}, u32[]{:S(2)}) copy-start(bf16[384,512]{1,0:T(8,128)(2,1)} %param.15) | copy-start | bytes 1179652
  56.8 0.9 copy-start.5
  57.7 3.1 %copy-start = (f32[192,128]{1,0:T(8,128)S(1)}, f32[192,128]{1,0:T(8,128)}, u32[]{:S(2)}) copy-start(f32[192,128]{1,0:T(8,128)} %constant.38) | copy-start | bytes 294916
  57.7 3.1 %copy-start.6 = (f32[192,128]{1,0:T(8,128)S(1)}, f32[192,128]{1,0:T(8,128)}, u32[]{:S(2)}) copy-start(f32[192,128]{1,0:T(8,128)} %constant.40) | copy-start | bytes 294916
  62.0 1.0 copy-start.3
  69.0 1.0 copy-start.2
  70.0 1.5 %copy-start.7 = (f32[192,128]{1,0:T(8,128)S(1)}, f32[192,128]{1,0:T(8,128)}, u32[]{:S(2)}) copy-start(f32[192,128]{1,0:T(8,128)} %constant.41) | copy-start | bytes 294916
  71.8 0.9 copy-start.4

commit v12 on v11

--- a/solution.py
+++ b/solution.py
@@ -317,9 +317,9 @@
     gathered = return_and_gather(mixed.reshape(seq_count, half, width, LANES), seq_count, chans, 1)
     gathered = gathered.reshape(half, chans * seq_count * width, LANES)
     summed = jnp.einsum(
-        "ncm,co->nmo", gathered, out_weight, preferred_element_type=jnp.float32
-    )
-    return summed.reshape(rows, -1).astype(jnp.bfloat16)
+        "co,ncm->nom", out_weight, gathered, preferred_element_type=jnp.float32
+    )
+    return summed.astype(jnp.bfloat16).transpose(0, 2, 1).reshape(rows, -1)
 
 
 def solution(mesh):

time: 121 us -> 118 us (0.975)
  local copies, waits for them, and re-layouts: 12.1 us -> 8.93 us
    reshape x1 -> x0, local copies, waits for them, and re-layouts: 3.2 us -> none  [on_device(): gathered = gathered.reshape(half, chans * seq_count * width, LANES)]
where the time goes in v12:
time: 118 us
  Pallas kernels  80.9 us (69%)
  matrix products  18.2 us (15%)
  other arithmetic  9.7 us (8%)
  local copies, waits for them, and re-layouts  8.93 us (8%)
    pallas_call x1, Pallas kernels, exchange(): pl.pallas_call(functools.partial(exchange_kernel, group), out_shape=jax.S...  46.3 us
    pallas_call x1, Pallas kernels, return_and_gather(): pl.pallas_call(functools.partial(return_kernel, group, chans), out_shape=...  34.7 us
    dot_general x4, matrix products, contract(): jnp.einsum(pattern, first_op, second_op, precision=high, preferred_elemen...  12.5 us
    dot_general x1, matrix products, on_device(): jnp.einsum('co,ncm->nom', out_weight, gathered, preferred_element_type=jn...  5.71 us
    reshape x4, local copies, waits for them, and re-layouts, to_ncm(): return block.reshape(rows // LANES, LANES, width).transpose(0, 2, 1)  2.87 us
    unnamed x16, local copies, waits for them, and re-layouts  2.39 us

profile of v12, /device:TPU:1, one launch (start us, length us, event | category | flops | bytes accessed | tf_op | source)
XLA Modules:
  0.0 118.0 jit_solution(12519944512302541962)
XLA Ops:
  0.0 0.9 fusion.25
  0.9 1.2 %convert_element_type.13 = bf16[384,512]{1,0:T(8,128)(2,1)S(1)} convert(f32[384,512]{1,0:T(8,128)} %param.17) | non-fusion elementwise | flops 196608 | bytes 1179648 | tf_op jit(solution)/shard_map/convert_element_type | solution.py:304
  2.3 1.2 %copy.19 = bf16[3,128,512]{1,2,0:T(8,128)(2,1)S(1)} copy(bf16[3,128,512]{2,1,0:T(8,128)(2,1)} %bitcast.90) | data formatting | bytes 786432 | tf_op jit(solution)/shard_map/reshape | solution.py:294
  3.6 1.2 %copy.20 = bf16[3,128,512]{1,2,0:T(8,128)(2,1)S(1)} copy(bf16[3,128,512]{2,1,0:T(8,128)(2,1)} %bitcast.91) | data formatting | bytes 786432 | tf_op jit(solution)/shard_map/reshape | solution.py:294
  5.0 1.4 %pad_maximum_fusion.2.source = bf16[4,3,512,128]{3,2,1,0:T(8,128)(2,1)} fusion(bf16[1,3,512,128]{3,2,1,0:T(8,128)(2,1)S(1)} %bitcast.84, bf16[1,3,512,128]{3,2,1,0:T(8,128)(2,1)S(1)} %bitcast.87, bf16[1,3,512,128]{3,2,1,0:T(8,128)(2,1)S(1)} %bitcast.86, bf16[1,3,512,128]{3,2,1,0:T(8,128)(2,1)S(1)} %bitcast.85), kind=kLoop, calls=%fused_computation.14 | loop fusion | flops 2359296 | bytes 3145728 | tf_op jit(solution)/shard_map/stack | solution.py:305
  6.4 46.3 %shard_map.127 = bf16[4,96,16,128]{3,2,1,0:T(8,128)(2,1)} custom-call(bf16[4,3,512,128]{3,2,1,0:T(8,128)(2,1)} %pad_maximum_fusion.2.source), custom_call_target="tpu_custom_call" | custom-call | tf_op jit(solution)/shard_map/pallas_call | solution.py:92
  52.7 1.7 %convert_element_type.14 = f32[4,96,16,128]{3,2,1,0:T(8,128)S(1)} convert(bf16[4,96,16,128]{3,2,1,0:T(8,128)(2,1)} %shard_map.127) | non-fusion elementwise | flops 786432 | bytes 4718592 | tf_op jit(solution)/shard_map/convert_element_type | solution.py:310
  54.5 0.5 pad_slice_fusion
  55.1 0.5 pad_slice_fusion.1
  55.8 0.9 fusion.21
  57.0 0.7 copy-done.5
  57.6 3.1 %fusion.10 = f32[384,32,128]{2,0,1:T(8,128)S(1)} fusion(f32[384,96,1]{0,1,2:T(8,128)S(1)} %copy-done.5, f32[96,32,128]{2,1,0:T(8,128)S(1)} %pad_maximum_fusion.3), kind=kOutput, calls=%fused_computation.16 | convolution fusion | flops 905969664 | bytes 8011776 | tf_op jit(solution)/shard_map/kn,ncm->kcm/dot_general | solution.py:221
  60.7 1.3 %multiply_subtract_fusion = (f32[192,32,128]{2,0,1:T(8,128)S(1)}, f32[192,32,128]{2,0,1:T(8,128)S(1)}) fusion(f32[384,32,128]{2,0,1:T(8,128)S(1)} %fusion.10, f32[192,128]{1,0:T(8,128)S(1)} %copy-done.6, f32[192,128]{1,0:T(8,128)S(1)} %copy-done), kind=kLoop, calls=%fused_computation.13 | loop fusion | flops 4718592 | bytes 12779520 | tf_op jit(solution)/shard_map/sub | solution.py:253
  62.0 0.5 pad_maximum_fusion
  62.5 0.5 copy-done.3
  63.0 6.0 %fusion = f32[192,32,256]{2,1,0:T(8,128)S(1)} fusion(f32[256,256,1]{1,0,2:T(8,128)S(1)} %copy-done.3, f32[192,32,256]{2,0,1:T(8,128)S(1)} %pad_maximum_fusion), kind=kOutput, calls=%fused_computation.1 | convolution fusion | flops 2415919104 | bytes 12845056 | tf_op jit(solution)/shard_map/kcm,mj->kcj/dot_general | solution.py:221
  69.4 0.5 copy-done.2
  70.0 1.4 %fusion.4 = f32[192,16,256]{2,1,0:T(8,128)S(1)} fusion(f32[256,256,1]{1,0,2:T(8,128)S(1)} %copy-done.2, f32[192,16,128]{2,1,0:T(8,128)S(1)} %get-tuple-element.8, f32[192,16,128]{2,1,0:T(8,128)S(1)} %get-tuple-element.7), kind=kOutput, calls=%fused_computation.5 | convolution fusion | flops 1208745984 | bytes 6553600 | tf_op jit(solution)/shard_map/kcj,jm->kcm/dot_general | solution.py:221
  72.0 0.7 copy-done.4
  72.7 2.0 %fusion.8 = f32[96,16,128]{2,0,1:T(8,128)S(1)} fusion(f32[96,384,1]{1,0,2:T(8,128)S(1)} %copy-done.4, f32[384,16,128]{2,1,0:T(8,128)S(1)} %pad_maximum_fusion.1), kind=kOutput, calls=%fused_computation.10 | convolution fusion | flops 452984832 | bytes 4079616 | tf_op jit(solution)/shard_map/nk,kcm->ncm/dot_general | solution.py:221
  74.7 0.8 dynamic_slice.7
  76.0 1.6 %fusion.18 = bf16[96,16,128]{2,1,0:T(8,128)(2,1)} fusion(f32[96,16,127]{2,1,0:T(8,128)S(1)} %bitcast.82, f32[96,16,1]{2,1,0:T(8,128)S(1)} %pad_slice_fusion.5, f32[96,16,126]{2,1,0:T(8,128)S(1)} %bitcast.83, f32[96,16,2]{2,1,0:T(8,128)S(1)} %pad_slice_fusion.4, f32[96,16,128]{2,0,1:T(8,128)S(1)} %fusion.8, f32[96,16,128]{2,1,0:T(8,128)S(1)} %fusion.21, ...), kind=kLoop, calls=%fused_computation.31 | loop fusion | flops 2162688 | bytes 4325632 | tf_op jit(solution)/shard_map/convert_element_type | solution.py:315
  77.6 34.7 %shard_map.128 = bf16[3,8,32,16,128]{4,3,2,1,0:T(8,128)(2,1)} custom-call(bf16[32,3,16,128]{3,2,1,0:T(8,128)(2,1)} %bitcast.89), custom_call_target="tpu_custom_call" | custom-call | tf_op jit(solution)/shard_map/pallas_call | solution.py:201
  112.3 5.7 %fusion.12 = bf16[3,128,512]{2,1,0:T(8,128)(2,1)} fusion(bf16[3,4096,128]{2,1,0:T(8,128)(2,1)} %bitcast.77, bf16[4096,512]{1,0:T(8,128)(2,1)} %param.19), kind=kOutput, calls=%fused_computation.22 | convolution fusion | flops 1610809344 | bytes 7733248 | tf_op jit(solution)/shard_map/co,ncm->nom/dot_general | solution.py:319
  (22 shorter events, 2.6 us)
Async XLA Ops:
  0.0 4.8 %copy-start.1 = (bf16[384,512]{1,0:T(8,128)(2,1)S(1)}, bf16[384,512]{1,0:T(8,128)(2,1)}, u32[]{:S(2)}) copy-start(bf16[384,512]{1,0:T(8,128)(2,1)} %param.15) | copy-start | bytes 1179652
  56.7 0.9 copy-start.5
  57.6 3.1 %copy-start = (f32[192,128]{1,0:T(8,128)S(1)}, f32[192,128]{1,0:T(8,128)}, u32[]{:S(2)}) copy-start(f32[192,128]{1,0:T(8,128)} %constant.38) | copy-start | bytes 294916
  57.6 3.1 %copy-start.6 = (f32[192,128]{1,0:T(8,128)S(1)}, f32[192,128]{1,0:T(8,128)}, u32[]{:S(2)}) copy-start(f32[192,128]{1,0:T(8,128)} %constant.40) | copy-start | bytes 294916
  62.0 1.0 copy-start.3
  69.0 1.0 copy-start.2
  70.0 1.4 %copy-start.7 = (f32[192,128]{1,0:T(8,128)S(1)}, f32[192,128]{1,0:T(8,128)}, u32[]{:S(2)}) copy-start(f32[192,128]{1,0:T(8,128)} %constant.41) | copy-start | bytes 294916
  71.8 0.9 copy-start.4

commit v13 on v12

--- a/solution.py
+++ b/solution.py
@@ -36,10 +36,12 @@
     return lax.rem(x + sign * dx + outer, outer) * inner + lax.rem(z + sign * dz + inner, inner)
 
 
-def exchange_kernel(group, source, target, send_sem, recv_sem, local_sem):
+def exchange_kernel(group, count, *refs):
+    sources, target = refs[:count], refs[count]
+    send_sem, recv_sem, local_sem = refs[count + 1 :]
     me = lax.axis_index("seq")
     ch = lax.axis_index("ch")
-    half = source.shape[1]
+    half = sources[0].shape[0]
     width = target.shape[2]
     barrier = pltpu.get_barrier_semaphore()
     for step in range(1, group):
@@ -47,60 +49,69 @@
         pl.semaphore_signal(barrier, inc=1, device_id=(peer, ch), device_id_type=MESH)
     pl.semaphore_wait(barrier, group - 1)
 
-    def piece(ref_src, peer, origin):
+    def piece(plane, peer, origin):
         return (
-            ref_src.at[:, :, pl.ds(peer * width, width)],
-            target.at[:, pl.ds(origin * half, half)],
+            sources[plane].at[:, pl.ds(peer * width, width)],
+            target.at[plane, pl.ds(origin * half, half)],
         )
 
-    src, dst = piece(source, me, me)
-    local = pltpu.make_async_copy(src, dst, local_sem.at[0])
-    local.start()
+    locals_ = []
+    for plane in range(count):
+        src, dst = piece(plane, me, me)
+        cp = pltpu.make_async_copy(src, dst, local_sem.at[plane])
+        cp.start()
+        locals_.append(cp)
     inner, offsets = peer_offsets(group)
     sent = []
     for step, off in enumerate(offsets, start=1):
         peer = shifted_peer(me, off, inner, group, 1)
-        src, dst = piece(source, peer, me)
-        cp = pltpu.make_async_remote_copy(
-            src_ref=src,
-            dst_ref=dst,
-            send_sem=send_sem.at[step],
-            recv_sem=recv_sem.at[step],
-            device_id=(peer, ch),
-            device_id_type=MESH,
-        )
-        cp.start()
-        sent.append(cp)
-    local.wait()
+        for plane in range(count):
+            src, dst = piece(plane, peer, me)
+            cp = pltpu.make_async_remote_copy(
+                src_ref=src,
+                dst_ref=dst,
+                send_sem=send_sem.at[plane, step],
+                recv_sem=recv_sem.at[plane, step],
+                device_id=(peer, ch),
+                device_id_type=MESH,
+            )
+            cp.start()
+            sent.append(cp)
+    for cp in locals_:
+        cp.wait()
     for cp in sent:
         cp.wait_send()
     for step, off in enumerate(offsets, start=1):
         origin = shifted_peer(me, off, inner, group, -1)
-        src, dst = piece(source, me, origin)
-        pltpu.make_async_remote_copy(
-            src_ref=src,
-            dst_ref=dst,
-            send_sem=send_sem.at[step],
-            recv_sem=recv_sem.at[step],
-            device_id=(origin, ch),
-            device_id_type=MESH,
-        ).wait_recv()
-
-
-def exchange(stacked, group, tag):
-    planes, half, full, lanes = stacked.shape
+        for plane in range(count):
+            src, dst = piece(plane, me, origin)
+            pltpu.make_async_remote_copy(
+                src_ref=src,
+                dst_ref=dst,
+                send_sem=send_sem.at[plane, step],
+                recv_sem=recv_sem.at[plane, step],
+                device_id=(origin, ch),
+                device_id_type=MESH,
+            ).wait_recv()
+
+
+def exchange(planes, group, tag):
+    count = len(planes)
+    half, full, lanes = planes[0].shape
     return pl.pallas_call(
-        functools.partial(exchange_kernel, group),
-        out_shape=jax.ShapeDtypeStruct((planes, group * half, full // group, lanes), stacked.dtype),
-        in_specs=[pl.BlockSpec(memory_space=pl.ANY)],
+        functools.partial(exchange_kernel, group, count),
+        out_shape=jax.ShapeDtypeStruct(
+            (count, group * half, full // group, lanes), planes[0].dtype
+        ),
+        in_specs=[pl.BlockSpec(memory_space=pl.ANY)] * count,
         out_specs=pl.BlockSpec(memory_space=pl.ANY),
         scratch_shapes=[
-            pltpu.SemaphoreType.DMA((group,)),
-            pltpu.SemaphoreType.DMA((group,)),
-            pltpu.SemaphoreType.DMA((1,)),
+            pltpu.SemaphoreType.DMA((count, group)),
+            pltpu.SemaphoreType.DMA((count, group)),
+            pltpu.SemaphoreType.DMA((count,)),
         ],
         compiler_params=pltpu.CompilerParams(collective_id=tag, has_side_effects=True),
-    )(stacked)
+    )(*planes)
 
 
 def return_kernel(group, chans, source, target, send_sem, recv_sem, pass_sem, got_sem, fwd_sem, local_sem):
@@ -301,9 +312,9 @@
     width = out_gate.shape[1] // seq_count
     half = rows // LANES
 
-    planes = [out_gate, in_gate, values, long_filter.astype(jnp.bfloat16)]
-    stacked = jnp.stack([to_ncm(plane) for plane in planes])
-    spread = exchange(stacked, seq_count, 0)
+    planes = [to_ncm(out_gate), to_ncm(in_gate), to_ncm(values)]
+    planes.append(to_ncm(long_filter).astype(jnp.bfloat16))
+    spread = exchange(planes, seq_count, 0)
     start = seq_index * width
     taps = lax.dynamic_slice_in_dim(short_filter, start, width, axis=2)
     gain = lax.dynamic_slice_in_dim(skip_gain, start, width, axis=0)

time: 118 us -> 121 us (1.025)
  local copies, waits for them, and re-layouts: 8.93 us -> 11.7 us
  Pallas kernels: 80.9 us -> 82.7 us
  other arithmetic: 9.7 us -> 8.34 us
    reshape x4 -> x3, local copies, waits for them, and re-layouts: 2.87 us -> 4.74 us  [to_ncm(): return block.reshape(rows // LANES, LANES, width).transpose(0, 2, 1)]
    pallas_call x1, Pallas kernels: 46.3 us -> 48 us  [exchange(): pl.pallas_call(functools.partial(exchange_kernel, group, count), out_shap...]
    another operation x1 -> x0, other arithmetic: 1.37 us -> none  [on_device(): stacked = jnp.stack([to_ncm(plane) for plane in planes])]
where the time goes in v13:
time: 121 us
  Pallas kernels  82.7 us (68%)
  matrix products  18.2 us (15%)
  local copies, waits for them, and re-layouts  11.7 us (10%)
  other arithmetic  8.34 us (7%)
    pallas_call x1, Pallas kernels, exchange(): pl.pallas_call(functools.partial(exchange_kernel, group, count), out_shap...  48 us
    pallas_call x1, Pallas kernels, return_and_gather(): pl.pallas_call(functools.partial(return_kernel, group, chans), out_shape=...  34.7 us
    dot_general x4, matrix products, contract(): jnp.einsum(pattern, first_op, second_op, precision=high, preferred_elemen...  12.5 us
    dot_general x1, matrix products, on_device(): jnp.einsum('co,ncm->nom', out_weight, gathered, preferred_element_type=jn...  5.71 us
    reshape x3, local copies, waits for them, and re-layouts, to_ncm(): return block.reshape(rows // LANES, LANES, width).transpose(0, 2, 1)  4.74 us

profile of v13, /device:TPU:1, one launch (start us, length us, event | category | flops | bytes accessed | tf_op | source)
XLA Modules:
  0.0 121.1 jit_solution(17775479956498529806)
XLA Ops:
  0.0 0.9 fusion.25
  0.9 1.2 convert_element_type.17
  2.1 0.9 copy.22
  3.0 1.9 %copy.19 = bf16[3,128,512]{1,2,0:T(8,128)(2,1)} copy(bf16[3,128,512]{2,1,0:T(8,128)(2,1)} %bitcast.82) | data formatting | bytes 786432 | tf_op jit(solution)/shard_map/reshape | solution.py:305
  4.9 1.9 %copy.20 = bf16[3,128,512]{1,2,0:T(8,128)(2,1)} copy(bf16[3,128,512]{2,1,0:T(8,128)(2,1)} %bitcast.83) | data formatting | bytes 786432 | tf_op jit(solution)/shard_map/reshape | solution.py:305
  6.9 0.9 copy.21
  7.8 48.0 %shard_map.127 = bf16[4,96,16,128]{3,2,1,0:T(8,128)(2,1)} custom-call(bf16[3,512,128]{2,1,0:T(8,128)(2,1)} %bitcast.77, bf16[3,512,128]{2,1,0:T(8,128)(2,1)} %bitcast.78, bf16[3,512,128]{2,1,0:T(8,128)(2,1)} %bitcast.79, bf16[3,512,128]{2,1,0:T(8,128)(2,1)} %bitcast.76), custom_call_target="tpu_custom_call" | custom-call | tf_op jit(solution)/shard_map/pallas_call | solution.py:101
  55.8 1.7 %convert_element_type.20 = f32[4,96,16,128]{3,2,1,0:T(8,128)S(1)} convert(bf16[4,96,16,128]{3,2,1,0:T(8,128)(2,1)} %shard_map.127) | non-fusion elementwise | flops 786432 | bytes 4718592 | tf_op jit(solution)/shard_map/convert_element_type | solution.py:321
  57.7 0.5 pad_slice_fusion
  58.2 0.5 pad_slice_fusion.1
  59.0 0.9 fusion.21
  60.1 0.7 copy-done.5
  60.8 3.1 %fusion.10 = f32[384,32,128]{2,0,1:T(8,128)S(1)} fusion(f32[384,96,1]{0,1,2:T(8,128)S(1)} %copy-done.5, f32[96,32,128]{2,1,0:T(8,128)S(1)} %pad_maximum_fusion.2), kind=kOutput, calls=%fused_computation.15 | convolution fusion | flops 905969664 | bytes 8011776 | tf_op jit(solution)/shard_map/kn,ncm->kcm/dot_general | solution.py:232
  63.9 1.3 %multiply_subtract_fusion = (f32[192,32,128]{2,0,1:T(8,128)S(1)}, f32[192,32,128]{2,0,1:T(8,128)S(1)}) fusion(f32[384,32,128]{2,0,1:T(8,128)S(1)} %fusion.10, f32[192,128]{1,0:T(8,128)S(1)} %copy-done.6, f32[192,128]{1,0:T(8,128)S(1)} %copy-done), kind=kLoop, calls=%fused_computation.13 | loop fusion | flops 4718592 | bytes 12779520 | tf_op jit(solution)/shard_map/sub | solution.py:264
  65.2 0.5 pad_maximum_fusion
  66.1 6.0 %fusion = f32[192,32,256]{2,1,0:T(8,128)S(1)} fusion(f32[256,256,1]{1,0,2:T(8,128)S(1)} %copy-done.3, f32[192,32,256]{2,0,1:T(8,128)S(1)} %pad_maximum_fusion), kind=kOutput, calls=%fused_computation.1 | convolution fusion | flops 2415919104 | bytes 12845056 | tf_op jit(solution)/shard_map/kcm,mj->kcj/dot_general | solution.py:232
  72.6 0.5 copy-done.2
  73.1 1.4 %fusion.4 = f32[192,16,256]{2,1,0:T(8,128)S(1)} fusion(f32[256,256,1]{1,0,2:T(8,128)S(1)} %copy-done.2, f32[192,16,128]{2,1,0:T(8,128)S(1)} %get-tuple-element.8, f32[192,16,128]{2,1,0:T(8,128)S(1)} %get-tuple-element.7), kind=kOutput, calls=%fused_computation.5 | convolution fusion | flops 1208745984 | bytes 6553600 | tf_op jit(solution)/shard_map/kcj,jm->kcm/dot_general | solution.py:232
  75.2 0.7 copy-done.4
  75.8 2.0 %fusion.8 = f32[96,16,128]{2,0,1:T(8,128)S(1)} fusion(f32[96,384,1]{1,0,2:T(8,128)S(1)} %copy-done.4, f32[384,16,128]{2,1,0:T(8,128)S(1)} %pad_maximum_fusion.1), kind=kOutput, calls=%fused_computation.10 | convolution fusion | flops 452984832 | bytes 4079616 | tf_op jit(solution)/shard_map/nk,kcm->ncm/dot_general | solution.py:232
  77.8 0.8 dynamic_slice.7
  79.1 1.6 %fusion.18 = bf16[96,16,128]{2,1,0:T(8,128)(2,1)} fusion(f32[96,16,127]{2,1,0:T(8,128)S(1)} %bitcast.74, f32[96,16,1]{2,1,0:T(8,128)S(1)} %pad_slice_fusion.5, f32[96,16,126]{2,1,0:T(8,128)S(1)} %bitcast.75, f32[96,16,2]{2,1,0:T(8,128)S(1)} %pad_slice_fusion.4, f32[96,16,128]{2,0,1:T(8,128)S(1)} %fusion.8, f32[96,16,128]{2,1,0:T(8,128)S(1)} %fusion.21, ...), kind=kLoop, calls=%fused_computation.30 | loop fusion | flops 2162688 | bytes 4325632 | tf_op jit(solution)/shard_map/convert_element_type | solution.py:326
  80.7 34.7 %shard_map.128 = bf16[3,8,32,16,128]{4,3,2,1,0:T(8,128)(2,1)} custom-call(bf16[32,3,16,128]{3,2,1,0:T(8,128)(2,1)} %bitcast.81), custom_call_target="tpu_custom_call" | custom-call | tf_op jit(solution)/shard_map/pallas_call | solution.py:212
  115.4 5.7 %fusion.12 = bf16[3,128,512]{2,1,0:T(8,128)(2,1)} fusion(bf16[3,4096,128]{2,1,0:T(8,128)(2,1)} %bitcast.69, bf16[4096,512]{1,0:T(8,128)(2,1)} %param.19), kind=kOutput, calls=%fused_computation.21 | convolution fusion | flops 1610809344 | bytes 7733248 | tf_op jit(solution)/shard_map/co,ncm->nom/dot_general | solution.py:330
  (21 shorter events, 2.6 us)
Async XLA Ops:
  0.0 6.9 %copy-start.1 = (bf16[384,512]{1,0:T(8,128)(2,1)S(1)}, bf16[384,512]{1,0:T(8,128)(2,1)}, u32[]{:S(2)}) copy-start(bf16[384,512]{1,0:T(8,128)(2,1)} %param.15) | copy-start | bytes 1179652
  59.9 0.9 copy-start.5
  60.8 3.1 %copy-start = (f32[192,128]{1,0:T(8,128)S(1)}, f32[192,128]{1,0:T(8,128)}, u32[]{:S(2)}) copy-start(f32[192,128]{1,0:T(8,128)} %constant.38) | copy-start | bytes 294916
  60.8 3.1 %copy-start.6 = (f32[192,128]{1,0:T(8,128)S(1)}, f32[192,128]{1,0:T(8,128)}, u32[]{:S(2)}) copy-start(f32[192,128]{1,0:T(8,128)} %constant.40) | copy-start | bytes 294916
  65.2 1.0 copy-start.3
  72.2 1.0 copy-start.2
  73.1 1.4 %copy-start.7 = (f32[192,128]{1,0:T(8,128)S(1)}, f32[192,128]{1,0:T(8,128)}, u32[]{:S(2)}) copy-start(f32[192,128]{1,0:T(8,128)} %constant.41) | copy-start | bytes 294916
  74.9 0.9 copy-start.4

commit v14 on v12

--- a/solution.py
+++ b/solution.py
@@ -307,10 +307,10 @@
     start = seq_index * width
     taps = lax.dynamic_slice_in_dim(short_filter, start, width, axis=2)
     gain = lax.dynamic_slice_in_dim(skip_gain, start, width, axis=0)
-    spread = spread.astype(jnp.float32)
-    gate_late = short_conv(spread[0], taps[0])
-    mixed_in = short_conv(spread[1], taps[1]) * short_conv(spread[2], taps[2])
-    long_out = long_conv(mixed_in, spread[3])
+    plane = lambda index: spread[index].astype(jnp.float32)
+    gate_late = short_conv(plane(0), taps[0])
+    mixed_in = short_conv(plane(1), taps[1]) * short_conv(plane(2), taps[2])
+    long_out = long_conv(mixed_in, plane(3))
     filtered = long_out + gain[None, :, None] * mixed_in
     mixed = (gate_late * filtered).astype(jnp.bfloat16)
     chans = lax.axis_size("ch")

time: 118 us -> 125 us (1.059)
  other arithmetic: 9.7 us -> 13.4 us
  local copies, waits for them, and re-layouts: 8.93 us -> 12.3 us
    slice x4 -> x6, local copies, waits for them, and re-layouts: 1.62 us -> 5.21 us  [shift_seq(): prev[:, :, lanes - distance:]]
    mul x1, other arithmetic: 0.9 us -> 3.28 us  [on_device(): mixed_in = short_conv(plane(1), taps[1]) * short_conv(plane(2), taps[2])]
    convert_element_type x1, other arithmetic: 1.68 us -> 2.98 us  [on_device(): plane = lambda index: spread[index].astype(jnp.float32)]
where the time goes in v14:
time: 125 us
  Pallas kernels  80.9 us (65%)
  matrix products  18.2 us (15%)
  other arithmetic  13.4 us (11%)
  local copies, waits for them, and re-layouts  12.3 us (10%)
    pallas_call x1, Pallas kernels, exchange(): pl.pallas_call(functools.partial(exchange_kernel, group), out_shape=jax.S...  46.3 us
    pallas_call x1, Pallas kernels, return_and_gather(): pl.pallas_call(functools.partial(return_kernel, group, chans), out_shape=...  34.7 us
    dot_general x4, matrix products, contract(): jnp.einsum(pattern, first_op, second_op, precision=high, preferred_elemen...  12.5 us
    dot_general x1, matrix products, on_device(): jnp.einsum('co,ncm->nom', out_weight, gathered, preferred_element_type=jn...  5.71 us
    slice x6, local copies, waits for them, and re-layouts, shift_seq(): prev[:, :, lanes - distance:]  5.21 us
    mul x1, other arithmetic, on_device(): mixed_in = short_conv(plane(1), taps[1]) * short_conv(plane(2), taps[2])  3.28 us
    convert_element_type x1, other arithmetic, on_device(): plane = lambda index: spread[index].astype(jnp.float32)  2.98 us
    reshape x4, local copies, waits for them, and re-layouts, to_ncm(): return block.reshape(rows // LANES, LANES, width).transpose(0, 2, 1)  2.87 us

profile of v14, /device:TPU:1, one launch (start us, length us, event | category | flops | bytes accessed | tf_op | source)
XLA Modules:
  0.0 125.1 jit_solution(16955306012305418334)
XLA Ops:
  0.0 1.2 convert_element_type.34
  1.5 1.2 copy.19
  2.7 1.2 copy.20
  4.1 1.3 %pad_maximum_fusion.2.source = bf16[4,3,512,128]{3,2,1,0:T(8,128)(2,1)} fusion(bf16[1,3,512,128]{3,2,1,0:T(8,128)(2,1)S(1)} %bitcast.86, bf16[1,3,512,128]{3,2,1,0:T(8,128)(2,1)S(1)} %bitcast.89, bf16[1,3,512,128]{3,2,1,0:T(8,128)(2,1)S(1)} %bitcast.88, bf16[1,3,512,128]{3,2,1,0:T(8,128)(2,1)S(1)} %bitcast.87), kind=kLoop, calls=%fused_computation.14 | loop fusion | flops 2359296 | bytes 3145728 | tf_op jit(solution)/shard_map/stack | solution.py:305
  5.5 46.3 %shard_map.127 = bf16[4,96,16,128]{3,2,1,0:T(8,128)(2,1)} custom-call(bf16[4,3,512,128]{3,2,1,0:T(8,128)(2,1)} %pad_maximum_fusion.2.source), custom_call_target="tpu_custom_call" | custom-call | tf_op jit(solution)/shard_map/pallas_call | solution.py:92
  51.8 3.0 %slice_convert_fusion = (f32[1,96,16,128]{3,2,1,0:T(8,128)S(1)}, f32[96,16,128]{2,1,0:T(8,128)S(1)}, f32[96,16,128]{2,1,0:T(8,128)}, f32[96,16,128]{2,1,0:T(8,12...) fusion(bf16[4,96,16,128]{3,2,1,0:T(8,128)(2,1)} %shard_map.127), kind=kLoop, calls=%fused_computation.49 | loop fusion | flops 786432 | bytes 7077888 | tf_op jit(solution)/shard_map/convert_element_type | solution.py:310
  54.9 1.2 pad_slice_fusion
  56.0 1.2 pad_slice_fusion.1
  57.2 1.2 pad_slice_fusion.2
  58.4 1.2 pad_slice_fusion.3
  59.5 0.9 fusion.28
  60.5 3.3 %fusion.21 = f32[96,16,128]{2,1,0:T(8,128)S(1)} fusion(f32[96,16,127]{2,1,0:T(8,128)} %bitcast.83, f32[96,16,1]{2,1,0:T(8,128)} %pad_slice_fusion.3, f32[96,16,126]{2,1,0:T(8,128)} %bitcast.84, f32[96,16,2]{2,1,0:T(8,128)} %pad_slice_fusion.2, f32[96,16,127]{2,1,0:T(8,128)S(1)} %bitcast.81, f32[96,16,1]{2,1,0:T(8,128)} %pad_slice_fusion.1, ...), kind=kLoop, calls=%fused_computation.32 | loop fusion | flops 3342336 | bytes 4718976 | tf_op jit(solution)/shard_map/mul | solution.py:312
  64.0 0.7 copy-done.8
  64.7 3.0 %fusion.10 = f32[384,32,128]{2,0,1:T(8,128)S(1)} fusion(f32[384,96,1]{0,1,2:T(8,128)S(1)} %copy-done.8, f32[96,32,128]{2,1,0:T(8,128)S(1)} %pad_maximum_fusion.3), kind=kOutput, calls=%fused_computation.16 | convolution fusion | flops 905969664 | bytes 8011776 | tf_op jit(solution)/shard_map/kn,ncm->kcm/dot_general | solution.py:221
  67.8 1.3 %multiply_subtract_fusion = (f32[192,32,128]{2,0,1:T(8,128)S(1)}, f32[192,32,128]{2,0,1:T(8,128)S(1)}) fusion(f32[384,32,128]{2,0,1:T(8,128)S(1)} %fusion.10, f32[192,128]{1,0:T(8,128)S(1)} %copy-done.9, f32[192,128]{1,0:T(8,128)S(1)} %copy-done.3), kind=kLoop, calls=%fused_computation.13 | loop fusion | flops 4718592 | bytes 12779520 | tf_op jit(solution)/shard_map/sub | solution.py:253
  70.0 6.1 %fusion = f32[192,32,256]{2,1,0:T(8,128)S(1)} fusion(f32[256,256,1]{1,0,2:T(8,128)S(1)} %copy-done.6, f32[192,32,256]{2,0,1:T(8,128)S(1)} %pad_maximum_fusion), kind=kOutput, calls=%fused_computation.1 | convolution fusion | flops 2415919104 | bytes 12845056 | tf_op jit(solution)/shard_map/kcm,mj->kcj/dot_general | solution.py:221
  76.5 0.5 copy-done.5
  77.1 1.4 %fusion.4 = f32[192,16,256]{2,1,0:T(8,128)S(1)} fusion(f32[256,256,1]{1,0,2:T(8,128)S(1)} %copy-done.5, f32[192,16,128]{2,1,0:T(8,128)S(1)} %get-tuple-element.8, f32[192,16,128]{2,1,0:T(8,128)S(1)} %get-tuple-element.7), kind=kOutput, calls=%fused_computation.5 | convolution fusion | flops 1208745984 | bytes 6553600 | tf_op jit(solution)/shard_map/kcj,jm->kcm/dot_general | solution.py:221
  79.1 0.7 copy-done.7
  79.8 2.0 %fusion.8 = f32[96,16,128]{2,0,1:T(8,128)S(1)} fusion(f32[96,384,1]{1,0,2:T(8,128)S(1)} %copy-done.7, f32[384,16,128]{2,1,0:T(8,128)S(1)} %pad_maximum_fusion.1), kind=kOutput, calls=%fused_computation.10 | convolution fusion | flops 452984832 | bytes 4079616 | tf_op jit(solution)/shard_map/nk,kcm->ncm/dot_general | solution.py:221
  82.4 0.8 dynamic_slice.7
  83.1 1.6 %fusion.18 = bf16[96,16,128]{2,1,0:T(8,128)(2,1)} fusion(f32[96,16,127]{2,1,0:T(8,128)S(1)} %bitcast.79, f32[96,16,1]{2,1,0:T(8,128)S(1)} %pad_slice_fusion.5, f32[96,16,126]{2,1,0:T(8,128)S(1)} %bitcast.80, f32[96,16,2]{2,1,0:T(8,128)S(1)} %pad_slice_fusion.4, f32[96,16,128]{2,0,1:T(8,128)S(1)} %fusion.8, f32[96,16,128]{2,1,0:T(8,128)S(1)} %fusion.21, ...), kind=kLoop, calls=%fused_computation.27 | loop fusion | flops 2359296 | bytes 3932416 | tf_op jit(solution)/shard_map/convert_element_type | solution.py:315
  84.7 34.7 %shard_map.128 = bf16[3,8,32,16,128]{4,3,2,1,0:T(8,128)(2,1)} custom-call(bf16[32,3,16,128]{3,2,1,0:T(8,128)(2,1)} %bitcast.85), custom_call_target="tpu_custom_call" | custom-call | tf_op jit(solution)/shard_map/pallas_call | solution.py:201
  119.4 5.7 %fusion.12 = bf16[3,128,512]{2,1,0:T(8,128)(2,1)} fusion(bf16[3,4096,128]{2,1,0:T(8,128)(2,1)} %bitcast.78, bf16[4096,512]{1,0:T(8,128)(2,1)} %param.19), kind=kOutput, calls=%fused_computation.22 | convolution fusion | flops 1610809344 | bytes 7733248 | tf_op jit(solution)/shard_map/co,ncm->nom/dot_general | solution.py:319
  (30 shorter events, 3.3 us)
Async XLA Ops:
  0.0 3.9 %copy-start.4 = (bf16[384,512]{1,0:T(8,128)(2,1)S(1)}, bf16[384,512]{1,0:T(8,128)(2,1)}, u32[]{:S(2)}) copy-start(bf16[384,512]{1,0:T(8,128)(2,1)} %param.15) | copy-start | bytes 1179652
  54.9 5.6 %copy-start = (bf16[4,96,16,128]{3,2,1,0:T(8,128)(2,1)S(1)}, bf16[4,96,16,128]{3,2,1,0:T(8,128)(2,1)}, u32[]{:S(2)}) copy-start(bf16[4,96,16,128]{3,2,1,0:T(8,128)(2,1)} %shard_map.127) | copy-start | bytes 4718596
  60.5 3.3 %copy-start.1 = (f32[96,16,128]{2,1,0:T(8,128)S(1)}, f32[96,16,128]{2,1,0:T(8,128)}, u32[]{:S(2)}) copy-start(f32[96,16,128]{2,1,0:T(8,128)} %get-tuple-element.15) | copy-start | bytes 2359300
  63.8 0.9 copy-start.8
  64.7 3.1 %copy-start.3 = (f32[192,128]{1,0:T(8,128)S(1)}, f32[192,128]{1,0:T(8,128)}, u32[]{:S(2)}) copy-start(f32[192,128]{1,0:T(8,128)} %constant.38) | copy-start | bytes 294916
  64.7 3.1 %copy-start.9 = (f32[192,128]{1,0:T(8,128)S(1)}, f32[192,128]{1,0:T(8,128)}, u32[]{:S(2)}) copy-start(f32[192,128]{1,0:T(8,128)} %constant.40) | copy-start | bytes 294916
  69.0 1.0 copy-start.6
  76.1 1.0 copy-start.5
  77.1 1.4 %copy-start.10 = (f32[192,128]{1,0:T(8,128)S(1)}, f32[192,128]{1,0:T(8,128)}, u32[]{:S(2)}) copy-start(f32[192,128]{1,0:T(8,128)} %constant.41) | copy-start | bytes 294916
  78.9 0.9 copy-start.7
  79.8 2.0 %copy-start.2 = (f32[1,96,16,128]{3,2,1,0:T(8,128)S(1)}, f32[1,96,16,128]{3,2,1,0:T(8,128)}, u32[]{:S(2)}) copy-start(f32[1,96,16,128]{3,2,1,0:T(8,128)} %get-tuple-element.17) | copy-start | bytes 2359300

commit v15 on v12

--- a/solution.py
+++ b/solution.py
@@ -227,13 +227,16 @@
     total = 2 * seq_len
     outer = total // LANES
     half = seq_len // LANES
-    k1 = np.arange(outer)[:, None]
+    keep = outer // 2 + 1
+    rows = -(-keep // 8) * 8
+    k1 = np.arange(rows)[:, None]
     a1 = 2.0 * np.pi * ((k1 * np.arange(half)[None, :]) % outer) / outer
     at = 2.0 * np.pi * ((k1 * np.arange(LANES)[None, :]) % total) / total
     m2 = np.arange(LANES)
     a2 = 2.0 * np.pi * ((m2[:, None] * m2[None, :]) % LANES) / LANES
     c1, s1 = np.cos(a1), np.sin(a1)
     c2, s2 = np.cos(a2), np.sin(a2)
+    weight = np.where((k1 == 0) | (k1 == outer // 2), 1.0, 2.0) * (k1 < keep)
     f32 = lambda v: jnp.asarray(v, jnp.float32)
     return dict(
         first=f32(np.concatenate([c1, -s1], axis=0)),
@@ -241,7 +244,7 @@
         ts=f32(np.sin(at)[:, None, :]),
         fwd2=f32(np.block([[c2, -s2], [s2, c2]])),
         inv2=f32(np.block([[c2, s2], [-s2, c2]])),
-        last=f32(np.concatenate([c1.T, -s1.T], axis=1) / total),
+        last=f32(np.concatenate([(c1 * weight).T, -(s1 * weight).T], axis=1) / total),
     )
 
 

time: 118 us -> 109 us (0.924)
  matrix products: 18.2 us -> 12.4 us
  local copies, waits for them, and re-layouts: 8.93 us -> 7.23 us
  other arithmetic: 9.7 us -> 8.4 us
    dot_general x4, matrix products: 12.5 us -> 6.67 us  [contract(): jnp.einsum(pattern, first_op, second_op, precision=high, preferred_elemen...]
    reshape x4, local copies, waits for them, and re-layouts: 2.87 us -> 0.88 us  [to_ncm(): return block.reshape(rows // LANES, LANES, width).transpose(0, 2, 1)]
    unnamed x16 -> x20, local copies, waits for them, and re-layouts: 2.39 us -> 2.68 us
where the time goes in v15:
time: 109 us
  Pallas kernels  80.9 us (74%)
  matrix products  12.4 us (11%)
  other arithmetic  8.4 us (8%)
  local copies, waits for them, and re-layouts  7.23 us (7%)
    pallas_call x1, Pallas kernels, exchange(): pl.pallas_call(functools.partial(exchange_kernel, group), out_shape=jax.S...  46.3 us
    pallas_call x1, Pallas kernels, return_and_gather(): pl.pallas_call(functools.partial(return_kernel, group, chans), out_shape=...  34.6 us
    dot_general x4, matrix products, contract(): jnp.einsum(pattern, first_op, second_op, precision=high, preferred_elemen...  6.67 us
    dot_general x1, matrix products, on_device(): jnp.einsum('co,ncm->nom', out_weight, gathered, preferred_element_type=jn...  5.71 us
    unnamed x20, local copies, waits for them, and re-layouts  2.68 us

profile of v15, /device:TPU:1, one launch (start us, length us, event | category | flops | bytes accessed | tf_op | source)
XLA Modules:
  0.0 109.2 jit_solution(4447275022694320325)
XLA Ops:
  0.0 0.9 fusion.25
  0.9 1.2 %convert_element_type.13 = bf16[384,512]{1,0:T(8,128)(2,1)S(1)} convert(f32[384,512]{1,0:T(8,128)} %param.17) | non-fusion elementwise | flops 196608 | bytes 1179648 | tf_op jit(solution)/shard_map/convert_element_type | solution.py:307
  3.1 1.4 %pad_maximum_fusion.2.source = bf16[4,3,512,128]{3,2,1,0:T(8,128)(2,1)} fusion(bf16[1,3,512,128]{3,2,1,0:T(8,128)(2,1)S(1)} %bitcast.84, bf16[1,3,512,128]{3,2,1,0:T(8,128)(2,1)S(1)} %bitcast.87, bf16[1,3,512,128]{3,2,1,0:T(8,128)(2,1)S(1)} %bitcast.86, bf16[1,3,512,128]{3,2,1,0:T(8,128)(2,1)S(1)} %bitcast.85), kind=kLoop, calls=%fused_computation.14 | loop fusion | flops 2359296 | bytes 3145728 | tf_op jit(solution)/shard_map/stack | solution.py:308
  4.5 46.3 %shard_map.127 = bf16[4,96,16,128]{3,2,1,0:T(8,128)(2,1)} custom-call(bf16[4,3,512,128]{3,2,1,0:T(8,128)(2,1)} %pad_maximum_fusion.2.source), custom_call_target="tpu_custom_call" | custom-call | tf_op jit(solution)/shard_map/pallas_call | solution.py:92
  50.8 1.7 %convert_element_type.14 = f32[4,96,16,128]{3,2,1,0:T(8,128)S(1)} convert(bf16[4,96,16,128]{3,2,1,0:T(8,128)(2,1)} %shard_map.127) | non-fusion elementwise | flops 786432 | bytes 4718592 | tf_op jit(solution)/shard_map/convert_element_type | solution.py:313
  52.6 0.5 pad_slice_fusion
  53.2 0.5 pad_slice_fusion.1
  53.9 1.0 fusion.21
  55.2 0.7 copy-done.7
  55.8 2.2 %fusion.10 = f32[208,32,128]{2,0,1:T(8,128)S(1)} fusion(f32[208,96,1]{0,1,2:T(8,128)S(1)} %copy-done.7, f32[96,32,128]{2,1,0:T(8,128)S(1)} %pad_maximum_fusion.3), kind=kOutput, calls=%fused_computation.16 | convolution fusion | flops 490733568 | bytes 5060608 | tf_op jit(solution)/shard_map/kn,ncm->kcm/dot_general | solution.py:221
  58.1 0.4 multiply_subtract_fusion
  58.5 0.4 pad_maximum_fusion
  58.9 0.5 copy-done.3
  59.4 2.3 %fusion.2 = f32[104,32,256]{2,1,0:T(8,128)S(1)} fusion(f32[256,256,1]{1,0,2:T(8,128)S(1)} %copy-done.3, f32[104,32,256]{2,0,1:T(8,128)S(1)} %pad_maximum_fusion), kind=kOutput, calls=%fused_computation.3 | convolution fusion | flops 1308622848 | bytes 7077888 | tf_op jit(solution)/shard_map/kcm,mj->kcj/dot_general | solution.py:221
  62.0 0.7 copy-done.4
  62.7 0.8 fusion.4
  63.9 0.8 copy-done.6
  64.7 1.2 %fusion.8 = f32[96,16,128]{2,0,1:T(8,128)S(1)} fusion(f32[96,208,1]{1,0,2:T(8,128)S(1)} %copy-done.6, f32[208,16,128]{2,1,0:T(8,128)S(1)} %pad_maximum_fusion.1), kind=kOutput, calls=%fused_computation.10 | convolution fusion | flops 245366784 | bytes 2570240 | tf_op jit(solution)/shard_map/nk,kcm->ncm/dot_general | solution.py:221
  65.9 0.8 dynamic_slice.7
  66.7 0.3 pad_slice_fusion.4
  67.0 0.3 pad_slice_fusion.5
  67.2 1.6 %fusion.18 = bf16[96,16,128]{2,1,0:T(8,128)(2,1)} fusion(f32[96,16,127]{2,1,0:T(8,128)S(1)} %bitcast.82, f32[96,16,1]{2,1,0:T(8,128)S(1)} %pad_slice_fusion.5, f32[96,16,126]{2,1,0:T(8,128)S(1)} %bitcast.83, f32[96,16,2]{2,1,0:T(8,128)S(1)} %pad_slice_fusion.4, f32[96,16,128]{2,0,1:T(8,128)S(1)} %fusion.8, f32[96,16,128]{2,1,0:T(8,128)S(1)} %fusion.21, ...), kind=kLoop, calls=%fused_computation.31 | loop fusion | flops 2162688 | bytes 4325632 | tf_op jit(solution)/shard_map/convert_element_type | solution.py:318
  68.8 34.6 %shard_map.128 = bf16[3,8,32,16,128]{4,3,2,1,0:T(8,128)(2,1)} custom-call(bf16[32,3,16,128]{3,2,1,0:T(8,128)(2,1)} %bitcast.89), custom_call_target="tpu_custom_call" | custom-call | tf_op jit(solution)/shard_map/pallas_call | solution.py:201
  103.4 5.7 %fusion.12 = bf16[3,128,512]{2,1,0:T(8,128)(2,1)} fusion(bf16[3,4096,128]{2,1,0:T(8,128)(2,1)} %bitcast.77, bf16[4096,512]{1,0:T(8,128)(2,1)} %param.19), kind=kOutput, calls=%fused_computation.18 | convolution fusion | flops 1610809344 | bytes 7733248 | tf_op jit(solution)/shard_map/co,ncm->nom/dot_general | solution.py:322
  (26 shorter events, 2.1 us)
Async XLA Ops:
  0.0 2.4 %copy-start = (bf16[384,512]{1,0:T(8,128)(2,1)S(1)}, bf16[384,512]{1,0:T(8,128)(2,1)}, u32[]{:S(2)}) copy-start(bf16[384,512]{1,0:T(8,128)(2,1)} %param.13) | copy-start | bytes 1179652
  0.0 2.6 %copy-start.1 = (bf16[384,512]{1,0:T(8,128)(2,1)S(1)}, bf16[384,512]{1,0:T(8,128)(2,1)}, u32[]{:S(2)}) copy-start(bf16[384,512]{1,0:T(8,128)(2,1)} %param.14) | copy-start | bytes 1179652
  0.9 1.9 %copy-start.2 = (bf16[384,512]{1,0:T(8,128)(2,1)S(1)}, bf16[384,512]{1,0:T(8,128)(2,1)}, u32[]{:S(2)}) copy-start(bf16[384,512]{1,0:T(8,128)(2,1)} %param.15) | copy-start | bytes 1179652
  54.9 0.9 copy-start.7
  55.8 2.3 %copy-start.5 = (f32[104,128]{1,0:T(8,128)S(1)}, f32[104,128]{1,0:T(8,128)}, u32[]{:S(2)}) copy-start(f32[104,128]{1,0:T(8,128)} %constant.38) | copy-start | bytes 159748
  55.8 2.3 %copy-start.9 = (f32[104,128]{1,0:T(8,128)S(1)}, f32[104,128]{1,0:T(8,128)}, u32[]{:S(2)}) copy-start(f32[104,128]{1,0:T(8,128)} %constant.40) | copy-start | bytes 159748
  58.5 1.0 copy-start.3
  61.8 1.0 copy-start.4
  62.7 0.9 copy-start.8
  63.8 0.9 copy-start.6

commit v16 on v15

--- a/solution.py
+++ b/solution.py
@@ -308,8 +308,11 @@
     stacked = jnp.stack([to_ncm(plane) for plane in planes])
     spread = exchange(stacked, seq_count, 0)
     start = seq_index * width
-    taps = lax.dynamic_slice_in_dim(short_filter, start, width, axis=2)
-    gain = lax.dynamic_slice_in_dim(skip_gain, start, width, axis=0)
+    sets, tap_count = short_filter.shape[:2]
+    params = jnp.concatenate([short_filter.reshape(sets * tap_count, -1), skip_gain[None]])
+    params = lax.dynamic_slice_in_dim(params, start, width, axis=1)
+    taps = params[: sets * tap_count].reshape(sets, tap_count, width)
+    gain = params[sets * tap_count]
     spread = spread.astype(jnp.float32)
     gate_late = short_conv(spread[0], taps[0])
     mixed_in = short_conv(spread[1], taps[1]) * short_conv(spread[2], taps[2])

time: 109 us -> 109 us (level)
  no operation moved by 1% of the time
where the time goes in v16:
time: 109 us
  Pallas kernels  80.9 us (74%)
  matrix products  12.4 us (11%)
  other arithmetic  9.14 us (8%)
  local copies, waits for them, and re-layouts  6.37 us (6%)
    pallas_call x1, Pallas kernels, exchange(): pl.pallas_call(functools.partial(exchange_kernel, group), out_shape=jax.S...  46.3 us
    pallas_call x1, Pallas kernels, return_and_gather(): pl.pallas_call(functools.partial(return_kernel, group, chans), out_shape=...  34.6 us
    dot_general x4, matrix products, contract(): jnp.einsum(pattern, first_op, second_op, precision=high, preferred_elemen...  6.67 us
    dot_general x1, matrix products, on_device(): jnp.einsum('co,ncm->nom', out_weight, gathered, preferred_element_type=jn...  5.71 us
    unnamed x20, local copies, waits for them, and re-layouts  2.68 us

profile of v16, /device:TPU:1, one launch (start us, length us, event | category | flops | bytes accessed | tf_op | source)
XLA Modules:
  0.0 109.0 jit_solution(8579065867243881445)
XLA Ops:
  0.0 0.8 reshape.50
  0.8 0.7 fusion.24
  1.6 1.2 %convert_element_type.13 = bf16[384,512]{1,0:T(8,128)(2,1)S(1)} convert(f32[384,512]{1,0:T(8,128)} %param.17) | non-fusion elementwise | flops 196608 | bytes 1179648 | tf_op jit(solution)/shard_map/convert_element_type | solution.py:307
  3.7 1.4 %pad_maximum_fusion.2.source = bf16[4,3,512,128]{3,2,1,0:T(8,128)(2,1)} fusion(bf16[1,3,512,128]{3,2,1,0:T(8,128)(2,1)S(1)} %bitcast.87, bf16[1,3,512,128]{3,2,1,0:T(8,128)(2,1)S(1)} %bitcast.88, bf16[1,3,512,128]{3,2,1,0:T(8,128)(2,1)S(1)} %bitcast.90, bf16[1,3,512,128]{3,2,1,0:T(8,128)(2,1)S(1)} %bitcast.89), kind=kLoop, calls=%fused_computation.14 | loop fusion | flops 2359296 | bytes 3145728 | tf_op jit(solution)/shard_map/stack | solution.py:308
  5.1 46.3 %shard_map.127 = bf16[4,96,16,128]{3,2,1,0:T(8,128)(2,1)} custom-call(bf16[4,3,512,128]{3,2,1,0:T(8,128)(2,1)} %pad_maximum_fusion.2.source), custom_call_target="tpu_custom_call" | custom-call | tf_op jit(solution)/shard_map/pallas_call | solution.py:92
  51.4 1.7 %convert_element_type.14 = f32[4,96,16,128]{3,2,1,0:T(8,128)S(1)} convert(bf16[4,96,16,128]{3,2,1,0:T(8,128)(2,1)} %shard_map.127) | non-fusion elementwise | flops 786432 | bytes 4718592 | tf_op jit(solution)/shard_map/convert_element_type | solution.py:316
  53.2 0.5 pad_slice_fusion
  53.8 0.5 pad_slice_fusion.1
  54.5 1.0 fusion.21
  55.8 0.7 copy-done.7
  56.5 2.2 %fusion.10 = f32[208,32,128]{2,0,1:T(8,128)S(1)} fusion(f32[208,96,1]{0,1,2:T(8,128)S(1)} %copy-done.7, f32[96,32,128]{2,1,0:T(8,128)S(1)} %pad_maximum_fusion.3), kind=kOutput, calls=%fused_computation.16 | convolution fusion | flops 490733568 | bytes 5060608 | tf_op jit(solution)/shard_map/kn,ncm->kcm/dot_general | solution.py:221
  58.7 0.4 multiply_subtract_fusion
  59.1 0.4 pad_maximum_fusion
  59.5 0.5 copy-done.3
  60.0 2.3 %fusion.2 = f32[104,32,256]{2,1,0:T(8,128)S(1)} fusion(f32[256,256,1]{1,0,2:T(8,128)S(1)} %copy-done.3, f32[104,32,256]{2,0,1:T(8,128)S(1)} %pad_maximum_fusion), kind=kOutput, calls=%fused_computation.3 | convolution fusion | flops 1308622848 | bytes 7077888 | tf_op jit(solution)/shard_map/kcm,mj->kcj/dot_general | solution.py:221
  62.6 0.7 copy-done.4
  63.3 0.8 fusion.4
  64.6 0.8 copy-done.6
  65.3 1.2 %fusion.8 = f32[96,16,128]{2,0,1:T(8,128)S(1)} fusion(f32[96,208,1]{1,0,2:T(8,128)S(1)} %copy-done.6, f32[208,16,128]{2,1,0:T(8,128)S(1)} %pad_maximum_fusion.1), kind=kOutput, calls=%fused_computation.10 | convolution fusion | flops 245366784 | bytes 2570240 | tf_op jit(solution)/shard_map/nk,kcm->ncm/dot_general | solution.py:221
  66.6 0.3 pad_slice_fusion.4
  66.8 0.3 pad_slice_fusion.5
  67.1 1.6 %fusion.18 = bf16[96,16,128]{2,1,0:T(8,128)(2,1)} fusion(f32[96,16,127]{2,1,0:T(8,128)S(1)} %bitcast.85, f32[96,16,1]{2,1,0:T(8,128)S(1)} %pad_slice_fusion.5, f32[96,16,126]{2,1,0:T(8,128)S(1)} %bitcast.86, f32[96,16,2]{2,1,0:T(8,128)S(1)} %pad_slice_fusion.4, f32[96,16,128]{2,0,1:T(8,128)S(1)} %fusion.8, f32[96,16,128]{2,1,0:T(8,128)S(1)} %fusion.21, ...), kind=kLoop, calls=%fused_computation.31 | loop fusion | flops 2162688 | bytes 4325632 | tf_op jit(solution)/shard_map/convert_element_type | solution.py:321
  68.7 34.6 %shard_map.128 = bf16[3,8,32,16,128]{4,3,2,1,0:T(8,128)(2,1)} custom-call(bf16[32,3,16,128]{3,2,1,0:T(8,128)(2,1)} %bitcast.92), custom_call_target="tpu_custom_call" | custom-call | tf_op jit(solution)/shard_map/pallas_call | solution.py:201
  103.3 5.7 %fusion.12 = bf16[3,128,512]{2,1,0:T(8,128)(2,1)} fusion(bf16[3,4096,128]{2,1,0:T(8,128)(2,1)} %bitcast.80, bf16[4096,512]{1,0:T(8,128)(2,1)} %param.19), kind=kOutput, calls=%fused_computation.18 | convolution fusion | flops 1610809344 | bytes 7733248 | tf_op jit(solution)/shard_map/co,ncm->nom/dot_general | solution.py:325
  (27 shorter events, 2.1 us)
Async XLA Ops:
  0.0 3.0 %copy-start = (bf16[384,512]{1,0:T(8,128)(2,1)S(1)}, bf16[384,512]{1,0:T(8,128)(2,1)}, u32[]{:S(2)}) copy-start(bf16[384,512]{1,0:T(8,128)(2,1)} %param.15) | copy-start | bytes 1179652
  0.0 3.3 %copy-start.1 = (bf16[384,512]{1,0:T(8,128)(2,1)S(1)}, bf16[384,512]{1,0:T(8,128)(2,1)}, u32[]{:S(2)}) copy-start(bf16[384,512]{1,0:T(8,128)(2,1)} %param.13) | copy-start | bytes 1179652
  1.6 1.9 %copy-start.2 = (bf16[384,512]{1,0:T(8,128)(2,1)S(1)}, bf16[384,512]{1,0:T(8,128)(2,1)}, u32[]{:S(2)}) copy-start(bf16[384,512]{1,0:T(8,128)(2,1)} %param.14) | copy-start | bytes 1179652
  55.5 0.9 copy-start.7
  56.4 2.3 %copy-start.5 = (f32[104,128]{1,0:T(8,128)S(1)}, f32[104,128]{1,0:T(8,128)}, u32[]{:S(2)}) copy-start(f32[104,128]{1,0:T(8,128)} %constant.38) | copy-start | bytes 159748
  56.4 2.3 %copy-start.9 = (f32[104,128]{1,0:T(8,128)S(1)}, f32[104,128]{1,0:T(8,128)}, u32[]{:S(2)}) copy-start(f32[104,128]{1,0:T(8,128)} %constant.40) | copy-start | bytes 159748
  59.1 1.0 copy-start.3
  62.4 1.0 copy-start.4
  63.3 0.9 copy-start.8
  64.4 0.9 copy-start.6

commit v17 on v16

--- a/solution.py
+++ b/solution.py
@@ -313,10 +313,10 @@
     params = lax.dynamic_slice_in_dim(params, start, width, axis=1)
     taps = params[: sets * tap_count].reshape(sets, tap_count, width)
     gain = params[sets * tap_count]
-    spread = spread.astype(jnp.float32)
-    gate_late = short_conv(spread[0], taps[0])
-    mixed_in = short_conv(spread[1], taps[1]) * short_conv(spread[2], taps[2])
-    long_out = long_conv(mixed_in, spread[3])
+    wide = spread[1:].astype(jnp.float32)
+    mixed_in = short_conv(wide[0], taps[1]) * short_conv(wide[1], taps[2])
+    long_out = long_conv(mixed_in, wide[2])
+    gate_late = short_conv(spread[0].astype(jnp.float32), taps[0])
     filtered = long_out + gain[None, :, None] * mixed_in
     mixed = (gate_late * filtered).astype(jnp.bfloat16)
     chans = lax.axis_size("ch")

time: 109 us -> 109 us (level)
    unnamed x20 -> x22, local copies, waits for them, and re-layouts: 2.68 us -> 3.21 us
where the time goes in v17:
time: 109 us
  Pallas kernels  80.9 us (74%)
  matrix products  12.2 us (11%)
  other arithmetic  8.96 us (8%)
  local copies, waits for them, and re-layouts  6.85 us (6%)
    pallas_call x1, Pallas kernels, exchange(): pl.pallas_call(functools.partial(exchange_kernel, group), out_shape=jax.S...  46.3 us
    pallas_call x1, Pallas kernels, return_and_gather(): pl.pallas_call(functools.partial(return_kernel, group, chans), out_shape=...  34.7 us
    dot_general x4, matrix products, contract(): jnp.einsum(pattern, first_op, second_op, precision=high, preferred_elemen...  6.48 us
    dot_general x1, matrix products, on_device(): jnp.einsum('co,ncm->nom', out_weight, gathered, preferred_element_type=jn...  5.71 us
    unnamed x22, local copies, waits for them, and re-layouts  3.21 us

profile of v17, /device:TPU:1, one launch (start us, length us, event | category | flops | bytes accessed | tf_op | source)
XLA Modules:
  0.0 109.2 jit_solution(2212139253398873868)
XLA Ops:
  0.0 0.8 reshape.51
  0.8 0.7 fusion.25
  1.6 1.2 %convert_element_type.19 = bf16[384,512]{1,0:T(8,128)(2,1)S(1)} convert(f32[384,512]{1,0:T(8,128)} %param.17) | non-fusion elementwise | flops 196608 | bytes 1179648 | tf_op jit(solution)/shard_map/convert_element_type | solution.py:307
  3.7 1.4 %pad_maximum_fusion.2.source = bf16[4,3,512,128]{3,2,1,0:T(8,128)(2,1)} fusion(bf16[1,3,512,128]{3,2,1,0:T(8,128)(2,1)S(1)} %bitcast.88, bf16[1,3,512,128]{3,2,1,0:T(8,128)(2,1)S(1)} %bitcast.89, bf16[1,3,512,128]{3,2,1,0:T(8,128)(2,1)S(1)} %bitcast.91, bf16[1,3,512,128]{3,2,1,0:T(8,128)(2,1)S(1)} %bitcast.90), kind=kLoop, calls=%fused_computation.14 | loop fusion | flops 2359296 | bytes 3145728 | tf_op jit(solution)/shard_map/stack | solution.py:308
  5.1 46.3 %shard_map.127 = bf16[4,96,16,128]{3,2,1,0:T(8,128)(2,1)} custom-call(bf16[4,3,512,128]{3,2,1,0:T(8,128)(2,1)} %pad_maximum_fusion.2.source), custom_call_target="tpu_custom_call" | custom-call | tf_op jit(solution)/shard_map/pallas_call | solution.py:92
  51.4 1.5 %slice_convert_fusion = f32[3,96,16,128]{3,2,1,0:T(8,128)S(1)} fusion(bf16[4,96,16,128]{3,2,1,0:T(8,128)(2,1)} %shard_map.127), kind=kLoop, calls=%fused_computation.19 | loop fusion | flops 589824 | bytes 3538944 | tf_op jit(solution)/shard_map/convert_element_type | solution.py:316
  53.0 0.5 pad_slice_fusion
  53.5 0.5 pad_slice_fusion.1
  54.2 0.9 fusion.21
  55.4 0.7 copy-done.8
  56.1 2.2 %fusion.10 = f32[208,32,128]{2,0,1:T(8,128)S(1)} fusion(f32[208,96,1]{0,1,2:T(8,128)S(1)} %copy-done.8, f32[96,32,128]{2,1,0:T(8,128)S(1)} %pad_maximum_fusion.3), kind=kOutput, calls=%fused_computation.16 | convolution fusion | flops 490733568 | bytes 5060608 | tf_op jit(solution)/shard_map/kn,ncm->kcm/dot_general | solution.py:221
  58.3 0.4 multiply_subtract_fusion
  58.9 0.7 copy-done.4
  59.6 2.3 %fusion.2 = f32[104,32,256]{2,1,0:T(8,128)S(1)} fusion(f32[256,256,1]{1,0,2:T(8,128)S(1)} %copy-done.4, f32[104,32,256]{2,0,1:T(8,128)S(1)} %pad_maximum_fusion), kind=kOutput, calls=%fused_computation.3 | convolution fusion | flops 1308622848 | bytes 7077888 | tf_op jit(solution)/shard_map/kcm,mj->kcj/dot_general | solution.py:221
  62.2 0.7 copy-done.5
  62.9 0.8 fusion.4
  64.1 0.8 copy-done.7
  64.9 1.1 fusion.8
  66.0 0.3 copy-done
  66.3 0.3 slice_convert_fusion.1
  66.9 0.3 pad_slice_fusion.5
  67.2 1.6 %fusion.18 = bf16[96,16,128]{2,1,0:T(8,128)(2,1)} fusion(f32[96,16,127]{2,1,0:T(8,128)S(1)} %bitcast.85, f32[96,16,1]{2,1,0:T(8,128)S(1)} %pad_slice_fusion.5, f32[96,16,126]{2,1,0:T(8,128)S(1)} %bitcast.86, f32[96,16,2]{2,1,0:T(8,128)S(1)} %pad_slice_fusion.4, f32[96,16,128]{2,0,1:T(8,128)S(1)} %fusion.8, f32[96,16,128]{2,1,0:T(8,128)S(1)} %fusion.21, ...), kind=kLoop, calls=%fused_computation.31 | loop fusion | flops 2359296 | bytes 3932416 | tf_op jit(solution)/shard_map/convert_element_type | solution.py:321
  68.8 34.7 %shard_map.128 = bf16[3,8,32,16,128]{4,3,2,1,0:T(8,128)(2,1)} custom-call(bf16[32,3,16,128]{3,2,1,0:T(8,128)(2,1)} %bitcast.87), custom_call_target="tpu_custom_call" | custom-call | tf_op jit(solution)/shard_map/pallas_call | solution.py:201
  103.5 5.7 %fusion.12 = bf16[3,128,512]{2,1,0:T(8,128)(2,1)} fusion(bf16[3,4096,128]{2,1,0:T(8,128)(2,1)} %bitcast.80, bf16[4096,512]{1,0:T(8,128)(2,1)} %param.19), kind=kOutput, calls=%fused_computation.18 | convolution fusion | flops 1610809344 | bytes 7733248 | tf_op jit(solution)/shard_map/co,ncm->nom/dot_general | solution.py:325
  (31 shorter events, 2.5 us)
Async XLA Ops:
  0.0 3.0 %copy-start.1 = (bf16[384,512]{1,0:T(8,128)(2,1)S(1)}, bf16[384,512]{1,0:T(8,128)(2,1)}, u32[]{:S(2)}) copy-start(bf16[384,512]{1,0:T(8,128)(2,1)} %param.15) | copy-start | bytes 1179652
  0.0 3.3 %copy-start.2 = (bf16[384,512]{1,0:T(8,128)(2,1)S(1)}, bf16[384,512]{1,0:T(8,128)(2,1)}, u32[]{:S(2)}) copy-start(bf16[384,512]{1,0:T(8,128)(2,1)} %param.13) | copy-start | bytes 1179652
  1.6 1.9 %copy-start.3 = (bf16[384,512]{1,0:T(8,128)(2,1)S(1)}, bf16[384,512]{1,0:T(8,128)(2,1)}, u32[]{:S(2)}) copy-start(bf16[384,512]{1,0:T(8,128)(2,1)} %param.14) | copy-start | bytes 1179652
  55.1 0.9 copy-start.8
  56.0 2.2 %copy-start.6 = (f32[104,128]{1,0:T(8,128)S(1)}, f32[104,128]{1,0:T(8,128)}, u32[]{:S(2)}) copy-start(f32[104,128]{1,0:T(8,128)} %constant.38) | copy-start | bytes 159748
  56.0 2.3 %copy-start.10 = (f32[104,128]{1,0:T(8,128)S(1)}, f32[104,128]{1,0:T(8,128)}, u32[]{:S(2)}) copy-start(f32[104,128]{1,0:T(8,128)} %constant.40) | copy-start | bytes 159748
  58.7 1.0 copy-start.4
  62.0 1.0 copy-start.5
  62.9 0.9 copy-start.9
  64.0 0.9 copy-start.7
  64.9 1.4 %copy-start = (bf16[4,96,16,128]{3,2,1,0:T(8,128)(2,1)S(1)}, bf16[4,96,16,128]{3,2,1,0:T(8,128)(2,1)}, u32[]{:S(2)}) copy-start(bf16[4,96,16,128]{3,2,1,0:T(8,128)(2,1)} %shard_map.127) | copy-start | bytes 4718596

commit v18 on v16

--- a/solution.py
+++ b/solution.py
@@ -41,21 +41,21 @@
     ch = lax.axis_index("ch")
     half = source.shape[1]
     width = target.shape[2]
+
+    def piece(ref_src, peer, origin):
+        return (
+            ref_src.at[:, :, pl.ds(peer * width, width)],
+            target.at[:, pl.ds(origin * half, half)],
+        )
+
+    src, dst = piece(source, me, me)
+    local = pltpu.make_async_copy(src, dst, local_sem.at[0])
+    local.start()
     barrier = pltpu.get_barrier_semaphore()
     for step in range(1, group):
         peer = lax.rem(me + step, group)
         pl.semaphore_signal(barrier, inc=1, device_id=(peer, ch), device_id_type=MESH)
     pl.semaphore_wait(barrier, group - 1)
-
-    def piece(ref_src, peer, origin):
-        return (
-            ref_src.at[:, :, pl.ds(peer * width, width)],
-            target.at[:, pl.ds(origin * half, half)],
-        )
-
-    src, dst = piece(source, me, me)
-    local = pltpu.make_async_copy(src, dst, local_sem.at[0])
-    local.start()
     inner, offsets = peer_offsets(group)
     sent = []
     for step, off in enumerate(offsets, start=1):
@@ -109,6 +109,13 @@
     half = source.shape[1]
     sibling = ch + 1 - 2 * lax.rem(ch, 2)
     across = [lax.rem(ch + 2 * hop, chans) for hop in range(1, chans // 2)]
+    locals_ = []
+    for part in range(half):
+        cp = pltpu.make_async_copy(
+            source.at[me, part], target.at[part, ch, me], local_sem.at[part]
+        )
+        cp.start()
+        locals_.append(cp)
     barrier = pltpu.get_barrier_semaphore()
     for step in range(1, group):
         peer = lax.rem(me + step, group)
@@ -129,13 +136,7 @@
 
     inner, offsets = peer_offsets(group)
     sent = []
-    locals_ = []
-    for part in range(half):
-        cp = pltpu.make_async_copy(
-            source.at[me, part], target.at[part, ch, me], local_sem.at[part]
-        )
-        cp.start()
-        locals_.append(cp)
+    for part in range(half):
         for step, off in enumerate(offsets, start=1):
             peer = shifted_peer(me, off, inner, group, 1)
             cp = pltpu.make_async_remote_copy(

time: 109 us -> 109 us (level)
  no operation moved by 1% of the time
where the time goes in v18:
time: 109 us
  Pallas kernels  80.9 us (74%)
  matrix products  12.4 us (11%)
  other arithmetic  9.14 us (8%)
  local copies, waits for them, and re-layouts  6.37 us (6%)
    pallas_call x1, Pallas kernels, exchange(): pl.pallas_call(functools.partial(exchange_kernel, group), out_shape=jax.S...  46.3 us
    pallas_call x1, Pallas kernels, return_and_gather(): pl.pallas_call(functools.partial(return_kernel, group, chans), out_shape=...  34.6 us
    dot_general x4, matrix products, contract(): jnp.einsum(pattern, first_op, second_op, precision=high, preferred_elemen...  6.68 us
    dot_general x1, matrix products, on_device(): jnp.einsum('co,ncm->nom', out_weight, gathered, preferred_element_type=jn...  5.71 us
    unnamed x20, local copies, waits for them, and re-layouts  2.68 us

profile of v18, /device:TPU:1, one launch (start us, length us, event | category | flops | bytes accessed | tf_op | source)
XLA Modules:
  0.0 109.0 jit_solution(9983749180371268928)
XLA Ops:
  0.0 0.8 reshape.50
  0.8 0.7 fusion.24
  1.6 1.2 %convert_element_type.13 = bf16[384,512]{1,0:T(8,128)(2,1)S(1)} convert(f32[384,512]{1,0:T(8,128)} %param.17) | non-fusion elementwise | flops 196608 | bytes 1179648 | tf_op jit(solution)/shard_map/convert_element_type | solution.py:308
  3.7 1.4 %pad_maximum_fusion.2.source = bf16[4,3,512,128]{3,2,1,0:T(8,128)(2,1)} fusion(bf16[1,3,512,128]{3,2,1,0:T(8,128)(2,1)S(1)} %bitcast.87, bf16[1,3,512,128]{3,2,1,0:T(8,128)(2,1)S(1)} %bitcast.88, bf16[1,3,512,128]{3,2,1,0:T(8,128)(2,1)S(1)} %bitcast.90, bf16[1,3,512,128]{3,2,1,0:T(8,128)(2,1)S(1)} %bitcast.89), kind=kLoop, calls=%fused_computation.14 | loop fusion | flops 2359296 | bytes 3145728 | tf_op jit(solution)/shard_map/stack | solution.py:309
  5.1 46.3 %shard_map.127 = bf16[4,96,16,128]{3,2,1,0:T(8,128)(2,1)} custom-call(bf16[4,3,512,128]{3,2,1,0:T(8,128)(2,1)} %pad_maximum_fusion.2.source), custom_call_target="tpu_custom_call" | custom-call | tf_op jit(solution)/shard_map/pallas_call | solution.py:92
  51.4 1.7 %convert_element_type.14 = f32[4,96,16,128]{3,2,1,0:T(8,128)S(1)} convert(bf16[4,96,16,128]{3,2,1,0:T(8,128)(2,1)} %shard_map.127) | non-fusion elementwise | flops 786432 | bytes 4718592 | tf_op jit(solution)/shard_map/convert_element_type | solution.py:317
  53.3 0.5 pad_slice_fusion
  53.8 0.5 pad_slice_fusion.1
  54.6 1.0 fusion.21
  55.8 0.7 copy-done.7
  56.5 2.3 %fusion.10 = f32[208,32,128]{2,0,1:T(8,128)S(1)} fusion(f32[208,96,1]{0,1,2:T(8,128)S(1)} %copy-done.7, f32[96,32,128]{2,1,0:T(8,128)S(1)} %pad_maximum_fusion.3), kind=kOutput, calls=%fused_computation.16 | convolution fusion | flops 490733568 | bytes 5060608 | tf_op jit(solution)/shard_map/kn,ncm->kcm/dot_general | solution.py:222
  58.7 0.4 multiply_subtract_fusion
  59.1 0.4 pad_maximum_fusion
  59.6 0.5 copy-done.3
  60.1 2.3 %fusion.2 = f32[104,32,256]{2,1,0:T(8,128)S(1)} fusion(f32[256,256,1]{1,0,2:T(8,128)S(1)} %copy-done.3, f32[104,32,256]{2,0,1:T(8,128)S(1)} %pad_maximum_fusion), kind=kOutput, calls=%fused_computation.3 | convolution fusion | flops 1308622848 | bytes 7077888 | tf_op jit(solution)/shard_map/kcm,mj->kcj/dot_general | solution.py:222
  62.6 0.7 copy-done.4
  63.4 0.8 fusion.4
  64.6 0.8 copy-done.6
  65.3 1.2 %fusion.8 = f32[96,16,128]{2,0,1:T(8,128)S(1)} fusion(f32[96,208,1]{1,0,2:T(8,128)S(1)} %copy-done.6, f32[208,16,128]{2,1,0:T(8,128)S(1)} %pad_maximum_fusion.1), kind=kOutput, calls=%fused_computation.10 | convolution fusion | flops 245366784 | bytes 2570240 | tf_op jit(solution)/shard_map/nk,kcm->ncm/dot_general | solution.py:222
  66.6 0.3 pad_slice_fusion.4
  66.9 0.3 pad_slice_fusion.5
  67.1 1.6 %fusion.18 = bf16[96,16,128]{2,1,0:T(8,128)(2,1)} fusion(f32[96,16,127]{2,1,0:T(8,128)S(1)} %bitcast.85, f32[96,16,1]{2,1,0:T(8,128)S(1)} %pad_slice_fusion.5, f32[96,16,126]{2,1,0:T(8,128)S(1)} %bitcast.86, f32[96,16,2]{2,1,0:T(8,128)S(1)} %pad_slice_fusion.4, f32[96,16,128]{2,0,1:T(8,128)S(1)} %fusion.8, f32[96,16,128]{2,1,0:T(8,128)S(1)} %fusion.21, ...), kind=kLoop, calls=%fused_computation.31 | loop fusion | flops 2162688 | bytes 4325632 | tf_op jit(solution)/shard_map/convert_element_type | solution.py:322
  68.7 34.6 %shard_map.128 = bf16[3,8,32,16,128]{4,3,2,1,0:T(8,128)(2,1)} custom-call(bf16[32,3,16,128]{3,2,1,0:T(8,128)(2,1)} %bitcast.92), custom_call_target="tpu_custom_call" | custom-call | tf_op jit(solution)/shard_map/pallas_call | solution.py:202
  103.3 5.7 %fusion.12 = bf16[3,128,512]{2,1,0:T(8,128)(2,1)} fusion(bf16[3,4096,128]{2,1,0:T(8,128)(2,1)} %bitcast.80, bf16[4096,512]{1,0:T(8,128)(2,1)} %param.19), kind=kOutput, calls=%fused_computation.18 | convolution fusion | flops 1610809344 | bytes 7733248 | tf_op jit(solution)/shard_map/co,ncm->nom/dot_general | solution.py:326
  (27 shorter events, 2.1 us)
Async XLA Ops:
  0.0 3.0 %copy-start = (bf16[384,512]{1,0:T(8,128)(2,1)S(1)}, bf16[384,512]{1,0:T(8,128)(2,1)}, u32[]{:S(2)}) copy-start(bf16[384,512]{1,0:T(8,128)(2,1)} %param.15) | copy-start | bytes 1179652
  0.0 3.3 %copy-start.1 = (bf16[384,512]{1,0:T(8,128)(2,1)S(1)}, bf16[384,512]{1,0:T(8,128)(2,1)}, u32[]{:S(2)}) copy-start(bf16[384,512]{1,0:T(8,128)(2,1)} %param.13) | copy-start | bytes 1179652
  1.6 1.9 %copy-start.2 = (bf16[384,512]{1,0:T(8,128)(2,1)S(1)}, bf16[384,512]{1,0:T(8,128)(2,1)}, u32[]{:S(2)}) copy-start(bf16[384,512]{1,0:T(8,128)(2,1)} %param.14) | copy-start | bytes 1179652
  55.6 0.9 copy-start.7
  56.5 2.3 %copy-start.5 = (f32[104,128]{1,0:T(8,128)S(1)}, f32[104,128]{1,0:T(8,128)}, u32[]{:S(2)}) copy-start(f32[104,128]{1,0:T(8,128)} %constant.38) | copy-start | bytes 159748
  56.5 2.3 %copy-start.9 = (f32[104,128]{1,0:T(8,128)S(1)}, f32[104,128]{1,0:T(8,128)}, u32[]{:S(2)}) copy-start(f32[104,128]{1,0:T(8,128)} %constant.40) | copy-start | bytes 159748
  59.1 1.0 copy-start.3
  62.4 1.0 copy-start.4
  63.4 0.9 copy-start.8
  64.4 0.9 copy-start.6

commit v19 on v16

--- a/solution.py
+++ b/solution.py
@@ -243,7 +243,6 @@
         tc=f32(np.cos(at)[:, None, :]),
         ts=f32(np.sin(at)[:, None, :]),
         fwd2=f32(np.block([[c2, -s2], [s2, c2]])),
-        inv2=f32(np.block([[c2, s2], [-s2, c2]])),
         last=f32(np.concatenate([(c1 * weight).T, -(s1 * weight).T], axis=1) / total),
     )
 
@@ -258,7 +257,7 @@
 
 
 def inverse(spectrum, tb):
-    z = contract("kcj,jm->kcm", spectrum, tb["inv2"])
+    z = contract("kcj,mj->kcm", spectrum, tb["fwd2"])
     zr, zi = z[:, :, :LANES], z[:, :, LANES:]
     tc, ts = tb["tc"], tb["ts"]
     stacked = jnp.concatenate([zr * tc - zi * ts, zr * ts + zi * tc], axis=0)

time: 109 us -> 109 us (level)
    unnamed x20 -> x18, local copies, waits for them, and re-layouts: 2.68 us -> 1.96 us
where the time goes in v19:
time: 109 us; the launch traced here: 108 us
  Pallas kernels  80.9 us (74%)
  matrix products  12.4 us (11%)
  other arithmetic  9.14 us (8%)
  local copies, waits for them, and re-layouts  5.65 us (5%)
    pallas_call x1, Pallas kernels, exchange(): pl.pallas_call(functools.partial(exchange_kernel, group), out_shape=jax.S...  46.3 us
    pallas_call x1, Pallas kernels, return_and_gather(): pl.pallas_call(functools.partial(return_kernel, group, chans), out_shape=...  34.6 us
    dot_general x4, matrix products, contract(): jnp.einsum(pattern, first_op, second_op, precision=high, preferred_elemen...  6.71 us
    dot_general x1, matrix products, on_device(): jnp.einsum('co,ncm->nom', out_weight, gathered, preferred_element_type=jn...  5.71 us

profile of v19, /device:TPU:1, one launch (start us, length us, event | category | flops | bytes accessed | tf_op | source)
XLA Modules:
  0.0 108.4 jit_solution(587244540313366807)
XLA Ops:
  0.0 0.8 reshape.50
  0.8 0.7 fusion.24
  1.6 1.2 %convert_element_type.13 = bf16[384,512]{1,0:T(8,128)(2,1)S(1)} convert(f32[384,512]{1,0:T(8,128)} %param.16) | non-fusion elementwise | flops 196608 | bytes 1179648 | tf_op jit(solution)/shard_map/convert_element_type | solution.py:306
  3.7 1.4 %pad_maximum_fusion.2.source = bf16[4,3,512,128]{3,2,1,0:T(8,128)(2,1)} fusion(bf16[1,3,512,128]{3,2,1,0:T(8,128)(2,1)S(1)} %bitcast.86, bf16[1,3,512,128]{3,2,1,0:T(8,128)(2,1)S(1)} %bitcast.87, bf16[1,3,512,128]{3,2,1,0:T(8,128)(2,1)S(1)} %bitcast.89, bf16[1,3,512,128]{3,2,1,0:T(8,128)(2,1)S(1)} %bitcast.88), kind=kLoop, calls=%fused_computation.14 | loop fusion | flops 2359296 | bytes 3145728 | tf_op jit(solution)/shard_map/stack | solution.py:307
  5.1 46.3 %shard_map.118 = bf16[4,96,16,128]{3,2,1,0:T(8,128)(2,1)} custom-call(bf16[4,3,512,128]{3,2,1,0:T(8,128)(2,1)} %pad_maximum_fusion.2.source), custom_call_target="tpu_custom_call" | custom-call | tf_op jit(solution)/shard_map/pallas_call | solution.py:92
  51.4 1.7 %convert_element_type.14 = f32[4,96,16,128]{3,2,1,0:T(8,128)S(1)} convert(bf16[4,96,16,128]{3,2,1,0:T(8,128)(2,1)} %shard_map.118) | non-fusion elementwise | flops 786432 | bytes 4718592 | tf_op jit(solution)/shard_map/convert_element_type | solution.py:315
  53.2 0.5 pad_slice_fusion
  53.8 0.5 pad_slice_fusion.1
  54.6 1.0 fusion.21
  55.6 0.2 pad_maximum_fusion.3
  55.8 0.7 copy-done.6
  56.5 2.3 %fusion.10 = f32[208,32,128]{2,0,1:T(8,128)S(1)} fusion(f32[208,96,1]{0,1,2:T(8,128)S(1)} %copy-done.6, f32[96,32,128]{2,1,0:T(8,128)S(1)} %pad_maximum_fusion.3), kind=kOutput, calls=%fused_computation.16 | convolution fusion | flops 490733568 | bytes 5060608 | tf_op jit(solution)/shard_map/kn,ncm->kcm/dot_general | solution.py:221
  58.7 0.4 multiply_subtract_fusion
  59.1 0.4 pad_maximum_fusion
  59.6 0.5 copy-done
  60.1 2.3 %fusion.2 = f32[104,32,256]{2,1,0:T(8,128)S(1)} fusion(f32[256,256,1]{1,0,2:T(8,128)S(1)} %copy-done, f32[104,32,256]{2,0,1:T(8,128)S(1)} %pad_maximum_fusion), kind=kOutput, calls=%fused_computation.3 | convolution fusion | flops 1308622848 | bytes 7077888 | tf_op jit(solution)/shard_map/kcm,mj->kcj/dot_general | solution.py:221
  62.6 0.9 fusion.4
  63.9 0.8 copy-done.5
  64.7 1.2 %fusion.8 = f32[96,16,128]{2,0,1:T(8,128)S(1)} fusion(f32[96,208,1]{1,0,2:T(8,128)S(1)} %copy-done.5, f32[208,16,128]{2,1,0:T(8,128)S(1)} %pad_maximum_fusion.1), kind=kOutput, calls=%fused_computation.10 | convolution fusion | flops 245366784 | bytes 2570240 | tf_op jit(solution)/shard_map/nk,kcm->ncm/dot_general | solution.py:221
  65.9 0.3 pad_slice_fusion.4
  66.2 0.3 pad_slice_fusion.5
  66.4 1.6 %fusion.18 = bf16[96,16,128]{2,1,0:T(8,128)(2,1)} fusion(f32[96,16,127]{2,1,0:T(8,128)S(1)} %bitcast.84, f32[96,16,1]{2,1,0:T(8,128)S(1)} %pad_slice_fusion.5, f32[96,16,126]{2,1,0:T(8,128)S(1)} %bitcast.85, f32[96,16,2]{2,1,0:T(8,128)S(1)} %pad_slice_fusion.4, f32[96,16,128]{2,0,1:T(8,128)S(1)} %fusion.8, f32[96,16,128]{2,1,0:T(8,128)S(1)} %fusion.21, ...), kind=kLoop, calls=%fused_computation.31 | loop fusion | flops 2162688 | bytes 4325632 | tf_op jit(solution)/shard_map/convert_element_type | solution.py:320
  68.0 34.6 %shard_map.119 = bf16[3,8,32,16,128]{4,3,2,1,0:T(8,128)(2,1)} custom-call(bf16[32,3,16,128]{3,2,1,0:T(8,128)(2,1)} %bitcast.91), custom_call_target="tpu_custom_call" | custom-call | tf_op jit(solution)/shard_map/pallas_call | solution.py:201
  102.6 5.7 %fusion.12 = bf16[3,128,512]{2,1,0:T(8,128)(2,1)} fusion(bf16[3,4096,128]{2,1,0:T(8,128)(2,1)} %bitcast.79, bf16[4096,512]{1,0:T(8,128)(2,1)} %param.18), kind=kOutput, calls=%fused_computation.18 | convolution fusion | flops 1610809344 | bytes 7733248 | tf_op jit(solution)/shard_map/co,ncm->nom/dot_general | solution.py:324
  (25 shorter events, 1.8 us)
Async XLA Ops:
  0.0 3.0 %copy-start.1 = (bf16[384,512]{1,0:T(8,128)(2,1)S(1)}, bf16[384,512]{1,0:T(8,128)(2,1)}, u32[]{:S(2)}) copy-start(bf16[384,512]{1,0:T(8,128)(2,1)} %param.14) | copy-start | bytes 1179652
  0.0 3.3 %copy-start.2 = (bf16[384,512]{1,0:T(8,128)(2,1)S(1)}, bf16[384,512]{1,0:T(8,128)(2,1)}, u32[]{:S(2)}) copy-start(bf16[384,512]{1,0:T(8,128)(2,1)} %param.12) | copy-start | bytes 1179652
  1.6 1.9 %copy-start.3 = (bf16[384,512]{1,0:T(8,128)(2,1)S(1)}, bf16[384,512]{1,0:T(8,128)(2,1)}, u32[]{:S(2)}) copy-start(bf16[384,512]{1,0:T(8,128)(2,1)} %param.13) | copy-start | bytes 1179652
  55.6 0.9 copy-start.6
  56.5 2.3 %copy-start.4 = (f32[104,128]{1,0:T(8,128)S(1)}, f32[104,128]{1,0:T(8,128)}, u32[]{:S(2)}) copy-start(f32[104,128]{1,0:T(8,128)} %constant.35) | copy-start | bytes 159748
  56.5 2.3 %copy-start.8 = (f32[104,128]{1,0:T(8,128)S(1)}, f32[104,128]{1,0:T(8,128)}, u32[]{:S(2)}) copy-start(f32[104,128]{1,0:T(8,128)} %constant.37) | copy-start | bytes 159748
  59.1 1.0 copy-start
  62.6 0.9 copy-start.7
  63.8 0.9 copy-start.5
